TPU v7x, 32 devices: a whole 2x2x4 slice. The times are simulated.
32 devices in a mesh: groups: 2 (over x), range: 16 (over z, y, core).
Axes of the slice: x: 2, y: 2, z: 4, core: 2. Of those that a mesh axis runs over, the one named last changes fastest.
Arguments:
- echoes: bfloat16 [4, 256, 16384], P('groups', 'range'), parts along dimension 0, may hold values from -6 to 6
- range_reference: float32 [2, 16384], replicated, may hold values from -6 to 6
- kernels: float32 [16, 8], replicated, may hold values from -2 to 2
- shifts: int32 [128, 256], P('range'), may hold values from 0 to 12
- phase_index: int32 [128, 256], P('range'), may hold values from 0 to 15
- centroid: int32 [128], P('range'), may hold values from 0 to 255
- azimuth_reference: float32 [2, 128, 256], P(None, 'range'), may hold values from -6 to 6
Outputs:
- focused_image: bfloat16 [4, 256, 16384], P('groups', None, 'range'), parts along dimension 0
There are 2 independent parts, one for each index of `groups`. A program takes and returns all parts, laid end to end along the dimension named above; an argument that names none is the same for every part. Nothing has to cross between parts.
Inputs may be any that keep to these rules, and one draw needn't show every extreme that they name: `shifts`: whole range cells by which a block's energy at a Doppler bin has migrated. `phase_index`: row of kernels used by a block at a Doppler bin. `centroid`: doppler bins by which a block's azimuth reference is turned.
All inputs are finite; a program needn't handle non-finite values.
Results may differ from a plain program's by a relative error of at most 0.014.
Values may be sent and summed in bfloat16 or wider, within the bound.
No kernel may reach another device: no remote copies, remote signals or barrier semaphores. Data moves between devices by JAX's collectives and lax.ppermute only.
A program may use at most 128 MiB of HBM per device.

v0:
```python
import math

import jax
import jax.numpy as jnp
from jax import lax
from jax.sharding import PartitionSpec as P

R1 = 128
RB = 128
MAXSHIFT = 12
HALO = 16


def extended(cells, sides, width):
    for axis, dim in sides:
        count = lax.axis_size(axis)
        ends = count - 1
        head = lax.slice_in_dim(cells, 0, width, axis=dim)
        tail = lax.slice_in_dim(cells, cells.shape[dim] - width, cells.shape[dim], axis=dim)
        cells = jnp.concatenate(
            [
                lax.ppermute(tail, axis, [(i, (i + 1) % count) for i in range(ends)]),
                cells,
                lax.ppermute(head, axis, [((i + 1) % count, i) for i in range(ends)]),
            ],
            axis=dim,
        )
    return cells


def transform_matrix(length, orient):
    number_line = jnp.arange(length, dtype=jnp.int32)
    angles = (
        2.0
        * math.pi
        / length
        * (number_line[:, None] * number_line[None, :] % length).astype(jnp.float32)
    )
    cosine = jnp.cos(angles)
    sine_part = orient * jnp.sin(angles)
    matrix = jnp.stack([jnp.stack([cosine, -sine_part], 1), jnp.stack([sine_part, cosine], 1)], 0)
    return matrix.astype(jnp.bfloat16)


def twiddle(first_len, second_len, orient, factor):
    first_axis = jnp.arange(first_len, dtype=jnp.int32)
    second_axis = jnp.arange(second_len, dtype=jnp.int32)
    whole = first_len * second_len
    angles = (
        2.0
        * math.pi
        / whole
        * (first_axis[:, None] * second_axis[None, :] % whole).astype(jnp.float32)
    )
    return (jnp.cos(angles) * factor, orient * jnp.sin(angles) * factor)


def complex_times(values, real_part, imag_part):
    return jnp.stack(
        [
            values[0] * real_part - values[1] * imag_part,
            values[0] * imag_part + values[1] * real_part,
        ],
        0,
    )


def product_of(pattern, matrix, values):
    return jnp.einsum(pattern, matrix, values, preferred_element_type=jnp.float32)


def range_lines(pulse_lines, reference_slots, range_first, range_second):
    values = pulse_lines.reshape(2, -1, range_first, range_second)
    twist_real, twist_imag = twiddle(range_first, range_second, -1.0, 1.0 / math.sqrt(range_first))
    halfway = complex_times(
        product_of("oaib,ipbm->opam", transform_matrix(range_first, -1.0), values),
        twist_real,
        twist_imag,
    ).astype(jnp.bfloat16)
    spectrum = product_of("oaib,ipkb->opka", transform_matrix(range_second, -1.0), halfway) * (
        1.0 / math.sqrt(range_second)
    )
    spectrum = complex_times(spectrum, reference_slots[0], reference_slots[1]).astype(jnp.bfloat16)
    back_real, back_imag = twiddle(range_first, range_second, 1.0, 1.0 / math.sqrt(range_second))
    halfway = complex_times(
        product_of("oaib,ipkb->opka", transform_matrix(range_second, 1.0), spectrum),
        back_real,
        back_imag,
    ).astype(jnp.bfloat16)
    result = product_of("oaib,ipbm->opam", transform_matrix(range_first, 1.0), halfway) * (
        1.0 / math.sqrt(range_first)
    )
    return result.reshape(2, -1, range_first * range_second).astype(jnp.bfloat16)


def azimuth_forward(cell_block, azimuth_first, azimuth_second):
    values = cell_block.reshape(2, azimuth_first, azimuth_second, -1)
    twist_real, twist_imag = twiddle(
        azimuth_first, azimuth_second, -1.0, 1.0 / math.sqrt(azimuth_first)
    )
    halfway = complex_times(
        product_of("oaib,ibmc->oamc", transform_matrix(azimuth_first, -1.0), values),
        twist_real[:, :, None],
        twist_imag[:, :, None],
    ).astype(jnp.bfloat16)
    spectrum = product_of("oaib,ikbc->okac", transform_matrix(azimuth_second, -1.0), halfway) * (
        1.0 / math.sqrt(azimuth_second)
    )
    return spectrum.astype(jnp.bfloat16).reshape(2, azimuth_first * azimuth_second, values.shape[3])


def azimuth_inverse(spectrum, azimuth_first, azimuth_second):
    back_real, back_imag = twiddle(
        azimuth_first, azimuth_second, 1.0, 1.0 / math.sqrt(azimuth_second)
    )
    halfway = complex_times(
        product_of("oaib,ikbc->okac", transform_matrix(azimuth_second, 1.0), spectrum),
        back_real[:, :, None],
        back_imag[:, :, None],
    ).astype(jnp.bfloat16)
    result = product_of("oaib,ibmc->oamc", transform_matrix(azimuth_first, 1.0), halfway) * (
        1.0 / math.sqrt(azimuth_first)
    )
    return result.reshape(2, azimuth_first * azimuth_second, -1).astype(jnp.bfloat16)


def local(echoes, range_reference, kernels, shifts, phase_index, centroid, azimuth_reference):
    ranks = lax.axis_size("range")
    pulses = echoes.shape[1]
    samples = echoes.shape[2]
    cell_count = samples // ranks
    range_first = R1
    range_second = samples // range_first
    total_pulses = ranks * pulses
    phase_count = kernels.shape[0]
    tap_count = kernels.shape[1]
    lead_taps = tap_count // 2 - 1
    block_count = cell_count // RB
    reference_slots = range_reference.reshape(2, range_second, range_first).transpose(0, 2, 1)
    compressed = range_lines(echoes, reference_slots, range_first, range_second)
    blocks = compressed.reshape(2, pulses, ranks, cell_count)
    arrived = lax.all_to_all(blocks, "range", split_axis=2, concat_axis=1, tiled=True)
    spectrum = azimuth_forward(arrived.reshape(2, total_pulses, arrived.shape[3]), ranks, pulses)
    padded = extended(spectrum, (("range", 2),), HALO)
    shift_rows = (
        shifts.reshape(block_count, pulses, ranks)
        .transpose(0, 2, 1)
        .reshape(block_count, total_pulses)
    )
    phase_rows = (
        phase_index.reshape(block_count, pulses, ranks)
        .transpose(0, 2, 1)
        .reshape(block_count, total_pulses)
    )
    onehot = (
        phase_rows[:, :, None] == jnp.arange(phase_count, dtype=jnp.int32)[None, None, :]
    ).astype(jnp.float32)
    weights = jnp.einsum("bfq,qt->bft", onehot, kernels, precision=lax.Precision.HIGHEST)
    offset_count = MAXSHIFT + tap_count
    offsets = jnp.arange(offset_count, dtype=jnp.int32)
    spread = jnp.zeros((offset_count, block_count, total_pulses), jnp.float32)
    for tap_index in range(tap_count):
        spread = spread + jnp.where(
            shift_rows[None] + tap_index == offsets[:, None, None],
            weights[None, :, :, tap_index],
            0.0,
        )
    spread = spread.transpose(0, 2, 1)
    summed = jnp.zeros((2, total_pulses, block_count, RB), jnp.float32)
    for offset_index in range(offset_count):
        begin = HALO - lead_taps + offset_index
        window = lax.slice_in_dim(padded, begin, begin + cell_count, axis=2).reshape(
            2, total_pulses, block_count, RB
        )
        summed = summed + spread[offset_index][None, :, :, None] * window
    doubled = jnp.concatenate([azimuth_reference, azimuth_reference], 2)
    starts = (total_pulses - centroid) % total_pulses

    def turn_row(row_pair, start):
        return lax.dynamic_slice_in_dim(row_pair, start, total_pulses, 1)

    natural = jax.vmap(turn_row, in_axes=(1, 0), out_axes=1)(doubled, starts)
    rolled = (
        natural.reshape(2, block_count, pulses, ranks)
        .transpose(0, 3, 2, 1)
        .reshape(2, total_pulses, block_count)
    )
    rolled = rolled[:, :, :, None]
    focused = complex_times(summed, rolled[0], rolled[1]).astype(jnp.bfloat16)
    focused = focused.reshape(2, ranks, pulses, cell_count)
    return azimuth_inverse(focused, ranks, pulses)


def solution(mesh):
    in_specs = (
        P("groups", "range", None),
        P(),
        P(),
        P("range", None),
        P("range", None),
        P("range"),
        P(None, "range", None),
    )
    out_specs = P("groups", None, "range")
    return jax.shard_map(local, mesh=mesh, in_specs=in_specs, out_specs=out_specs, check_vma=False)
```

profile of v0, /device:TPU:9, one launch (start us, length us, event | category | flops | bytes accessed | tf_op | source)
XLA Modules:
  0.0 103.0 jit_solution(8670445554674825801)
XLA Ops:
  1.4 1.5 %copy.139 = bf16[4,8,128,128]{3,2,1,0:T(8,128)(2,1)S(1)} copy(bf16[4,8,128,128]{3,1,2,0:T(8,128)(2,1)} %bitcast.504) | data formatting | bytes 2097152
  5.8 0.7 copy.85
  7.0 2.1 %copy.86 = bf16[2,16,16,1024]{3,0,1,2:T(2,128)(2,1)} copy(bf16[2,16,16,1024]{3,2,1,0:T(8,128)(2,1)S(1)} %convert_element_type.305) | data formatting | bytes 2097152 | tf_op jit(solution)/shard_map/convert_element_type | solution.py:93
  9.1 6.7 %all-to-all-start = ((bf16[2,16,16,1024]{3,0,1,2:T(2,128)(2,1)}), bf16[2,16,16,1024]{3,0,1,2:T(2,128)(2,1)S(1)}, u32[]{:S(2)}, u32[]{:S(2)}) async-start(bf16[2,16,16,1024]{3,0,1,2:T(2,128)(2,1)} %copy.86), calls=%async_computation | async-start | bytes 2097152 | tf_op jit(solution)/shard_map/all_to_all | solution.py:142
  17.0 0.8 copy.76
  17.8 0.8 copy.136
  18.6 0.8 copy.74
  19.4 0.8 copy.135
  20.1 0.8 copy.72
  20.9 0.8 copy.134
  21.7 0.6 pad_maximum_fusion.13
  22.3 0.8 copy.70
  23.1 0.8 copy.133
  23.9 0.8 copy.68
  24.7 0.8 copy.132
  25.5 0.8 copy.66
  26.3 0.8 copy.131
  27.0 0.8 copy.63
  27.8 1.5 %copy.91 = f32[2,8,512]{0,1,2:T(8,128)S(1)} copy(f32[2,8,512]{2,1,0:T(8,128)} %pad_maximum_fusion.13) | data formatting | bytes 65536 | tf_op jit(solution)/shard_map/concatenate | solution.py:176
  29.4 3.0 %gather_fusion = f32[8,2,256]{1,0,2:T(8,128)} fusion(f32[8,2,512]{1,0,2:T(8,128)S(1)} %bitcast.502, s32[8]{0:T(128)S(1)} %fusion.128), kind=kCustom, calls=%fused_computation | custom fusion | bytes 32864 | tf_op jit(solution)/shard_map/vmap()/gather | solution.py:180
  32.4 2.1 %copy.92 = f32[2,8,16,16]{2,3,1,0:T(8,128)S(1)} copy(f32[2,8,16,16]{0,1,3,2:T(8,128)} %bitcast.503) | data formatting | bytes 32768 | tf_op jit(solution)/shard_map/reshape | solution.py:184
  34.8 0.6 fusion.105
  35.4 3.4 %select_add_fusion = f32[20,256,8]{2,1,0:T(8,128)S(1)} fusion(f32[256,8]{1,0:T(8,128)S(1)} %bitcast.505, s32[256,8]{1,0:T(8,128)S(1)} %copy.78, f32[256,8]{1,0:T(8,128)S(1)} %bitcast.506, s32[256,8]{1,0:T(8,128)} %copy.76, f32[256,8]{1,0:T(8,128)} %bitcast.507, s32[256,8]{1,0:T(8,128)} %copy.74, f32[256,8]{1,0:T(8,128)} %bitcast.508, s32[256,8]{1,0:T(8,128)} %copy.72, ...), kind=kLoop, calls=%fused_computation.16 | loop fusion | flops 942080 | bytes 294912 | tf_op jit(solution)/shard_map/add | solution.py:163
  38.9 0.6 slice_bitcast_fusion.18
  39.5 1.4 %slice_bitcast_fusion.19 = (f32[256,8]{1,0:T(8,128)S(1)}, f32[256,8]{1,0:T(8,128)S(1)}, f32[256,8]{1,0:T(8,128)}, f32[256,8]{1,0:T(8,128)}, f32[256,8]{1,0:T(8,1...) fusion(f32[20,256,8]{2,1,0:T(8,128)S(1)} %select_add_fusion), kind=kLoop, calls=%fused_computation.172 | loop fusion | bytes 311296 | tf_op jit(solution)/shard_map/mul | solution.py:175
  40.9 0.7 convolution_bitcast_fusion.1
  42.0 0.8 fusion.24
  42.9 0.8 fusion.137
  43.7 2.3 %collective-permute-start.1 = (bf16[2,256,16]{2,1,0:T(8,128)(2,1)S(1)}, bf16[2,256,16]{2,1,0:T(8,128)(2,1)S(1)}, u32[]{:S(2)}, u32[]{:S(2)}) collective-permute-start(bf16[2,256,16]{2,1,0:T(8,128)(2,1)S(1)} %get-tuple-element.56), channel_id=1, source_target_pairs={{1,0},{2,1},{3,2},{4,3},{5,4},{6,5},{7,6},{8,7},{9,8},{10,9},{11,1... | collective-permute-start | bytes 49160 | tf_op jit(solution)/shard_map/ppermute | solution.py:24
  46.0 0.7 broadcast_multiply_fusion.3
  46.6 0.8 copy.122
  47.4 0.8 copy.121
  48.9 3.3 %collective-permute-start = (bf16[2,256,16]{2,1,0:T(8,128)(2,1)}, bf16[2,256,16]{2,1,0:T(8,128)(2,1)S(1)}, u32[]{:S(2)}, u32[]{:S(2)}) collective-permute-start(bf16[2,256,16]{2,1,0:T(8,128)(2,1)} %get-tuple-element.55), channel_id=1, source_target_pairs={{0,1},{1,2},{2,3},{3,4},{4,5},{5,6},{6,7},{7,8},{8,9},{9,10},{10,1... | collective-permute-start | bytes 49160 | tf_op jit(solution)/shard_map/ppermute | solution.py:22
  52.2 6.2 %fusion.32 = (f32[2,256,1024]{2,1,0:T(8,128)}, f32[2,256,1024]{2,1,0:T(8,128)}, f32[2,256,1024]{2,1,0:T(8,128)S(1)}, f32[2,256,1024]{2,1,0:T(8,128)S(1)}, f32[2,...) fusion(bf16[2,256,16]{2,1,0:T(8,128)(2,1)S(1)} %collective-perm, ...), kind=kLoop, calls=%fused_computation.90 | loop fusion | flops 18874368 | bytes 19939328 | tf_op jit(solution)/shard_map/convert_element_type | solution.py:175
  58.4 4.9 %fusion.50 = (f32[2,256,1024]{2,1,0:T(8,128)S(1)}, f32[2,256,1024]{2,1,0:T(8,128)S(1)}, f32[2,256,1024]{2,1,0:T(8,128)S(1)}, f32[2,256,1024]{2,1,0:T(8,128)S(1)}...) fusion(bf16[2,256,16]{2,1,0:T(8,128)(2,1)S(1)} %collective-permute-done.1, ...), kind=kLoop, calls=%fused_computation.108 | loop fusion | flops 14680064 | bytes 15745024 | tf_op jit(solution)/shard_map/convert_element_type | solution.py:175
  63.3 2.1 %copy.160 = f32[64,8,8,128]{3,2,1,0:T(8,128)S(1)} copy(f32[64,8,8,128]{3,1,2,0:T(8,128)} %bitcast.495) | data formatting | bytes 4194304
  71.5 1.1 %copy-done.4 = f32[2,256,1024]{2,1,0:T(8,128)S(1)} copy-done((f32[2,256,1024]{2,1,0:T(8,128)S(1)}, f32[2,256,1024]{2,1,0:T(8,128)}, u32[]{:S(2)}) %copy-start.4) | copy-done | bytes 2097176
  73.1 1.1 %copy-done.3 = f32[2,256,1024]{2,1,0:T(8,128)S(1)} copy-done((f32[2,256,1024]{2,1,0:T(8,128)S(1)}, f32[2,256,1024]{2,1,0:T(8,128)}, u32[]{:S(2)}) %copy-start.3) | copy-done | bytes 2097176
  74.2 1.8 %copy.145 = f32[64,8,8,128]{3,2,1,0:T(8,128)} copy(f32[64,8,8,128]{3,1,2,0:T(8,128)S(1)} %bitcast.479) | data formatting | bytes 4194304
  76.0 3.9 %fusion.28 = (f32[2,256,1024]{2,1,0:T(8,128)}, f32[2,256,1024]{2,1,0:T(8,128)}, f32[2,256,1024]{2,1,0:T(8,128)}) fusion(bf16[2,256,1024]{2,1,0:T(8,128)(2,1)S(1)} %bitcast.459, bf16[2,256,16]{2,1,0:T(8,128)(2,1)S(1)} %collective-permute-done), kind=kLoop, calls=%fused_computation.86 | loop fusion | flops 6291456 | bytes 7356416 | tf_op jit(solution)/shard_map/convert_element_type | solution.py:175
  79.9 2.2 %copy.143 = f32[64,8,8,128]{3,2,1,0:T(8,128)S(1)} copy(f32[64,8,8,128]{3,1,2,0:T(8,128)} %bitcast.498) | data formatting | bytes 4194304
  82.2 1.8 %copy.142 = f32[64,8,8,128]{3,2,1,0:T(8,128)} copy(f32[64,8,8,128]{3,1,2,0:T(8,128)S(1)} %bitcast.497) | data formatting | bytes 4194304
  84.1 1.8 %copy.141 = f32[64,8,8,128]{3,2,1,0:T(8,128)} copy(f32[64,8,8,128]{3,1,2,0:T(8,128)S(1)} %bitcast.496) | data formatting | bytes 4194304
  86.9 9.3 %fusion = f32[2,256,8,128]{3,2,1,0:T(8,128)} fusion(f32[256,8]{1,0:T(8,128)S(1)} %get-tuple-element.6, f32[256,8]{1,0:T(8,128)S(1)} %copy-done.7, f32[256,8]{1,0:T(8,128)S(1)} %copy-done.8, f32[256,8]{1,0:T(8,128)S(1)} %copy-done.9, f32[256,8]{1,0:T(8,128)S(1)} %copy-done.10, f32[256,8]{1,0:T(8,128)S(1)} %copy-done.11, f32[256,8]{1,0:T(8,128)S(1)} %copy-done.12, ...), kind=kLoop, calls=%fused_computation.26 | loop fusion | flops 20447232 | bytes 44204032 | tf_op jit(solution)/shard_map/add | solution.py:175
  96.2 2.2 %subtract_convert_fusion.1 = (bf16[1,256,8,128]{3,2,1,0:T(8,128)(2,1)S(1)}, bf16[1,256,8,128]{3,2,1,0:T(8,128)(2,1)S(1)}) fusion(f32[2,256,8,128]{3,2,1,0:T(8,128)} %fusion, f32[256,8]{1,0:T(8,128)} %bitcast.516, f32[256,8]{1,0:T(8,128)} %bitcast.517), kind=kLoop, calls=%fused_computation.143 | loop fusion | flops 2097152 | bytes 3162112 | tf_op jit(solution)/shard_map/convert.25
  98.9 0.5 convolution_bitcast_fusion
  99.4 1.2 %copy.181 = f32[16,1024,2,16]{1,0,3,2:T(8,128)S(1)} copy(f32[16,1024,2,16]{1,3,2,0:T(8,128)S(1)} %convolution_bitcast_fusion) | data formatting | bytes 4194304 | tf_op jit(solution)/shard_map/oaib,ikbc->okac/dot_general | solution.py:69
  101.5 1.5 %copy.97 = bf16[2,16,16,1024]{3,2,1,0:T(8,128)(2,1)} copy(bf16[2,16,16,1024]{3,1,2,0:T(8,128)(2,1)S(1)} %fusion.19) | data formatting | bytes 2097152 | tf_op jit(solution)/shard_map/convert_element_type | solution.py:124
  (125 shorter events, 16.2 us)
Async XLA Ops:
  0.0 16.1 %copy-start = (f32[16,8]{0,1:T(8,128)S(1)}, f32[16,8]{0,1:T(8,128)}, u32[]{:S(2)}) copy-start(f32[16,8]{0,1:T(8,128)} %param.9) | copy-start | bytes 1540
  0.0 2.9 %copy-start.25 = (f32[2,16384]{1,0:T(2,128)S(1)}, f32[2,16384]{1,0:T(2,128)}, u32[]{:S(2)}) copy-start(f32[2,16384]{1,0:T(2,128)} %param.8) | copy-start | bytes 393220
  7.0 8.8 %copy-start.30 = (s32[8,256]{1,0:T(8,128)S(1)}, s32[8,256]{1,0:T(8,128)}, u32[]{:S(2)}) copy-start(s32[8,256]{1,0:T(8,128)} %param.11) | copy-start | bytes 24580
  7.0 9.4 %copy-start.31 = (s32[8,256]{1,0:T(8,128)S(1)}, s32[8,256]{1,0:T(8,128)}, u32[]{:S(2)}) copy-start(s32[8,256]{1,0:T(8,128)} %param.10) | copy-start | bytes 24580
  9.1 12.6 %copy-start.29 = (f32[2,8,256]{2,1,0:T(8,128)S(1)}, f32[2,8,256]{2,1,0:T(8,128)}, u32[]{:S(2)}) copy-start(f32[2,8,256]{2,1,0:T(8,128)} %param.13) | copy-start | bytes 49156
  9.1 13.2 %copy-start.32 = (s32[8]{0:T(128)S(1)}, s32[8]{0:T(128)}, u32[]{:S(2)}) copy-start(s32[8]{0:T(128)} %param.12) | copy-start | bytes 100
  9.1 31.8 %all-to-all-start = ((bf16[2,16,16,1024]{3,0,1,2:T(2,128)(2,1)}), bf16[2,16,16,1024]{3,0,1,2:T(2,128)(2,1)S(1)}, u32[]{:S(2)}, u32[]{:S(2)}) async-start(bf16[2,16,16,1024]{3,0,1,2:T(2,128)(2,1)} %copy.86), calls=%async_computation | async-start | bytes 2097152 | tf_op jit(solution)/shard_map/all_to_all | solution.py:142
  43.7 8.5 %collective-permute-start.1 = (bf16[2,256,16]{2,1,0:T(8,128)(2,1)S(1)}, bf16[2,256,16]{2,1,0:T(8,128)(2,1)S(1)}, u32[]{:S(2)}, u32[]{:S(2)}) collective-permute-start(bf16[2,256,16]{2,1,0:T(8,128)(2,1)S(1)} %get-tuple-element.56), channel_id=1, source_target_pairs={{1,0},{2,1},{3,2},{4,3},{5,4},{6,5},{7,6},{8,7},{9,8},{10,9},{11,1... | collective-permute-start | bytes 49160 | tf_op jit(solution)/shard_map/ppermute | solution.py:24
  48.9 27.1 %collective-permute-start = (bf16[2,256,16]{2,1,0:T(8,128)(2,1)}, bf16[2,256,16]{2,1,0:T(8,128)(2,1)S(1)}, u32[]{:S(2)}, u32[]{:S(2)}) collective-permute-start(bf16[2,256,16]{2,1,0:T(8,128)(2,1)} %get-tuple-element.55), channel_id=1, source_target_pairs={{0,1},{1,2},{2,3},{3,4},{4,5},{5,6},{6,7},{7,8},{8,9},{9,10},{10,1... | collective-permute-start | bytes 49160 | tf_op jit(solution)/shard_map/ppermute | solution.py:22
  71.0 1.6 %copy-start.4 = (f32[2,256,1024]{2,1,0:T(8,128)S(1)}, f32[2,256,1024]{2,1,0:T(8,128)}, u32[]{:S(2)}) copy-start(f32[2,256,1024]{2,1,0:T(8,128)} %get-tuple-element.40) | copy-start | bytes 6291460
  72.6 1.6 %copy-start.3 = (f32[2,256,1024]{2,1,0:T(8,128)S(1)}, f32[2,256,1024]{2,1,0:T(8,128)}, u32[]{:S(2)}) copy-start(f32[2,256,1024]{2,1,0:T(8,128)} %get-tuple-element.39) | copy-start | bytes 6291460
  79.9 2.2 %copy-start.6 = (f32[2,256,1024]{2,1,0:T(8,128)S(1)}, f32[2,256,1024]{2,1,0:T(8,128)}, u32[]{:S(2)}) copy-start(f32[2,256,1024]{2,1,0:T(8,128)} %get-tuple-element.38) | copy-start | bytes 6291460
  82.1 1.9 %copy-start.5 = (f32[2,256,1024]{2,1,0:T(8,128)S(1)}, f32[2,256,1024]{2,1,0:T(8,128)}, u32[]{:S(2)}) copy-start(f32[2,256,1024]{2,1,0:T(8,128)} %get-tuple-element.36) | copy-start | bytes 6291460
  82.1 3.8 %copy-start.23 = (f32[256,8]{1,0:T(8,128)S(1)}, f32[256,8]{1,0:T(8,128)}, u32[]{:S(2)}) copy-start(f32[256,8]{1,0:T(8,128)} %get-tuple-element.23) | copy-start | bytes 24580
  82.1 3.8 %copy-start.24 = (f32[256,8]{1,0:T(8,128)S(1)}, f32[256,8]{1,0:T(8,128)}, u32[]{:S(2)}) copy-start(f32[256,8]{1,0:T(8,128)} %slice_bitcast_fusion.18) | copy-start | bytes 24580
  84.0 2.0 %copy-start.2 = (f32[64,8,8,128]{3,2,1,0:T(8,128)S(1)}, f32[64,8,8,128]{3,2,1,0:T(8,128)}, u32[]{:S(2)}) copy-start(f32[64,8,8,128]{3,2,1,0:T(8,128)} %copy.145) | copy-start | bytes 6291460
  84.0 2.0 %copy-start.7 = (f32[256,8]{1,0:T(8,128)S(1)}, f32[256,8]{1,0:T(8,128)}, u32[]{:S(2)}) copy-start(f32[256,8]{1,0:T(8,128)} %get-tuple-element.7) | copy-start | bytes 24580
  84.0 2.0 %copy-start.8 = (f32[256,8]{1,0:T(8,128)S(1)}, f32[256,8]{1,0:T(8,128)}, u32[]{:S(2)}) copy-start(f32[256,8]{1,0:T(8,128)} %get-tuple-element.8) | copy-start | bytes 24580
  84.0 2.0 %copy-start.9 = (f32[256,8]{1,0:T(8,128)S(1)}, f32[256,8]{1,0:T(8,128)}, u32[]{:S(2)}) copy-start(f32[256,8]{1,0:T(8,128)} %get-tuple-element.9) | copy-start | bytes 24580
  84.0 2.0 %copy-start.10 = (f32[256,8]{1,0:T(8,128)S(1)}, f32[256,8]{1,0:T(8,128)}, u32[]{:S(2)}) copy-start(f32[256,8]{1,0:T(8,128)} %get-tuple-element.10) | copy-start | bytes 24580
  84.0 2.2 %copy-start.11 = (f32[256,8]{1,0:T(8,128)S(1)}, f32[256,8]{1,0:T(8,128)}, u32[]{:S(2)}) copy-start(f32[256,8]{1,0:T(8,128)} %get-tuple-element.11) | copy-start | bytes 24580
  84.0 2.3 %copy-start.12 = (f32[256,8]{1,0:T(8,128)S(1)}, f32[256,8]{1,0:T(8,128)}, u32[]{:S(2)}) copy-start(f32[256,8]{1,0:T(8,128)} %get-tuple-element.12) | copy-start | bytes 24580
  84.0 2.4 %copy-start.13 = (f32[256,8]{1,0:T(8,128)S(1)}, f32[256,8]{1,0:T(8,128)}, u32[]{:S(2)}) copy-start(f32[256,8]{1,0:T(8,128)} %get-tuple-element.13) | copy-start | bytes 24580
  84.0 2.5 %copy-start.14 = (f32[256,8]{1,0:T(8,128)S(1)}, f32[256,8]{1,0:T(8,128)}, u32[]{:S(2)}) copy-start(f32[256,8]{1,0:T(8,128)} %get-tuple-element.14) | copy-start | bytes 24580
  84.1 2.6 %copy-start.15 = (f32[256,8]{1,0:T(8,128)S(1)}, f32[256,8]{1,0:T(8,128)}, u32[]{:S(2)}) copy-start(f32[256,8]{1,0:T(8,128)} %get-tuple-element.15) | copy-start | bytes 24580
  84.1 2.6 %copy-start.16 = (f32[256,8]{1,0:T(8,128)S(1)}, f32[256,8]{1,0:T(8,128)}, u32[]{:S(2)}) copy-start(f32[256,8]{1,0:T(8,128)} %get-tuple-element.16) | copy-start | bytes 24580
  84.1 2.6 %copy-start.17 = (f32[256,8]{1,0:T(8,128)S(1)}, f32[256,8]{1,0:T(8,128)}, u32[]{:S(2)}) copy-start(f32[256,8]{1,0:T(8,128)} %get-tuple-element.17) | copy-start | bytes 24580
  84.1 2.6 %copy-start.18 = (f32[256,8]{1,0:T(8,128)S(1)}, f32[256,8]{1,0:T(8,128)}, u32[]{:S(2)}) copy-start(f32[256,8]{1,0:T(8,128)} %get-tuple-element.18) | copy-start | bytes 24580
  84.1 2.7 %copy-start.19 = (f32[256,8]{1,0:T(8,128)S(1)}, f32[256,8]{1,0:T(8,128)}, u32[]{:S(2)}) copy-start(f32[256,8]{1,0:T(8,128)} %get-tuple-element.19) | copy-start | bytes 24580
  84.1 2.7 %copy-start.20 = (f32[256,8]{1,0:T(8,128)S(1)}, f32[256,8]{1,0:T(8,128)}, u32[]{:S(2)}) copy-start(f32[256,8]{1,0:T(8,128)} %get-tuple-element.20) | copy-start | bytes 24580
  84.1 2.7 %copy-start.21 = (f32[256,8]{1,0:T(8,128)S(1)}, f32[256,8]{1,0:T(8,128)}, u32[]{:S(2)}) copy-start(f32[256,8]{1,0:T(8,128)} %get-tuple-element.21) | copy-start | bytes 24580
  84.1 2.8 %copy-start.22 = (f32[256,8]{1,0:T(8,128)S(1)}, f32[256,8]{1,0:T(8,128)}, u32[]{:S(2)}) copy-start(f32[256,8]{1,0:T(8,128)} %get-tuple-element.22) | copy-start | bytes 24580
  96.2 2.7 %copy-start.27 = (bf16[1,16,2,16]{3,1,2,0:T(8,128)(2,1)S(1)}, bf16[1,16,2,16]{3,1,2,0:T(8,128)(2,1)}, u32[]{:S(2)}) copy-start(bf16[1,16,2,16]{3,1,2,0:T(8,128)(2,1)} %get-tuple-element.80) | copy-start | bytes 3076
  96.2 2.7 %copy-start.28 = (bf16[1,16,2,16]{3,1,2,0:T(8,128)(2,1)S(1)}, bf16[1,16,2,16]{3,1,2,0:T(8,128)(2,1)}, u32[]{:S(2)}) copy-start(bf16[1,16,2,16]{3,1,2,0:T(8,128)(2,1)} %get-tuple-element.83) | copy-start | bytes 3076
  99.4 1.2 %copy-start.26 = (f32[16,16]{0,1:T(8,128)S(1)}, f32[16,16]{0,1:T(8,128)}, u32[]{:S(2)}) copy-start(f32[16,16]{0,1:T(8,128)} %broadcast_multiply_fusion.3) | copy-start | bytes 3076
  101.0 2.1 %copy-start.1 = (f32[16,8]{0,1:T(8,128)S(1)}, f32[16,8]{0,1:T(8,128)}, u32[]{:S(2)}) copy-start(f32[16,8]{0,1:T(8,128)} %param.9) | copy-start | bytes 1540
where the time goes:
time: 105 us; the launch traced here: 103 us
  local copies, waits for them, and re-layouts  50.4 us (48%)
  other arithmetic  35.1 us (33%)
  starting transfers between devices  12.3 us (12%)
  matrix products  4.52 us (4%)
    unnamed x88, local copies, waits for them, and re-layouts  21.5 us
    convert_element_type x3, other arithmetic, local(): summed = summed + spread[offset_index][None, :, :, None] * window  15 us
    add x1, other arithmetic, local(): summed = summed + spread[offset_index][None, :, :, None] * window  9.29 us
    all_to_all x1, starting transfers between devices, local(): lax.all_to_all(blocks, 'range', split_axis=2, concat_axis=1, tiled=True)  6.71 us
    eq x9, local copies, waits for them, and re-layouts, local(): shift_rows[None] + tap_index == offsets[:, None, None]  5.69 us
    broadcast_in_dim x8, local copies, waits for them, and re-layouts, local(): jnp.where(shift_rows[None] + tap_index == offsets[:, None, None], weights...  4.97 us
    another operation x12, other arithmetic  4.75 us
    dot_general x8, matrix products, product_of(): jnp.einsum(pattern, matrix, values, preferred_element_type=jnp.float32)  4.36 us
  transfers between devices with their start and end apart: 3, of which 0 were waited for; matrix products, arithmetic and copies ran while one was open for 48% of the time, Pallas kernels for 0%

commit v1 on v0

v1 whole, which is shorter than its diff:
```python
import functools
import math

import jax
import jax.numpy as jnp
import numpy as np
from jax import lax
from jax.experimental import pallas as pl
from jax.experimental.pallas import tpu as pltpu
from jax.sharding import PartitionSpec as P

R1 = 128
RB = 128
MAXSHIFT = 12
LANES = 128
SUB = 8
SLOT = 32
LEFT = 8
BF = jnp.bfloat16
F32 = jnp.float32


def rounded(values):
    return np.asarray(np.asarray(values, np.float32), BF).astype(np.float64)


def unit(rows, columns, length, orient):
    angles = 2.0 * math.pi / length * (np.outer(rows, columns) % length)
    return rounded(np.cos(angles)) + 1j * orient * rounded(np.sin(angles))


def turn(rows, columns, length, orient):
    angles = 2.0 * math.pi / length * (np.outer(rows, columns) % length)
    return np.exp(1j * orient * angles)


def real_form(matrix):
    return np.stack(
        [np.stack([matrix.real, -matrix.imag], 1), np.stack([matrix.imag, matrix.real], 1)], 0
    )


def as_bf(values):
    return np.asarray(np.asarray(values, np.float32), BF)


def planes(values):
    return np.asarray(np.stack([values.real, values.imag], 0), np.float32)


def dot(left, right):
    return jnp.dot(left, right, preferred_element_type=F32)


def dot_t(left, right):
    return lax.dot_general(left, right, (((1,), (1,)), ((), ())), preferred_element_type=F32)


def compress_kernel(
    dests, x_ref, e1_ref, t1_ref, w2_ref, r_ref, w3_ref, t3_ref, e4_ref, out_ref, s_in, s_out
):
    pulses = x_ref.shape[1]
    second = t1_ref.shape[2]
    first = R1
    blocks = first // dests
    scale = 1.0 / math.sqrt(first)
    for part in range(2):
        for n1 in range(first):
            s_in[part, pl.ds(n1 * pulses, pulses), :] = x_ref[
                part, :, n1 * second : (n1 + 1) * second
            ].astype(F32)

    def pair(group, carry):
        lines = []
        for k in range(2):
            p = group * 2 + k
            lines.append(
                jnp.concatenate(
                    [s_in[part, pl.ds(p, first, stride=pulses), :].astype(BF) for part in range(2)],
                    0,
                )
            )
        half = dot(e1_ref[...], jnp.concatenate(lines, 1))
        rows = []
        for k in range(2):
            re = half[:first, k * second : (k + 1) * second]
            im = half[first:, k * second : (k + 1) * second]
            tr, ti = t1_ref[0], t1_ref[1]
            rows.append(
                jnp.concatenate([(re * tr - im * ti).astype(BF), (re * ti + im * tr).astype(BF)], 1)
            )
        spec = dot(jnp.concatenate(rows, 0), w2_ref[...])
        rows = []
        for k in range(2):
            re = spec[k * first : (k + 1) * first, :second]
            im = spec[k * first : (k + 1) * first, second:]
            tr, ti = r_ref[0], r_ref[1]
            rows.append(
                jnp.concatenate([(re * tr - im * ti).astype(BF), (re * ti + im * tr).astype(BF)], 1)
            )
        back = dot(jnp.concatenate(rows, 0), w3_ref[...])
        lines = []
        for k in range(2):
            re = back[k * first : (k + 1) * first, :second]
            im = back[k * first : (k + 1) * first, second:]
            tr, ti = t3_ref[0], t3_ref[1]
            lines.append(
                jnp.concatenate([(re * tr - im * ti).astype(BF), (re * ti + im * tr).astype(BF)], 0)
            )
        done = dot(e4_ref[...], jnp.concatenate(lines, 1))
        for k in range(2):
            p = group * 2 + k
            s_out[pl.ds(pl.multiple_of(p * 2 * first, 2 * first), 2 * first), :] = (
                done[:, k * second : (k + 1) * second] * scale
            )
        return carry

    lax.fori_loop(0, pulses // 2, pair, 0)

    def tile(dest, part, block):
        row = (dest * 2 + part) * blocks + block
        return s_out[pl.ds(row, pulses, stride=2 * first), :]

    lane = lax.broadcasted_iota(jnp.int32, (SUB, LANES), 1)
    for dest in range(dests):
        for part in range(2):
            for block in range(blocks):
                row = (part * blocks + block) * pulses
                out_ref[dest, row : row + pulses, :] = tile(dest, part, block).astype(BF)
        halo = jnp.zeros((SUB, LANES), F32)
        for part in range(2):
            after = tile(dest + 1, part, 0) if dest + 1 < dests else None
            before = tile(dest - 1, part, blocks - 1) if dest > 0 else None
            for h in range(pulses // SUB):
                piece = jnp.zeros((SUB, LANES), F32)
                if after is not None:
                    piece = jnp.where(lane < 2 * SUB, after[h * SUB : (h + 1) * SUB], piece)
                if before is not None:
                    piece = jnp.where(lane >= LANES - 3, before[h * SUB : (h + 1) * SUB], piece)
                slot = part * (pulses // SUB) + h
                halo = halo + (pltpu.roll(piece, SLOT * slot, 1) if slot else piece)
        row = 2 * blocks * pulses
        out_ref[dest, row : row + SUB, :] = halo.astype(BF)


def params_kernel(ph_ref, k_ref, c_ref, a_ref, w_ref, ar_ref):
    blocks, bins = ph_ref.shape
    phases, taps = k_ref.shape
    phase = ph_ref[...]
    rows = [jnp.zeros((blocks, bins), F32) for _ in range(taps)]
    for q in range(phases):
        hit = phase == q
        for t in range(taps):
            rows[t] = jnp.where(hit, k_ref[q, t], rows[t])
    for t in range(taps):
        for h in range(bins // LANES):
            w_ref[t, h * blocks : (h + 1) * blocks, :] = rows[t][:, h * LANES : (h + 1) * LANES]
    for part in range(2):
        for b in range(blocks):
            line = pltpu.roll(a_ref[part, b : b + 1, :], c_ref[b], 1)
            for h in range(bins // LANES):
                ar_ref[part, h * blocks + b : h * blocks + b + 1, :] = line[
                    :, h * LANES : (h + 1) * LANES
                ]


def focus_kernel(y_ref, mf_ref, mi_ref, eye_ref, edge_ref, s_ref, w_ref, a_ref, out_ref, x_ref):
    sources = y_ref.shape[0]
    bins = out_ref.shape[1]
    cells = out_ref.shape[2]
    blocks = cells // RB
    pulses = bins // sources
    taps = w_ref.shape[0]
    halves = bins // LANES
    q_rows = halves * blocks
    stride = 2 * q_rows
    lead = taps // 2 - 1

    def put(jj, count, part, h, b, values):
        x_ref[pl.ds(jj * stride + part * q_rows + h * blocks + b, count, stride=stride), :] = values

    for first in range(0, blocks, 2):
        own = []
        for b in range(first, first + 2):
            own.append(
                jnp.concatenate(
                    [
                        y_ref[r, (o * blocks + b) * pulses : (o * blocks + b + 1) * pulses, :]
                        for r in range(sources)
                        for o in range(2)
                    ],
                    0,
                )
            )
        dop = dot(mf_ref[...], jnp.concatenate(own, 1)).astype(BF)
        turned = dot_t(eye_ref[...], dop)
        for k in range(2):
            b = first + k
            for part in range(2):
                for h in range(halves):
                    col = part * bins + h * LANES
                    here = turned[k * RB : (k + 1) * RB, col : col + LANES]
                    put(LEFT, RB, part, h, b, here)
                    if b > 0:
                        put(LEFT + RB, 2 * SUB, part, h, b - 1, here[: 2 * SUB])
                    if b + 1 < blocks:
                        put(0, LEFT, part, h, b + 1, here[RB - LEFT :])
    own = []
    for r in range(sources):
        held = y_ref[r, 2 * blocks * pulses : 2 * blocks * pulses + SUB, :].astype(F32)
        for o in range(2):
            for h in range(pulses // SUB):
                slot = o * (pulses // SUB) + h
                own.append(pltpu.roll(held, LANES - SLOT * slot, 1) if slot else held)
    dop = dot(mf_ref[...], jnp.concatenate(own, 0).astype(BF)).astype(BF)
    turned = dot_t(edge_ref[...], dop)
    for part in range(2):
        for h in range(halves):
            col = part * bins + h * LANES
            put(LEFT + RB, 2 * SUB, part, h, blocks - 1, turned[: 2 * SUB, col : col + LANES])
            put(0, LEFT, part, h, 0, turned[2 * SUB : 3 * SUB, col : col + LANES])

    for g in range(q_rows // SUB):
        shift = s_ref[g * SUB : (g + 1) * SUB, :]
        bits = [(shift & (1 << k)) != 0 for k in range(4)]
        weights = [w_ref[t, g * SUB : (g + 1) * SUB, :] for t in range(taps)]
        for part in range(2):
            base = part * q_rows + g * SUB
            seen = [{} for _ in range(5)]

            def moved(level, i):
                if i not in seen[level]:
                    if level == 0:
                        row = (i + LEFT - lead) * stride + base
                        seen[0][i] = x_ref[row : row + SUB, :]
                    else:
                        step = 1 << (level - 1)
                        seen[level][i] = jnp.where(
                            bits[level - 1], moved(level - 1, i + step), moved(level - 1, i)
                        )
                return seen[level][i]

            for j in range(RB):
                total = weights[0] * moved(4, j)
                for t in range(1, taps):
                    total = total + weights[t] * moved(4, j + t)
                x_ref[j * stride + base : j * stride + base + SUB, :] = total

    for first in range(0, blocks, 2):
        lines = []
        for b in range(first, first + 2):
            re_parts, im_parts = [], []
            for h in range(halves):
                q = h * blocks + b
                re = x_ref[pl.ds(q, RB, stride=stride), :]
                im = x_ref[pl.ds(q_rows + q, RB, stride=stride), :]
                ar = a_ref[0, q : q + 1, :]
                ai = a_ref[1, q : q + 1, :]
                re_parts.append((re * ar - im * ai).astype(BF))
                im_parts.append((re * ai + im * ar).astype(BF))
            lines.append(jnp.concatenate(re_parts + im_parts, 1))
        image = dot_t(mi_ref[...], jnp.concatenate(lines, 0)).astype(BF)
        for part in range(2):
            out_ref[part, :, first * RB : (first + 2) * RB] = image[part * bins : (part + 1) * bins]


def vmem(count):
    return [pl.BlockSpec(memory_space=pltpu.VMEM)] * count


def local(echoes, range_reference, kernels, shifts, phase_index, centroid, azimuth_reference):
    ranks = lax.axis_size("range")
    pulses, samples = echoes.shape[1:]
    first, second = R1, samples // R1
    cells = samples // ranks
    blocks = cells // RB
    bins = ranks * pulses
    taps = kernels.shape[1]
    halves = bins // LANES
    q_rows = halves * blocks
    assert second == RB and pulses == 2 * SUB and bins % LANES == 0 and blocks % 2 == 0

    n1, n2 = np.arange(first), np.arange(second)
    e1 = real_form(unit(n1, n1, first, -1.0)).reshape(2 * first, 2 * first)
    t1 = turn(n1, n2, samples, -1.0) / math.sqrt(first)
    w2 = real_form(unit(n2, n2, second, -1.0)).transpose(2, 3, 0, 1).reshape(2 * second, 2 * second)
    w3 = real_form(unit(n2, n2, second, 1.0)).transpose(2, 3, 0, 1).reshape(2 * second, 2 * second)
    t3 = turn(n1, n2, samples, 1.0) / math.sqrt(second)
    e4 = real_form(unit(n1, n1, first, 1.0)).reshape(2, ranks, blocks, 2 * first)
    e4 = e4.transpose(1, 0, 2, 3).reshape(2 * first, 2 * first)
    slots = range_reference.reshape(2, second, first).transpose(0, 2, 1) * (1.0 / math.sqrt(second))
    rows = 2 * blocks * pulses + SUB
    sent = pl.pallas_call(
        functools.partial(compress_kernel, ranks),
        out_shape=jax.ShapeDtypeStruct((ranks, rows, LANES), BF),
        in_specs=vmem(8),
        out_specs=pl.BlockSpec(memory_space=pltpu.VMEM),
        scratch_shapes=[
            pltpu.VMEM((2, first * pulses, second), F32),
            pltpu.VMEM((pulses * 2 * first, second), F32),
        ],
        compiler_params=pltpu.CompilerParams(vmem_limit_bytes=40 << 20),
        name="compress",
    )(echoes, as_bf(e1), planes(t1), as_bf(w2), slots, as_bf(w3), planes(t3), as_bf(e4))

    arrived = lax.all_to_all(sent, "range", 0, 0)

    weights, turned = pl.pallas_call(
        params_kernel,
        out_shape=(
            jax.ShapeDtypeStruct((taps, q_rows, LANES), F32),
            jax.ShapeDtypeStruct((2, q_rows, LANES), F32),
        ),
        in_specs=[
            pl.BlockSpec(memory_space=pltpu.VMEM),
            pl.BlockSpec(memory_space=pltpu.SMEM),
            pl.BlockSpec(memory_space=pltpu.SMEM),
            pl.BlockSpec(memory_space=pltpu.VMEM),
        ],
        out_specs=tuple(vmem(2)),
        name="params",
    )(phase_index, kernels, centroid, azimuth_reference)
    spots = shifts.reshape(blocks, halves, LANES).transpose(1, 0, 2).reshape(q_rows, LANES)

    f = np.arange(bins)
    k1, k2 = f % ranks, f // ranks
    r, p = np.arange(ranks), np.arange(pulses)
    ahead = (
        unit(k1, r, ranks, -1.0)[:, :, None]
        * (turn(k1, p, bins, -1.0) * unit(k2, p, pulses, -1.0))[:, None, :]
        / math.sqrt(bins)
    )
    ahead = real_form(ahead.reshape(bins, bins)).reshape(2 * bins, 2, ranks, pulses)
    ahead = ahead.transpose(0, 2, 1, 3).reshape(2 * bins, 2 * bins)
    behind = (
        unit(r, k1, ranks, 1.0)[:, None, :]
        * (turn(p, k1, bins, 1.0) * unit(p, k2, pulses, 1.0))[None, :, :]
        / math.sqrt(bins)
    )
    behind = real_form(behind.reshape(bins, bins)).reshape(2 * bins, 2 * bins)
    edge = np.zeros((SLOT, LANES))
    edge[: 2 * SUB, : 2 * SUB] = np.eye(2 * SUB)
    edge[2 * SUB : 3 * SUB, LANES - SUB :] = np.eye(SUB)
    span = LEFT + RB + 3 * SUB
    return pl.pallas_call(
        focus_kernel,
        out_shape=jax.ShapeDtypeStruct((2, bins, cells), BF),
        in_specs=vmem(8),
        out_specs=pl.BlockSpec(memory_space=pltpu.VMEM),
        scratch_shapes=[pltpu.VMEM((span * 2 * q_rows, LANES), F32)],
        compiler_params=pltpu.CompilerParams(vmem_limit_bytes=48 << 20),
        name="focus",
    )(
        arrived,
        as_bf(ahead),
        as_bf(behind),
        as_bf(np.eye(2 * RB)),
        as_bf(edge),
        spots,
        weights,
        turned,
    )


def solution(mesh):
    in_specs = (
        P("groups", "range", None),
        P(),
        P(),
        P("range", None),
        P("range", None),
        P("range"),
        P(None, "range", None),
    )
    out_specs = P("groups", None, "range")
    return jax.shard_map(local, mesh=mesh, in_specs=in_specs, out_specs=out_specs, check_vma=False)
```

time: 105 us -> 57.5 us (0.55); the launches traced: 103 us -> 56.9 us
  local copies, waits for them, and re-layouts: 50.4 us -> 8.99 us
  other arithmetic: 35.1 us -> 0.97 us
  waiting for transfers between devices: 0.01 us -> 23.3 us
  Pallas kernels: 0 us -> 16.9 us
  starting transfers between devices: 12.3 us -> 6.72 us
  matrix products: 4.52 us -> 0 us
    all_to_all x1, waiting for transfers between devices: 0.01 us -> 23.3 us  [local(): arrived = lax.all_to_all(sent, 'range', 0, 0)]
    pallas_call x0 -> x3, Pallas kernels: none -> 16.9 us  [the longest x1 8.43 us: local(): pl.pallas_call(functools.partial(compress_kernel, ranks), out_shape=jax.S...]
    convert_element_type x3 -> x0, other arithmetic: 15 us -> none  [local(): summed = summed + spread[offset_index][None, :, :, None] * window]
    add x2 -> x0, other arithmetic: 12.7 us -> none  [the longest x1 9.29 us: local(): summed = summed + spread[offset_index][None, :, :, None] * window]
    unnamed x88 -> x32, local copies, waits for them, and re-layouts: 21.5 us -> 8.9 us
    eq x10 -> x0, local copies, waits for them, and re-layouts: 5.78 us -> none  [the longest x9 5.69 us: local(): shift_rows[None] + tap_index == offsets[:, None, None]]
    ppermute x2 -> x0, starting transfers between devices: 5.55 us -> none  [the longest x1 3.26 us: extended(): lax.ppermute(tail, axis, [(i, (i + 1) % count) for i in range(ends)])]
    another operation x15 -> x0, other arithmetic: 5.48 us -> none
  transfers between devices with their start and end apart: 3 -> 1, of which waited for: 0 -> 1; matrix products, arithmetic and copies ran while one was open for 48% -> 1% of each run, Pallas kernels for 0% -> 3%
where the time goes in v1:
time: 57.5 us; the launch traced here: 56.9 us
  waiting for transfers between devices  23.3 us (41%)
  Pallas kernels  16.9 us (29%)
  local copies, waits for them, and re-layouts  8.99 us (16%)
  starting transfers between devices  6.72 us (12%)
  other arithmetic  0.97 us (2%)
    all_to_all x1, waiting for transfers between devices, local(): arrived = lax.all_to_all(sent, 'range', 0, 0)  23.3 us
    unnamed x32, local copies, waits for them, and re-layouts  8.9 us
    pallas_call x1, Pallas kernels, local(): pl.pallas_call(functools.partial(compress_kernel, ranks), out_shape=jax.S...  8.43 us
    pallas_call x1, Pallas kernels, local(): pl.pallas_call(focus_kernel, out_shape=jax.ShapeDtypeStruct((2, bins, cel...  6.83 us
    all_to_all x1, starting transfers between devices, local(): arrived = lax.all_to_all(sent, 'range', 0, 0)  6.72 us
    pallas_call x1, Pallas kernels, local(): pl.pallas_call(params_kernel, out_shape=(jax.ShapeDtypeStruct((taps, q_ro...  1.65 us
  transfers between devices with their start and end apart: 1, of which 1 were waited for; matrix products, arithmetic and copies ran while one was open for 1% of the time, Pallas kernels for 3%

profile of v1, /device:TPU:9, one launch (start us, length us, event | category | flops | bytes accessed | tf_op | source)
XLA Modules:
  0.0 56.9 jit_solution(3939985077768939528)
XLA Ops:
  0.0 1.0 %multiply_bitcast_fusion = f32[1,2,128,128]{3,1,2,0:T(2,128)S(1)} fusion(f32[2,16384]{1,0:T(2,128)} %param.18), kind=kLoop, calls=%fused_computation.1 | loop fusion | flops 32768 | bytes 262144
  1.0 0.1 copy.19
  1.1 0.0 copy-start
  1.1 1.2 %copy-done = bf16[2,16,16384]{2,1,0:T(8,128)(2,1)S(1)} copy-done((bf16[2,16,16384]{2,1,0:T(8,128)(2,1)S(1)}, bf16[2,16,16384]{2,1,0:T(8,128)(2,1)}, u32[]{:S(2)}) %copy-start) | copy-done | bytes 1048600
  2.3 0.0 copy-start.3
  2.3 0.9 %copy-done.3 = bf16[256,256]{1,0:T(8,128)(2,1)S(1)} copy-done((bf16[256,256]{1,0:T(8,128)(2,1)S(1)}, bf16[256,256]{1,0:T(8,128)(2,1)}, u32[]{:S(2)}) %copy-start.3) | copy-done | bytes 131096
  3.2 0.0 copy-start.4
  3.2 0.9 %copy-done.4 = f32[2,128,128]{2,1,0:T(8,128)S(1)} copy-done((f32[2,128,128]{2,1,0:T(8,128)S(1)}, f32[2,128,128]{2,1,0:T(8,128)}, u32[]{:S(2)}) %copy-start.4) | copy-done | bytes 131096
  4.1 0.0 copy-start.5
  4.1 0.9 %copy-done.5 = bf16[256,256]{1,0:T(8,128)(2,1)S(1)} copy-done((bf16[256,256]{1,0:T(8,128)(2,1)S(1)}, bf16[256,256]{1,0:T(8,128)(2,1)}, u32[]{:S(2)}) %copy-start.5) | copy-done | bytes 131096
  5.0 0.0 copy-start.6
  5.0 0.9 %copy-done.6 = bf16[256,256]{1,0:T(8,128)(2,1)S(1)} copy-done((bf16[256,256]{1,0:T(8,128)(2,1)S(1)}, bf16[256,256]{1,0:T(8,128)(2,1)}, u32[]{:S(2)}) %copy-start.6) | copy-done | bytes 131096
  5.9 0.0 copy-start.7
  5.9 0.9 %copy-done.7 = f32[2,128,128]{2,1,0:T(8,128)S(1)} copy-done((f32[2,128,128]{2,1,0:T(8,128)S(1)}, f32[2,128,128]{2,1,0:T(8,128)}, u32[]{:S(2)}) %copy-start.7) | copy-done | bytes 131096
  6.8 0.0 copy-start.8
  6.9 0.9 %copy-done.8 = bf16[256,256]{1,0:T(8,128)(2,1)S(1)} copy-done((bf16[256,256]{1,0:T(8,128)(2,1)S(1)}, bf16[256,256]{1,0:T(8,128)(2,1)}, u32[]{:S(2)}) %copy-start.8) | copy-done | bytes 131096
  7.8 8.4 %compress.1 = bf16[16,264,128]{2,1,0:T(8,128)(2,1)} custom-call(bf16[2,16,16384]{2,1,0:T(8,128)(2,1)S(1)} %copy-done, bf16[256,256]{1,0:T(8,128)(2,1)S(1)} %copy-done.3, f32[2,128,128]{2,1,0:T(8,128)S(1)} %copy-done.4, bf16[256,256]{1,0:T(8,128)(2,1)S(1)} %copy-done.5, f32[2,128,128]{2,1,0:T(8,128)S(1)} %bitcast.11, bf16[256,256]{1,0:T(8,128)(2,1)S(1)} %copy-done.6, ...), custom_call_target="tpu_custom_call" | custom-call | tf_op jit(solution)/shard_map/compress/pallas_call | solution.py:293
  16.2 0.0 copy-start.14
  16.2 0.0 copy-start.1
  16.2 0.0 copy-start.2
  16.2 0.0 copy-start.9
  16.2 0.0 copy-start.12
  16.2 0.0 copy-start.13
  16.2 6.7 %all-to-all-start = ((bf16[16,264,128]{2,1,0:T(8,128)(2,1)}), bf16[16,264,128]{2,1,0:T(8,128)(2,1)S(1)}, u32[]{:S(2)}, u32[]{:S(2)}) async-start(bf16[16,264,128]{2,1,0:T(8,128)(2,1)} %compress.1), calls=%async_computation | async-start | bytes 2162688 | tf_op jit(solution)/shard_map/all_to_all | solution.py:306
  22.9 0.0 copy-done.14
  22.9 0.7 %copy.20.k_ref = f32[16,8]{1,0:T(8,128)} copy(f32[16,8]{0,1:T(8,128)S(1)} %copy-done.14) | data formatting | bytes 1024 | tf_op args[2]
  23.6 1.7 %params.1 = (f32[8,16,128]{2,1,0:T(8,128)}, f32[2,16,128]{2,1,0:T(8,128)}) custom-call(s32[8,256]{1,0:T(8,128)} %ph_ref.1, f32[16,8]{1,0:T(8,128)} %copy.20.k_ref, s32[8]{0:T(128)} %c_ref.1, f32[2,8,256]{2,1,0:T(8,128)} %a_ref.1), custom_call_target="tpu_custom_call" | custom-call | tf_op jit(solution)/shard_map/params/pallas_call | solution.py:308
  25.3 23.3 %all-to-all-done.y_ref = bf16[16,264,128]{2,1,0:T(8,128)(2,1)S(1)} async-done(((bf16[16,264,128]{2,1,0:T(8,128)(2,1)}), bf16[16,264,128]{2,1,0:T(8,128)(2,1)S(1)}, u32[]{:S(2)}, u32[]{:S(2)}) %all-to-all-start) | async-done | bytes 1081376 | tf_op jit(solution)/shard_map/all_to_all | solution.py:306
  48.5 0.0 copy-done.1
  48.5 0.0 copy-done.2
  48.5 0.0 copy-done.9
  48.5 0.0 copy-done.12
  48.5 0.0 copy-done.13
  48.6 0.0 copy-start.10
  48.6 0.8 %copy-done.10 = f32[8,16,128]{2,1,0:T(8,128)S(1)} copy-done((f32[8,16,128]{2,1,0:T(8,128)S(1)}, f32[8,16,128]{2,1,0:T(8,128)}, u32[]{:S(2)}) %copy-start.10) | copy-done | bytes 65560
  49.4 0.0 copy-start.11
  49.4 0.7 %copy-done.11 = f32[2,16,128]{2,1,0:T(8,128)S(1)} copy-done((f32[2,16,128]{2,1,0:T(8,128)S(1)}, f32[2,16,128]{2,1,0:T(8,128)}, u32[]{:S(2)}) %copy-start.11) | copy-done | bytes 16408
  50.1 6.8 %focus.1 = bf16[2,256,1024]{2,1,0:T(8,128)(2,1)} custom-call(bf16[16,264,128]{2,1,0:T(8,128)(2,1)S(1)} %all-to-all-done.y_ref, bf16[512,512]{1,0:T(8,128)(2,1)S(1)} %copy-done.1, bf16[512,512]{1,0:T(8,128)(2,1)S(1)} %copy-done.2, bf16[256,256]{1,0:T(8,128)(2,1)S(1)} %copy-done.9, bf16[32,128]{1,0:T(8,128)(2,1)S(1)} %copy-done.13, s32[16,128]{1,0:T(8,128)S(1)} %bitcast.12, ...), custom_call_target="tpu_custom_call" | custom-call | tf_op jit(solution)/shard_map/focus/pallas_call | solution.py:345
  (1 shorter events, 0.0 us)
Async XLA Ops:
  1.1 1.2 %copy-start = (bf16[2,16,16384]{2,1,0:T(8,128)(2,1)S(1)}, bf16[2,16,16384]{2,1,0:T(8,128)(2,1)}, u32[]{:S(2)}) copy-start(bf16[2,16,16384]{2,1,0:T(8,128)(2,1)} %x_ref.1) | copy-start | bytes 3145732
  2.3 0.9 %copy-start.3 = (bf16[256,256]{1,0:T(8,128)(2,1)S(1)}, bf16[256,256]{1,0:T(8,128)(2,1)}, u32[]{:S(2)}) copy-start(bf16[256,256]{1,0:T(8,128)(2,1)} %constant.22.clone.e1_ref) | copy-start | bytes 393220
  3.2 0.9 %copy-start.4 = (f32[2,128,128]{2,1,0:T(8,128)S(1)}, f32[2,128,128]{2,1,0:T(8,128)}, u32[]{:S(2)}) copy-start(f32[2,128,128]{2,1,0:T(8,128)} %constant.23.clone.t1_ref) | copy-start | bytes 393220
  4.1 0.9 %copy-start.5 = (bf16[256,256]{1,0:T(8,128)(2,1)S(1)}, bf16[256,256]{1,0:T(8,128)(2,1)}, u32[]{:S(2)}) copy-start(bf16[256,256]{1,0:T(8,128)(2,1)} %constant.24.clone.w2_ref) | copy-start | bytes 393220
  5.0 0.9 %copy-start.6 = (bf16[256,256]{1,0:T(8,128)(2,1)S(1)}, bf16[256,256]{1,0:T(8,128)(2,1)}, u32[]{:S(2)}) copy-start(bf16[256,256]{1,0:T(8,128)(2,1)} %constant.25.clone.w3_ref) | copy-start | bytes 393220
  5.9 0.9 %copy-start.7 = (f32[2,128,128]{2,1,0:T(8,128)S(1)}, f32[2,128,128]{2,1,0:T(8,128)}, u32[]{:S(2)}) copy-start(f32[2,128,128]{2,1,0:T(8,128)} %constant.26.clone.t3_ref) | copy-start | bytes 393220
  6.8 0.9 %copy-start.8 = (bf16[256,256]{1,0:T(8,128)(2,1)S(1)}, bf16[256,256]{1,0:T(8,128)(2,1)}, u32[]{:S(2)}) copy-start(bf16[256,256]{1,0:T(8,128)(2,1)} %constant.27.clone.e4_ref) | copy-start | bytes 393220
  16.2 6.8 %copy-start.14 = (f32[16,8]{0,1:T(8,128)S(1)}, f32[16,8]{0,1:T(8,128)}, u32[]{:S(2)}) copy-start(f32[16,8]{0,1:T(8,128)} %param.19) | copy-start | bytes 1540
  16.2 32.3 %copy-start.1 = (bf16[512,512]{1,0:T(8,128)(2,1)S(1)}, bf16[512,512]{1,0:T(8,128)(2,1)}, u32[]{:S(2)}) copy-start(bf16[512,512]{1,0:T(8,128)(2,1)} %constant.28.clone.mf_ref) | copy-start | bytes 1572868
  16.2 32.3 %copy-start.2 = (bf16[512,512]{1,0:T(8,128)(2,1)S(1)}, bf16[512,512]{1,0:T(8,128)(2,1)}, u32[]{:S(2)}) copy-start(bf16[512,512]{1,0:T(8,128)(2,1)} %constant.29.clone.mi_ref) | copy-start | bytes 1572868
  16.2 32.3 %copy-start.9 = (bf16[256,256]{1,0:T(8,128)(2,1)S(1)}, bf16[256,256]{1,0:T(8,128)(2,1)}, u32[]{:S(2)}) copy-start(bf16[256,256]{1,0:T(8,128)(2,1)} %constant.30.clone.eye_ref) | copy-start | bytes 393220
  16.2 32.3 %copy-start.12 = (s32[8,256]{1,0:T(8,128)S(1)}, s32[8,256]{1,0:T(8,128)}, u32[]{:S(2)}) copy-start(s32[8,256]{1,0:T(8,128)} %param.20) | copy-start | bytes 24580
  16.2 32.3 %copy-start.13 = (bf16[32,128]{1,0:T(8,128)(2,1)S(1)}, bf16[32,128]{1,0:T(8,128)(2,1)}, u32[]{:S(2)}) copy-start(bf16[32,128]{1,0:T(8,128)(2,1)} %constant.31.clone.edge_ref) | copy-start | bytes 24580
  16.2 32.3 %all-to-all-start = ((bf16[16,264,128]{2,1,0:T(8,128)(2,1)}), bf16[16,264,128]{2,1,0:T(8,128)(2,1)S(1)}, u32[]{:S(2)}, u32[]{:S(2)}) async-start(bf16[16,264,128]{2,1,0:T(8,128)(2,1)} %compress.1), calls=%async_computation | async-start | bytes 2162688 | tf_op jit(solution)/shard_map/all_to_all | solution.py:306
  48.6 0.8 %copy-start.10 = (f32[8,16,128]{2,1,0:T(8,128)S(1)}, f32[8,16,128]{2,1,0:T(8,128)}, u32[]{:S(2)}) copy-start(f32[8,16,128]{2,1,0:T(8,128)} %get-tuple-element.7.w_ref) | copy-start | bytes 196612
  49.4 0.7 %copy-start.11 = (f32[2,16,128]{2,1,0:T(8,128)S(1)}, f32[2,16,128]{2,1,0:T(8,128)}, u32[]{:S(2)}) copy-start(f32[2,16,128]{2,1,0:T(8,128)} %get-tuple-element.8.a_ref) | copy-start | bytes 49156

commit v2 on v1

v2 whole, which is shorter than its diff:
```python
import functools
import math

import jax
import jax.numpy as jnp
import numpy as np
from jax import lax
from jax.experimental import pallas as pl
from jax.experimental.pallas import tpu as pltpu
from jax.sharding import PartitionSpec as P

R1 = 128
RB = 128
MAXSHIFT = 12
LANES = 128
SUB = 8
SLOT = 32
LEFT = 8
BF = jnp.bfloat16
F32 = jnp.float32
TAP = BF
AT_ONCE = 16


def rounded(values):
    return np.asarray(np.asarray(values, np.float32), BF).astype(np.float64)


def unit(rows, columns, length, orient):
    angles = 2.0 * math.pi / length * (np.outer(rows, columns) % length)
    return rounded(np.cos(angles)) + 1j * orient * rounded(np.sin(angles))


def turn(rows, columns, length, orient):
    angles = 2.0 * math.pi / length * (np.outer(rows, columns) % length)
    return np.exp(1j * orient * angles)


def real_form(matrix):
    return np.stack(
        [np.stack([matrix.real, -matrix.imag], 1), np.stack([matrix.imag, matrix.real], 1)], 0
    )


def as_bf(values):
    return np.asarray(np.asarray(values, np.float32), BF)


def planes(values):
    return np.asarray(np.stack([values.real, values.imag], 0), np.float32)


def dot(left, right):
    return jnp.dot(left, right, preferred_element_type=F32)


def dot_t(left, right):
    return lax.dot_general(left, right, (((1,), (1,)), ((), ())), preferred_element_type=F32)


def turned_by(values, table, axis):
    re, im = values
    tr, ti = table
    return jnp.concatenate([(re * tr - im * ti).astype(BF), (re * ti + im * tr).astype(BF)], axis)


def compress_kernel(
    dests, x_hbm, m_hbm, t_hbm, r_hbm, out_hbm, x_v, m_v, t_v, r_v, s_in, s_out, o_v, r_sq, in_sem, out_sem
):
    pulses = x_hbm.shape[1]
    samples = x_hbm.shape[2]
    first = R1
    second = samples // first
    blocks = first // dests
    scale = 1.0 / math.sqrt(first)
    gap_in = pulses + 1
    gap_out = 2 * first + 1
    parts = 2

    copies = [pltpu.make_async_copy(r_hbm, r_v, in_sem.at[0])]
    span = samples // parts
    for part in range(2):
        for k in range(parts):
            piece = pl.ds(k * span, span)
            copies.append(
                pltpu.make_async_copy(
                    x_hbm.at[part, :, piece], x_v.at[part, :, piece], in_sem.at[len(copies)]
                )
            )
    copies.append(pltpu.make_async_copy(m_hbm, m_v, in_sem.at[len(copies)]))
    copies.append(pltpu.make_async_copy(t_hbm, t_v, in_sem.at[len(copies)]))
    for copy in copies:
        copy.start()

    copies[0].wait()
    for k2 in range(second):
        r_sq[pl.ds(k2, 2, stride=second + 1), :] = r_v[:, k2 * first : (k2 + 1) * first]
    slots = []
    for part in range(2):
        row = part * (second + 1)
        slots.append(jnp.transpose(r_sq[row : row + second, :]) * (1.0 / math.sqrt(second)))
    for part in range(2):
        r_sq[part * first : (part + 1) * first, :] = slots[part]

    for part in range(2):
        for k in range(parts):
            copies[1 + part * parts + k].wait()
            for n1 in range(k * first // parts, (k + 1) * first // parts):
                row = (part * first + n1) * gap_in
                s_in[row : row + pulses, :] = x_v[part, :, n1 * second : (n1 + 1) * second].astype(
                    F32
                )
    copies[-2].wait()
    copies[-1].wait()

    for group in range(0, pulses, AT_ONCE):
        lines = []
        for p in range(group, group + AT_ONCE):
            lines.append(
                jnp.concatenate(
                    [
                        s_in[pl.ds(part * first * gap_in + p, first, stride=gap_in), :].astype(BF)
                        for part in range(2)
                    ],
                    0,
                )
            )
        half = dot(m_v[0], jnp.concatenate(lines, 1))
        table = (t_v[0], t_v[1])
        rows = []
        for k in range(AT_ONCE):
            cols = slice(k * second, (k + 1) * second)
            rows.append(turned_by((half[:first, cols], half[first:, cols]), table, 1))
        spec = dot(jnp.concatenate(rows, 0), m_v[1])
        table = (r_sq[:first, :], r_sq[first : 2 * first, :])
        rows = []
        for k in range(AT_ONCE):
            here = spec[k * first : (k + 1) * first]
            rows.append(turned_by((here[:, :second], here[:, second:]), table, 1))
        back = dot(jnp.concatenate(rows, 0), m_v[2])
        table = (t_v[2], t_v[3])
        lines = []
        for k in range(AT_ONCE):
            here = back[k * first : (k + 1) * first]
            lines.append(turned_by((here[:, :second], here[:, second:]), table, 0))
        done = dot(m_v[3], jnp.concatenate(lines, 1))
        for k in range(AT_ONCE):
            row = (group + k) * gap_out
            s_out[row : row + 2 * first, :] = done[:, k * second : (k + 1) * second] * scale

    def tile(dest, part, block):
        return s_out[pl.ds((dest * 2 + part) * blocks + block, pulses, stride=gap_out), :]

    lane = lax.broadcasted_iota(jnp.int32, (SUB, LANES), 1)
    sends = []
    for dest in range(dests):
        for part in range(2):
            for block in range(blocks):
                row = (part * blocks + block) * pulses
                o_v[dest, row : row + pulses, :] = tile(dest, part, block).astype(BF)
        halo = jnp.zeros((SUB, LANES), F32)
        for part in range(2):
            after = tile(dest + 1, part, 0) if dest + 1 < dests else None
            before = tile(dest - 1, part, blocks - 1) if dest > 0 else None
            for h in range(pulses // SUB):
                piece = jnp.zeros((SUB, LANES), F32)
                if after is not None:
                    piece = jnp.where(lane < 2 * SUB, after[h * SUB : (h + 1) * SUB], piece)
                if before is not None:
                    piece = jnp.where(lane >= LANES - 3, before[h * SUB : (h + 1) * SUB], piece)
                slot = part * (pulses // SUB) + h
                halo = halo + (pltpu.roll(piece, SLOT * slot, 1) if slot else piece)
        row = 2 * blocks * pulses
        o_v[dest, row : row + SUB, :] = halo.astype(BF)
        sends.append(pltpu.make_async_copy(o_v.at[dest], out_hbm.at[dest], out_sem.at[dest]))
        sends[-1].start()
    for send in sends:
        send.wait()


def focus_kernel(
    y_ref, mf_ref, mi_ref, eye_ref, edge_ref, s_ref, ph_ref, k_ref, c_ref, a_ref, out_ref, x_ref, ar_ref, d_ref
):
    sources = y_ref.shape[0]
    bins = out_ref.shape[1]
    cells = out_ref.shape[2]
    blocks = cells // RB
    pulses = bins // sources
    phases, taps = k_ref.shape
    halves = bins // LANES
    q_rows = halves * blocks
    stride = 2 * q_rows + 1
    lead = taps // 2 - 1

    for part in range(2):
        for b in range(blocks):
            line = pltpu.roll(a_ref[part, b : b + 1, :], c_ref[b], 1)
            for h in range(halves):
                q = h * blocks + b
                ar_ref[part, q : q + 1, :] = line[:, h * LANES : (h + 1) * LANES]

    def put(jj, count, part, h, b, values):
        x_ref[pl.ds(jj * stride + part * q_rows + h * blocks + b, count, stride=stride), :] = values

    own = []
    for b in range(blocks):
        own.append(
            jnp.concatenate(
                [
                    y_ref[r, (o * blocks + b) * pulses : (o * blocks + b + 1) * pulses, :]
                    for r in range(sources)
                    for o in range(2)
                ],
                0,
            )
        )
    side = []
    for r in range(sources):
        held = y_ref[r, 2 * blocks * pulses : 2 * blocks * pulses + SUB, :].astype(F32)
        for o in range(2):
            for h in range(pulses // SUB):
                slot = o * (pulses // SUB) + h
                side.append(pltpu.roll(held, LANES - SLOT * slot, 1) if slot else held)
    own.append(jnp.concatenate(side, 0).astype(BF))
    d_ref[...] = dot(mf_ref[...], jnp.concatenate(own, 1)).astype(BF)
    for first in range(0, blocks, 2):
        turned = dot_t(eye_ref[...], d_ref[:, first * RB : (first + 2) * RB])
        for k in range(2):
            b = first + k
            for part in range(2):
                for h in range(halves):
                    col = part * bins + h * LANES
                    here = turned[k * RB : (k + 1) * RB, col : col + LANES]
                    put(LEFT, RB, part, h, b, here)
                    if b > 0:
                        put(LEFT + RB, 2 * SUB, part, h, b - 1, here[: 2 * SUB])
                    if b + 1 < blocks:
                        put(0, LEFT, part, h, b + 1, here[RB - LEFT :])
    turned = dot_t(edge_ref[...], d_ref[:, cells:])
    for part in range(2):
        for h in range(halves):
            col = part * bins + h * LANES
            put(LEFT + RB, 2 * SUB, part, h, blocks - 1, turned[: 2 * SUB, col : col + LANES])
            put(0, LEFT, part, h, 0, turned[2 * SUB : 3 * SUB, col : col + LANES])

    high = SUB * (4 // jnp.dtype(TAP).itemsize)
    for g in range(q_rows // high):
        shift = s_ref[g * high : (g + 1) * high, :]
        phase = ph_ref[g * high : (g + 1) * high, :]
        weights = [jnp.zeros((high, LANES), F32) for _ in range(taps)]
        for q in range(phases):
            hit = phase == q
            for t in range(taps):
                weights[t] = jnp.where(hit, k_ref[q, t], weights[t])
        weights = [w.astype(TAP) for w in weights]
        if TAP == BF:
            shift = shift.astype(jnp.int16)
        bits = [(shift & (1 << k)) != 0 for k in range(4)]
        for part in range(2):
            base = part * q_rows + g * high
            seen = [{} for _ in range(5)]

            def moved(level, i):
                if i not in seen[level]:
                    if level == 0:
                        row = (i + LEFT - lead) * stride + base
                        seen[0][i] = x_ref[row : row + high, :].astype(TAP)
                    else:
                        step = 1 << (level - 1)
                        seen[level][i] = jnp.where(
                            bits[level - 1], moved(level - 1, i + step), moved(level - 1, i)
                        )
                return seen[level][i]

            for j in range(RB):
                total = weights[0] * moved(4, j)
                for t in range(1, taps):
                    total = total + weights[t] * moved(4, j + t)
                x_ref[j * stride + base : j * stride + base + high, :] = total.astype(F32)

    for first in range(0, blocks, 2):
        lines = []
        for b in range(first, first + 2):
            re_parts, im_parts = [], []
            for h in range(halves):
                q = h * blocks + b
                re = x_ref[pl.ds(q, RB, stride=stride), :]
                im = x_ref[pl.ds(q_rows + q, RB, stride=stride), :]
                ar = ar_ref[0, q : q + 1, :]
                ai = ar_ref[1, q : q + 1, :]
                re_parts.append((re * ar - im * ai).astype(BF))
                im_parts.append((re * ai + im * ar).astype(BF))
            lines.append(jnp.concatenate(re_parts + im_parts, 1))
        image = dot_t(mi_ref[...], jnp.concatenate(lines, 0)).astype(BF)
        for part in range(2):
            out_ref[part, :, first * RB : (first + 2) * RB] = image[part * bins : (part + 1) * bins]


def vmem(count):
    return [pl.BlockSpec(memory_space=pltpu.VMEM)] * count


def local(echoes, range_reference, kernels, shifts, phase_index, centroid, azimuth_reference):
    ranks = lax.axis_size("range")
    pulses, samples = echoes.shape[1:]
    first, second = R1, samples // R1
    cells = samples // ranks
    blocks = cells // RB
    bins = ranks * pulses
    taps = kernels.shape[1]
    halves = bins // LANES
    q_rows = halves * blocks
    assert second == RB and pulses == 2 * SUB and bins % LANES == 0 and blocks % 2 == 0

    n1, n2 = np.arange(first), np.arange(second)
    e1 = real_form(unit(n1, n1, first, -1.0)).reshape(2 * first, 2 * first)
    t1 = turn(n1, n2, samples, -1.0) / math.sqrt(first)
    w2 = real_form(unit(n2, n2, second, -1.0)).transpose(2, 3, 0, 1).reshape(2 * second, 2 * second)
    w3 = real_form(unit(n2, n2, second, 1.0)).transpose(2, 3, 0, 1).reshape(2 * second, 2 * second)
    t3 = turn(n1, n2, samples, 1.0) / math.sqrt(second)
    e4 = real_form(unit(n1, n1, first, 1.0)).reshape(2, ranks, blocks, 2 * first)
    e4 = e4.transpose(1, 0, 2, 3).reshape(2 * first, 2 * first)
    rows = 2 * blocks * pulses + SUB
    anywhere = pl.BlockSpec(memory_space=pl.ANY)
    sent = pl.pallas_call(
        functools.partial(compress_kernel, ranks),
        out_shape=jax.ShapeDtypeStruct((ranks, rows, LANES), BF),
        in_specs=[anywhere] * 4,
        out_specs=anywhere,
        scratch_shapes=[
            pltpu.VMEM((2, pulses, samples), BF),
            pltpu.VMEM((4, 2 * first, 2 * first), BF),
            pltpu.VMEM((4, first, second), F32),
            pltpu.VMEM((2, samples), F32),
            pltpu.VMEM((2 * first * (pulses + 1), second), F32),
            pltpu.VMEM((pulses * (2 * first + 1), second), F32),
            pltpu.VMEM((ranks, rows, LANES), BF),
            pltpu.VMEM((2 * first + SUB, second), F32),
            pltpu.SemaphoreType.DMA((8,)),
            pltpu.SemaphoreType.DMA((ranks,)),
        ],
        compiler_params=pltpu.CompilerParams(vmem_limit_bytes=60 << 20),
        name="compress",
    )(
        echoes,
        np.stack([as_bf(e1), as_bf(w2), as_bf(w3), as_bf(e4)]),
        np.concatenate([planes(t1), planes(t3)]),
        range_reference,
    )

    arrived = lax.all_to_all(sent, "range", 0, 0)

    def spread(table):
        return table.reshape(blocks, halves, LANES).transpose(1, 0, 2).reshape(q_rows, LANES)

    f = np.arange(bins)
    k1, k2 = f % ranks, f // ranks
    r, p = np.arange(ranks), np.arange(pulses)
    ahead = (
        unit(k1, r, ranks, -1.0)[:, :, None]
        * (turn(k1, p, bins, -1.0) * unit(k2, p, pulses, -1.0))[:, None, :]
        / math.sqrt(bins)
    )
    ahead = real_form(ahead.reshape(bins, bins)).reshape(2 * bins, 2, ranks, pulses)
    ahead = ahead.transpose(0, 2, 1, 3).reshape(2 * bins, 2 * bins)
    behind = (
        unit(r, k1, ranks, 1.0)[:, None, :]
        * (turn(p, k1, bins, 1.0) * unit(p, k2, pulses, 1.0))[None, :, :]
        / math.sqrt(bins)
    )
    behind = real_form(behind.reshape(bins, bins)).reshape(2 * bins, 2 * bins)
    edge = np.zeros((SLOT, LANES))
    edge[: 2 * SUB, : 2 * SUB] = np.eye(2 * SUB)
    edge[2 * SUB : 3 * SUB, LANES - SUB :] = np.eye(SUB)
    span = LEFT + RB + 3 * SUB
    return pl.pallas_call(
        focus_kernel,
        out_shape=jax.ShapeDtypeStruct((2, bins, cells), BF),
        in_specs=vmem(7)
        + [
            pl.BlockSpec(memory_space=pltpu.SMEM),
            pl.BlockSpec(memory_space=pltpu.SMEM),
            pl.BlockSpec(memory_space=pltpu.VMEM),
        ],
        out_specs=pl.BlockSpec(memory_space=pltpu.VMEM),
        scratch_shapes=[
            pltpu.VMEM((span * (2 * q_rows + 1), LANES), F32),
            pltpu.VMEM((2, q_rows, LANES), F32),
            pltpu.VMEM((2 * bins, cells + LANES), BF),
        ],
        compiler_params=pltpu.CompilerParams(vmem_limit_bytes=48 << 20),
        name="focus",
    )(
        arrived,
        as_bf(ahead),
        as_bf(behind),
        as_bf(np.eye(2 * RB)),
        as_bf(edge),
        spread(shifts),
        spread(phase_index),
        kernels,
        centroid,
        azimuth_reference,
    )


def solution(mesh):
    in_specs = (
        P("groups", "range", None),
        P(),
        P(),
        P("range", None),
        P("range", None),
        P("range"),
        P(None, "range", None),
    )
    out_specs = P("groups", None, "range")
    return jax.shard_map(local, mesh=mesh, in_specs=in_specs, out_specs=out_specs, check_vma=False)
```

time: 57.5 us -> 41.2 us (0.72)
  local copies, waits for them, and re-layouts: 8.99 us -> 0.13 us
  Pallas kernels: 16.9 us -> 8.5 us
  waiting for transfers between devices: 23.3 us -> 25.5 us
  other arithmetic: 0.97 us -> 0 us
    unnamed x32 -> x19, local copies, waits for them, and re-layouts: 8.9 us -> 0.13 us
    pallas_call x1, Pallas kernels: 8.43 us -> 4.18 us  [local(): pl.pallas_call(functools.partial(compress_kernel, ranks), out_shape=jax.S...]
    pallas_call x1, Pallas kernels: 6.83 us -> 4.33 us  [local(): pl.pallas_call(focus_kernel, out_shape=jax.ShapeDtypeStruct((2, bins, cel...]
    all_to_all x1, waiting for transfers between devices: 23.3 us -> 25.5 us  [local(): arrived = lax.all_to_all(sent, 'range', 0, 0)]
    pallas_call x1 -> x0, Pallas kernels: 1.65 us -> none  [local(): pl.pallas_call(params_kernel, out_shape=(jax.ShapeDtypeStruct((taps, q_ro...]
    unnamed x1 -> x0, other arithmetic: 0.97 us -> none
  transfers between devices with their start and end apart: 1 -> 1, of which waited for: 1 -> 1; matrix products, arithmetic and copies ran while one was open for 1% -> 0% of each run, Pallas kernels for 3% -> 0%
where the time goes in v2:
time: 41.2 us; the launch traced here: 41 us
  waiting for transfers between devices  25.5 us (62%)
  Pallas kernels  8.5 us (21%)
  starting transfers between devices  6.72 us (16%)
    all_to_all x1, waiting for transfers between devices, local(): arrived = lax.all_to_all(sent, 'range', 0, 0)  25.5 us
    all_to_all x1, starting transfers between devices, local(): arrived = lax.all_to_all(sent, 'range', 0, 0)  6.72 us
    pallas_call x1, Pallas kernels, local(): pl.pallas_call(focus_kernel, out_shape=jax.ShapeDtypeStruct((2, bins, cel...  4.33 us
    pallas_call x1, Pallas kernels, local(): pl.pallas_call(functools.partial(compress_kernel, ranks), out_shape=jax.S...  4.18 us
  transfers between devices with their start and end apart: 1, of which 1 were waited for; matrix products, arithmetic and copies ran while one was open for 0% of the time, Pallas kernels for 0%

profile of v2, /device:TPU:9, one launch (start us, length us, event | category | flops | bytes accessed | tf_op | source)
XLA Modules:
  0.0 41.0 jit_solution(5637386683924306721)
XLA Ops:
  0.0 4.2 %compress.1 = bf16[16,264,128]{2,1,0:T(8,128)(2,1)} custom-call(bf16[2,16,16384]{2,1,0:T(8,128)(2,1)} %x_hbm.1, bf16[4,256,256]{2,1,0:T(8,128)(2,1)} %constant.12.clone.m_hbm, f32[4,128,128]{2,1,0:T(8,128)} %constant.13.clone.t_hbm, f32[2,16384]{1,0:T(2,128)} %r_hbm.1), custom_call_target="tpu_custom_call" | custom-call | tf_op jit(solution)/shard_map/compress/pallas_call | solution.py:325
  4.2 0.0 copy-start.8
  4.2 0.0 copy-start
  4.2 0.0 copy-start.1
  4.2 0.0 copy-start.2
  4.2 0.0 copy-start.3
  4.2 0.0 copy-start.4
  4.3 0.0 copy-start.5
  4.3 0.0 copy-start.6
  4.3 0.0 copy-start.7
  4.3 6.7 %all-to-all-start = ((bf16[16,264,128]{2,1,0:T(8,128)(2,1)}), bf16[16,264,128]{2,1,0:T(8,128)(2,1)S(1)}, u32[]{:S(2)}, u32[]{:S(2)}) async-start(bf16[16,264,128]{2,1,0:T(8,128)(2,1)} %compress.1), calls=%async_computation | async-start | bytes 2162688 | tf_op jit(solution)/shard_map/all_to_all | solution.py:351
  11.0 0.0 copy-done.8
  11.0 0.1 copy.14.k_ref
  11.1 25.5 %all-to-all-done.y_ref = bf16[16,264,128]{2,1,0:T(8,128)(2,1)S(1)} async-done(((bf16[16,264,128]{2,1,0:T(8,128)(2,1)}), bf16[16,264,128]{2,1,0:T(8,128)(2,1)S(1)}, u32[]{:S(2)}, u32[]{:S(2)}) %all-to-all-start) | async-done | bytes 1081376 | tf_op jit(solution)/shard_map/all_to_all | solution.py:351
  36.6 0.0 copy-done
  36.6 0.0 copy-done.1
  36.6 0.0 copy-done.2
  36.6 0.0 copy-done.3
  36.6 0.0 copy-done.4
  36.6 0.0 copy-done.5
  36.6 0.0 copy-done.6
  36.6 0.0 copy-done.7
  36.7 4.3 %focus.1 = bf16[2,256,1024]{2,1,0:T(8,128)(2,1)} custom-call(bf16[16,264,128]{2,1,0:T(8,128)(2,1)S(1)} %all-to-all-done.y_ref, bf16[512,512]{1,0:T(8,128)(2,1)S(1)} %copy-done, bf16[512,512]{1,0:T(8,128)(2,1)S(1)} %copy-done.1, bf16[256,256]{1,0:T(8,128)(2,1)S(1)} %copy-done.2, bf16[32,128]{1,0:T(8,128)(2,1)S(1)} %copy-done.6, s32[16,128]{1,0:T(8,128)S(1)} %bitcast.10, ...), custom_call_target="tpu_custom_call" | custom-call | tf_op jit(solution)/shard_map/focus/pallas_call | solution.py:376
Async XLA Ops:
  4.2 6.8 %copy-start.8 = (f32[16,8]{0,1:T(8,128)S(1)}, f32[16,8]{0,1:T(8,128)}, u32[]{:S(2)}) copy-start(f32[16,8]{0,1:T(8,128)} %param.15) | copy-start | bytes 1540
  4.2 32.4 %copy-start = (bf16[512,512]{1,0:T(8,128)(2,1)S(1)}, bf16[512,512]{1,0:T(8,128)(2,1)}, u32[]{:S(2)}) copy-start(bf16[512,512]{1,0:T(8,128)(2,1)} %constant.14.clone.mf_ref) | copy-start | bytes 1572868
  4.2 32.4 %copy-start.1 = (bf16[512,512]{1,0:T(8,128)(2,1)S(1)}, bf16[512,512]{1,0:T(8,128)(2,1)}, u32[]{:S(2)}) copy-start(bf16[512,512]{1,0:T(8,128)(2,1)} %constant.15.clone.mi_ref) | copy-start | bytes 1572868
  4.2 32.4 %copy-start.2 = (bf16[256,256]{1,0:T(8,128)(2,1)S(1)}, bf16[256,256]{1,0:T(8,128)(2,1)}, u32[]{:S(2)}) copy-start(bf16[256,256]{1,0:T(8,128)(2,1)} %constant.16.clone.eye_ref) | copy-start | bytes 393220
  4.2 32.4 %copy-start.3 = (f32[2,8,256]{2,1,0:T(8,128)S(1)}, f32[2,8,256]{2,1,0:T(8,128)}, u32[]{:S(2)}) copy-start(f32[2,8,256]{2,1,0:T(8,128)} %a_ref.1) | copy-start | bytes 49156
  4.2 32.4 %copy-start.4 = (s32[8,256]{1,0:T(8,128)S(1)}, s32[8,256]{1,0:T(8,128)}, u32[]{:S(2)}) copy-start(s32[8,256]{1,0:T(8,128)} %param.16) | copy-start | bytes 24580
  4.3 32.4 %copy-start.5 = (s32[8,256]{1,0:T(8,128)S(1)}, s32[8,256]{1,0:T(8,128)}, u32[]{:S(2)}) copy-start(s32[8,256]{1,0:T(8,128)} %param.17) | copy-start | bytes 24580
  4.3 32.4 %copy-start.6 = (bf16[32,128]{1,0:T(8,128)(2,1)S(1)}, bf16[32,128]{1,0:T(8,128)(2,1)}, u32[]{:S(2)}) copy-start(bf16[32,128]{1,0:T(8,128)(2,1)} %constant.17.clone.edge_ref) | copy-start | bytes 24580
  4.3 32.4 %copy-start.7 = (s32[8]{0:T(128)S(1)}, s32[8]{0:T(128)}, u32[]{:S(2)}) copy-start(s32[8]{0:T(128)} %c_ref.1) | copy-start | bytes 100
  4.3 32.3 %all-to-all-start = ((bf16[16,264,128]{2,1,0:T(8,128)(2,1)}), bf16[16,264,128]{2,1,0:T(8,128)(2,1)S(1)}, u32[]{:S(2)}, u32[]{:S(2)}) async-start(bf16[16,264,128]{2,1,0:T(8,128)(2,1)} %compress.1), calls=%async_computation | async-start | bytes 2162688 | tf_op jit(solution)/shard_map/all_to_all | solution.py:351

commit v3 on v2

--- a/solution.py
+++ b/solution.py
@@ -11,7 +11,6 @@
 
 R1 = 128
 RB = 128
-MAXSHIFT = 12
 LANES = 128
 SUB = 8
 SLOT = 32
@@ -64,9 +63,10 @@
     return jnp.concatenate([(re * tr - im * ti).astype(BF), (re * ti + im * tr).astype(BF)], axis)
 
 
-def compress_kernel(
-    dests, x_hbm, m_hbm, t_hbm, r_hbm, out_hbm, x_v, m_v, t_v, r_v, s_in, s_out, o_v, r_sq, in_sem, out_sem
-):
+def compress_kernel(dests, me_ref, x_hbm, m_hbm, t_hbm, r_hbm, *refs):
+    outs = refs[:dests]
+    x_v, m_v, t_v, r_v, s_in, s_out, o_v, r_sq, in_sem, out_sem = refs[dests:]
+    me = me_ref[0]
     pulses = x_hbm.shape[1]
     samples = x_hbm.shape[2]
     first = R1
@@ -153,35 +153,35 @@
 
     lane = lax.broadcasted_iota(jnp.int32, (SUB, LANES), 1)
     sends = []
-    for dest in range(dests):
+    for k in reversed(range(dests)):
+        dest = me ^ k
         for part in range(2):
             for block in range(blocks):
                 row = (part * blocks + block) * pulses
-                o_v[dest, row : row + pulses, :] = tile(dest, part, block).astype(BF)
+                o_v[k, row : row + pulses, :] = tile(dest, part, block).astype(BF)
         halo = jnp.zeros((SUB, LANES), F32)
+        take = (lane < 2 * SUB) & (dest + 1 < dests)
+        give = (lane >= LANES - 3) & (dest > 0)
         for part in range(2):
-            after = tile(dest + 1, part, 0) if dest + 1 < dests else None
-            before = tile(dest - 1, part, blocks - 1) if dest > 0 else None
+            after = tile(jnp.minimum(dest + 1, dests - 1), part, 0)
+            before = tile(jnp.maximum(dest - 1, 0), part, blocks - 1)
             for h in range(pulses // SUB):
-                piece = jnp.zeros((SUB, LANES), F32)
-                if after is not None:
-                    piece = jnp.where(lane < 2 * SUB, after[h * SUB : (h + 1) * SUB], piece)
-                if before is not None:
-                    piece = jnp.where(lane >= LANES - 3, before[h * SUB : (h + 1) * SUB], piece)
+                rows = slice(h * SUB, (h + 1) * SUB)
+                piece = jnp.where(take, after[rows], jnp.where(give, before[rows], 0.0))
                 slot = part * (pulses // SUB) + h
                 halo = halo + (pltpu.roll(piece, SLOT * slot, 1) if slot else piece)
         row = 2 * blocks * pulses
-        o_v[dest, row : row + SUB, :] = halo.astype(BF)
-        sends.append(pltpu.make_async_copy(o_v.at[dest], out_hbm.at[dest], out_sem.at[dest]))
+        o_v[k, row : row + SUB, :] = halo.astype(BF)
+        sends.append(pltpu.make_async_copy(o_v.at[k], outs[k], out_sem.at[k]))
         sends[-1].start()
     for send in sends:
         send.wait()
 
 
-def focus_kernel(
-    y_ref, mf_ref, mi_ref, eye_ref, edge_ref, s_ref, ph_ref, k_ref, c_ref, a_ref, out_ref, x_ref, ar_ref, d_ref
-):
-    sources = y_ref.shape[0]
+def focus_kernel(sources, *refs):
+    y_refs = refs[:sources]
+    mf_ref, mi_ref, eye_ref, edge_ref, s_ref, ph_ref, k_ref, c_ref, a_ref = refs[sources:-4]
+    out_ref, x_ref, ar_ref, d_ref = refs[-4:]
     bins = out_ref.shape[1]
     cells = out_ref.shape[2]
     blocks = cells // RB
@@ -207,7 +207,7 @@
         own.append(
             jnp.concatenate(
                 [
-                    y_ref[r, (o * blocks + b) * pulses : (o * blocks + b + 1) * pulses, :]
+                    y_refs[r][(o * blocks + b) * pulses : (o * blocks + b + 1) * pulses, :]
                     for r in range(sources)
                     for o in range(2)
                 ],
@@ -216,7 +216,7 @@
         )
     side = []
     for r in range(sources):
-        held = y_ref[r, 2 * blocks * pulses : 2 * blocks * pulses + SUB, :].astype(F32)
+        held = y_refs[r][2 * blocks * pulses : 2 * blocks * pulses + SUB, :].astype(F32)
         for o in range(2):
             for h in range(pulses // SUB):
                 slot = o * (pulses // SUB) + h
@@ -296,6 +296,16 @@
             out_ref[part, :, first * RB : (first + 2) * RB] = image[part * bins : (part + 1) * bins]
 
 
+def order_of(ranks):
+    far = [k for k in range(ranks) if k >= ranks // 2]
+    near = [k for k in reversed(range(ranks)) if 0 < k < ranks // 2]
+    order = []
+    while far or near:
+        order += far[:2] + near[:1]
+        far, near = far[2:], near[1:]
+    return order
+
+
 def vmem(count):
     return [pl.BlockSpec(memory_space=pltpu.VMEM)] * count
 
@@ -307,7 +317,6 @@
     cells = samples // ranks
     blocks = cells // RB
     bins = ranks * pulses
-    taps = kernels.shape[1]
     halves = bins // LANES
     q_rows = halves * blocks
     assert second == RB and pulses == 2 * SUB and bins % LANES == 0 and blocks % 2 == 0
@@ -324,9 +333,9 @@
     anywhere = pl.BlockSpec(memory_space=pl.ANY)
     sent = pl.pallas_call(
         functools.partial(compress_kernel, ranks),
-        out_shape=jax.ShapeDtypeStruct((ranks, rows, LANES), BF),
-        in_specs=[anywhere] * 4,
-        out_specs=anywhere,
+        out_shape=[jax.ShapeDtypeStruct((rows, LANES), BF)] * ranks,
+        in_specs=[pl.BlockSpec(memory_space=pltpu.SMEM)] + [anywhere] * 4,
+        out_specs=[anywhere] * ranks,
         scratch_shapes=[
             pltpu.VMEM((2, pulses, samples), BF),
             pltpu.VMEM((4, 2 * first, 2 * first), BF),
@@ -342,13 +351,16 @@
         compiler_params=pltpu.CompilerParams(vmem_limit_bytes=60 << 20),
         name="compress",
     )(
+        lax.axis_index("range").astype(jnp.int32).reshape(1),
         echoes,
         np.stack([as_bf(e1), as_bf(w2), as_bf(w3), as_bf(e4)]),
         np.concatenate([planes(t1), planes(t3)]),
         range_reference,
     )
 
-    arrived = lax.all_to_all(sent, "range", 0, 0)
+    arrived = [sent[0]] * ranks
+    for k in order_of(ranks):
+        arrived[k] = lax.ppermute(sent[k], "range", [(i, i ^ k) for i in range(ranks)])
 
     def spread(table):
         return table.reshape(blocks, halves, LANES).transpose(1, 0, 2).reshape(q_rows, LANES)
@@ -369,14 +381,18 @@
         / math.sqrt(bins)
     )
     behind = real_form(behind.reshape(bins, bins)).reshape(2 * bins, 2 * bins)
+    column = jnp.arange(2 * bins, dtype=jnp.int32)
+    wanted = column ^ (lax.axis_index("range").astype(jnp.int32) * (2 * pulses))
+    choose = (column[:, None] == wanted[None, :]).astype(BF)
+    ahead = jnp.dot(as_bf(ahead), choose, preferred_element_type=F32).astype(BF)
     edge = np.zeros((SLOT, LANES))
     edge[: 2 * SUB, : 2 * SUB] = np.eye(2 * SUB)
     edge[2 * SUB : 3 * SUB, LANES - SUB :] = np.eye(SUB)
     span = LEFT + RB + 3 * SUB
     return pl.pallas_call(
-        focus_kernel,
+        functools.partial(focus_kernel, ranks),
         out_shape=jax.ShapeDtypeStruct((2, bins, cells), BF),
-        in_specs=vmem(7)
+        in_specs=vmem(6 + ranks)
         + [
             pl.BlockSpec(memory_space=pltpu.SMEM),
             pl.BlockSpec(memory_space=pltpu.SMEM),
@@ -391,15 +407,15 @@
         compiler_params=pltpu.CompilerParams(vmem_limit_bytes=48 << 20),
         name="focus",
     )(
-        arrived,
-        as_bf(ahead),
+        *arrived,
+        ahead,
         as_bf(behind),
         as_bf(np.eye(2 * RB)),
         as_bf(edge),
         spread(shifts),
         spread(phase_index),
         kernels,
-        centroid,
+        lax.rem(centroid, jnp.int32(bins)),
         azimuth_reference,
     )
 
@@ -415,4 +431,5 @@
         P(None, "range", None),
     )
     out_specs = P("groups", None, "range")
+
     return jax.shard_map(local, mesh=mesh, in_specs=in_specs, out_specs=out_specs, check_vma=False)

time: 41.2 us -> 43.6 us (1.058)
  starting transfers between devices: 6.72 us -> 19.5 us
  waiting for transfers between devices: 25.5 us -> 14.5 us
  matrix products: 0 us -> 0.49 us
    all_to_all x1 -> x0, waiting for transfers between devices: 25.5 us -> none  [local(): arrived = lax.all_to_all(sent, 'range', 0, 0)]
    ppermute x0 -> x15, starting transfers between devices: none -> 19.5 us  [local(): lax.ppermute(sent[k], 'range', [(i, i ^ k) for i in range(ranks)])]
    ppermute x0 -> x15, waiting for transfers between devices: none -> 14.5 us  [local(): lax.ppermute(sent[k], 'range', [(i, i ^ k) for i in range(ranks)])]
    all_to_all x1 -> x0, starting transfers between devices: 6.72 us -> none  [local(): arrived = lax.all_to_all(sent, 'range', 0, 0)]
    dot_general x0 -> x1, matrix products: none -> 0.49 us  [local(): ahead = jnp.dot(as_bf(ahead), choose, preferred_element_type=F32).astype(BF)]
  transfers between devices with their start and end apart: 1 -> 15, of which waited for: 1 -> 6; matrix products, arithmetic and copies ran while one was open for 0% -> 1% of each run, Pallas kernels for 0% -> 0%
where the time goes in v3:
time: 43.6 us; the launch traced here: 43.5 us
  starting transfers between devices  19.5 us (45%)
  waiting for transfers between devices  14.5 us (33%)
  Pallas kernels  8.67 us (20%)
  matrix products  0.49 us (1%)
    ppermute x15, starting transfers between devices, local(): lax.ppermute(sent[k], 'range', [(i, i ^ k) for i in range(ranks)])  19.5 us
    ppermute x15, waiting for transfers between devices, local(): lax.ppermute(sent[k], 'range', [(i, i ^ k) for i in range(ranks)])  14.5 us
    pallas_call x1, Pallas kernels, local(): pl.pallas_call(functools.partial(focus_kernel, ranks), out_shape=jax.Shap...  4.34 us
    pallas_call x1, Pallas kernels, local(): pl.pallas_call(functools.partial(compress_kernel, ranks), out_shape=[jax....  4.33 us
  transfers between devices with their start and end apart: 15, of which 6 were waited for; matrix products, arithmetic and copies ran while one was open for 1% of the time, Pallas kernels for 0%

profile of v3, /device:TPU:9, one launch (start us, length us, event | category | flops | bytes accessed | tf_op | source)
XLA Modules:
  0.0 43.5 jit_solution(11362684261574169410)
XLA Ops:
  0.0 4.3 %compress.1 = (bf16[264,128]{1,0:T(8,128)(2,1)}, bf16[264,128]{1,0:T(8,128)(2,1)}, bf16[264,128]{1,0:T(8,128)(2,1)}, bf16[264,128]{1,0:T(8,128)(2,1)}, bf16[264,...) custom-call(s32[1]{0:T(128)} %bitcast.me_ref, ...), custom_call_target="tpu_custom_call" | custom-call | tf_op jit(solution)/shard_map/compress/pallas_call | solution.py:334
  4.3 0.7 %collective-permute-start = (bf16[264,128]{1,0:T(8,128)(2,1)}, bf16[264,128]{1,0:T(8,128)(2,1)S(1)}, u32[]{:S(2)}, u32[]{:S(2)}) collective-permute-start(bf16[264,128]{1,0:T(8,128)(2,1)} %get-tuple-element.22), channel_id=1, source_target_pairs={{0,1},{1,0},{2,3},{3,2},{4,5},{5,4},{6,7},{7,6},{8,9},{9,8},{10,11... | collective-permute-start | bytes 202760 | tf_op jit(solution)/shard_map/ppermute | solution.py:363
  5.1 1.2 %collective-permute-start.1 = (bf16[264,128]{1,0:T(8,128)(2,1)}, bf16[264,128]{1,0:T(8,128)(2,1)S(1)}, u32[]{:S(2)}, u32[]{:S(2)}) collective-permute-start(bf16[264,128]{1,0:T(8,128)(2,1)} %get-tuple-element.23), channel_id=1, source_target_pairs={{0,2},{1,3},{2,0},{3,1},{4,6},{5,7},{6,4},{7,5},{8,10},{9,11},{10,... | collective-permute-start | bytes 202760 | tf_op jit(solution)/shard_map/ppermute | solution.py:363
  6.3 0.5 %collective-permute-start.2 = (bf16[264,128]{1,0:T(8,128)(2,1)}, bf16[264,128]{1,0:T(8,128)(2,1)S(1)}, u32[]{:S(2)}, u32[]{:S(2)}) collective-permute-start(bf16[264,128]{1,0:T(8,128)(2,1)} %get-tuple-element.24), channel_id=1, source_target_pairs={{0,3},{1,2},{2,1},{3,0},{4,7},{5,6},{6,5},{7,4},{8,11},{9,10},{10,... | collective-permute-start | bytes 202760 | tf_op jit(solution)/shard_map/ppermute | solution.py:363
  6.8 0.0 collective-permute-start.3
  6.8 1.8 %collective-permute-start.4 = (bf16[264,128]{1,0:T(8,128)(2,1)}, bf16[264,128]{1,0:T(8,128)(2,1)S(1)}, u32[]{:S(2)}, u32[]{:S(2)}) collective-permute-start(bf16[264,128]{1,0:T(8,128)(2,1)} %get-tuple-element.26), channel_id=1, source_target_pairs={{0,5},{1,4},{2,7},{3,6},{4,1},{5,0},{6,3},{7,2},{8,13},{9,12},{10,... | collective-permute-start | bytes 202760 | tf_op jit(solution)/shard_map/ppermute | solution.py:363
  8.6 0.0 collective-permute-done.refs_1_
  8.6 1.1 %collective-permute-start.5 = (bf16[264,128]{1,0:T(8,128)(2,1)}, bf16[264,128]{1,0:T(8,128)(2,1)S(1)}, u32[]{:S(2)}, u32[]{:S(2)}) collective-permute-start(bf16[264,128]{1,0:T(8,128)(2,1)} %get-tuple-element.27), channel_id=1, source_target_pairs={{0,6},{1,7},{2,4},{3,5},{4,2},{5,3},{6,0},{7,1},{8,14},{9,15},{10,... | collective-permute-start | bytes 202760 | tf_op jit(solution)/shard_map/ppermute | solution.py:363
  9.7 0.0 collective-permute-done.1.refs_2_
  9.7 1.7 %collective-permute-start.6 = (bf16[264,128]{1,0:T(8,128)(2,1)}, bf16[264,128]{1,0:T(8,128)(2,1)S(1)}, u32[]{:S(2)}, u32[]{:S(2)}) collective-permute-start(bf16[264,128]{1,0:T(8,128)(2,1)} %get-tuple-element.28), channel_id=1, source_target_pairs={{0,7},{1,6},{2,5},{3,4},{4,3},{5,2},{6,1},{7,0},{8,15},{9,14},{10,... | collective-permute-start | bytes 202760 | tf_op jit(solution)/shard_map/ppermute | solution.py:363
  11.4 0.0 collective-permute-done.2.refs_3_
  11.4 2.3 %collective-permute-start.7 = (bf16[264,128]{1,0:T(8,128)(2,1)}, bf16[264,128]{1,0:T(8,128)(2,1)S(1)}, u32[]{:S(2)}, u32[]{:S(2)}) collective-permute-start(bf16[264,128]{1,0:T(8,128)(2,1)} %get-tuple-element.29), channel_id=1, source_target_pairs={{0,8},{1,9},{2,10},{3,11},{4,12},{5,13},{6,14},{7,15},{8,0},{9,1},... | collective-permute-start | bytes 202760 | tf_op jit(solution)/shard_map/ppermute | solution.py:363
  13.7 0.0 collective-permute-done.3.refs_4_
  13.7 0.6 %collective-permute-start.8 = (bf16[264,128]{1,0:T(8,128)(2,1)}, bf16[264,128]{1,0:T(8,128)(2,1)S(1)}, u32[]{:S(2)}, u32[]{:S(2)}) collective-permute-start(bf16[264,128]{1,0:T(8,128)(2,1)} %get-tuple-element.30), channel_id=1, source_target_pairs={{0,9},{1,8},{2,11},{3,10},{4,13},{5,12},{6,15},{7,14},{8,1},{9,0},... | collective-permute-start | bytes 202760 | tf_op jit(solution)/shard_map/ppermute | solution.py:363
  14.4 0.0 collective-permute-done.4.refs_5_
  14.4 0.0 copy-start.9
  14.4 0.0 copy-start.8
  14.4 0.0 copy-start
  14.4 0.0 copy-start.1
  14.4 2.9 %collective-permute-start.9 = (bf16[264,128]{1,0:T(8,128)(2,1)}, bf16[264,128]{1,0:T(8,128)(2,1)S(1)}, u32[]{:S(2)}, u32[]{:S(2)}) collective-permute-start(bf16[264,128]{1,0:T(8,128)(2,1)} %get-tuple-element.31), channel_id=1, source_target_pairs={{0,10},{1,11},{2,8},{3,9},{4,14},{5,15},{6,12},{7,13},{8,2},{9,3},... | collective-permute-start | bytes 202760 | tf_op jit(solution)/shard_map/ppermute | solution.py:363
  17.3 0.0 copy-done.14
  17.3 0.0 copy-start.5
  17.3 0.0 copy-start.6
  17.3 0.5 %fusion.refs_16_ = bf16[512,512]{1,0:T(8,128)(2,1)S(1)} fusion(bf16[512,512]{1,0:T(8,128)(2,1)S(1)} %copy-done.14, s32[512]{0:T(512)S(1)} %iota_xor_fusion), kind=kOutput, calls=%fused_computation.1 | convolution fusion | flops 268959744 | bytes 1050624 | tf_op jit(solution)/shard_map/dot_general | solution.py:387
  17.8 0.0 copy-start.3
  17.8 0.0 collective-permute-done.5.refs_6_
  17.8 0.0 copy-done.12
  17.8 0.5 %collective-permute-start.10 = (bf16[264,128]{1,0:T(8,128)(2,1)S(1)}, bf16[264,128]{1,0:T(8,128)(2,1)S(1)}, u32[]{:S(2)}, u32[]{:S(2)}) collective-permute-start(bf16[264,128]{1,0:T(8,128)(2,1)S(1)} %copy-done.12), channel_id=1, source_target_pairs={{0,11},{1,10},{2,9},{3,8},{4,15},{5,14},{6,13},{7,12},{8,3},{9,2},... | collective-permute-start | bytes 202760 | tf_op jit(solution)/shard_map/ppermute | solution.py:363
  18.4 0.0 collective-permute-done.6.refs_7_
  18.4 0.0 copy-done.11
  18.4 2.4 %collective-permute-start.11 = (bf16[264,128]{1,0:T(8,128)(2,1)S(1)}, bf16[264,128]{1,0:T(8,128)(2,1)S(1)}, u32[]{:S(2)}, u32[]{:S(2)}) collective-permute-start(bf16[264,128]{1,0:T(8,128)(2,1)S(1)} %copy-done.11), channel_id=1, source_target_pairs={{0,12},{1,13},{2,14},{3,15},{4,8},{5,9},{6,10},{7,11},{8,4},{9,5},... | collective-permute-start | bytes 202760 | tf_op jit(solution)/shard_map/ppermute | solution.py:363
  20.8 0.0 collective-permute-done.7.refs_8_
  20.8 0.0 copy-done.10
  20.8 0.0 collective-permute-start.12
  20.8 3.3 %collective-permute-done.8.refs_9_ = bf16[264,128]{1,0:T(8,128)(2,1)S(1)} collective-permute-done((bf16[264,128]{1,0:T(8,128)(2,1)}, bf16[264,128]{1,0:T(8,128)(2,1)S(1)}, u32[]{:S(2)}, u32[]{:S(2)}) %collective-permute-start.8) | collective-permute-done | bytes 67616 | tf_op jit(solution)/shard_map/ppermute | solution.py:363
  24.1 1.2 %collective-permute-start.13 = (bf16[264,128]{1,0:T(8,128)(2,1)S(1)}, bf16[264,128]{1,0:T(8,128)(2,1)S(1)}, u32[]{:S(2)}, u32[]{:S(2)}) collective-permute-start(bf16[264,128]{1,0:T(8,128)(2,1)S(1)} %copy-done.9), channel_id=1, source_target_pairs={{0,14},{1,15},{2,12},{3,13},{4,10},{5,11},{6,8},{7,9},{8,6},{9,7},... | collective-permute-start | bytes 202760 | tf_op jit(solution)/shard_map/ppermute | solution.py:363
  25.3 1.0 %collective-permute-done.9.refs_10_ = bf16[264,128]{1,0:T(8,128)(2,1)S(1)} collective-permute-done((bf16[264,128]{1,0:T(8,128)(2,1)}, bf16[264,128]{1,0:T(8,128)(2,1)S(1)}, u32[]{:S(2)}, u32[]{:S(2)}) %collective-permute-start.9) | collective-permute-done | bytes 67616 | tf_op jit(solution)/shard_map/ppermute | solution.py:363
  26.3 0.0 copy-done.8
  26.3 2.6 %collective-permute-start.14 = (bf16[264,128]{1,0:T(8,128)(2,1)S(1)}, bf16[264,128]{1,0:T(8,128)(2,1)S(1)}, u32[]{:S(2)}, u32[]{:S(2)}) collective-permute-start(bf16[264,128]{1,0:T(8,128)(2,1)S(1)} %copy-done.8), channel_id=1, source_target_pairs={{0,15},{1,14},{2,13},{3,12},{4,11},{5,10},{6,9},{7,8},{8,7},{9,6},... | collective-permute-start | bytes 202760 | tf_op jit(solution)/shard_map/ppermute | solution.py:363
  28.9 0.0 copy-start.4
  28.9 0.1 copy.15.refs_22_
  28.9 0.0 collective-permute-done.10.refs_11_
  28.9 3.6 %collective-permute-done.11.refs_12_ = bf16[264,128]{1,0:T(8,128)(2,1)S(1)} collective-permute-done((bf16[264,128]{1,0:T(8,128)(2,1)S(1)}, bf16[264,128]{1,0:T(8,128)(2,1)S(1)}, u32[]{:S(2)}, u32[]{:S(2)}) %collective-permute-start.11) | collective-permute-done | bytes 67616 | tf_op jit(solution)/shard_map/ppermute | solution.py:363
  32.5 2.8 %collective-permute-done.12.refs_13_ = bf16[264,128]{1,0:T(8,128)(2,1)S(1)} collective-permute-done((bf16[264,128]{1,0:T(8,128)(2,1)S(1)}, bf16[264,128]{1,0:T(8,128)(2,1)S(1)}, u32[]{:S(2)}, u32[]{:S(2)}) %collective-permute-start.12) | collective-permute-done | bytes 67616 | tf_op jit(solution)/shard_map/ppermute | solution.py:363
  35.3 2.3 %collective-permute-done.13.refs_14_ = bf16[264,128]{1,0:T(8,128)(2,1)S(1)} collective-permute-done((bf16[264,128]{1,0:T(8,128)(2,1)S(1)}, bf16[264,128]{1,0:T(8,128)(2,1)S(1)}, u32[]{:S(2)}, u32[]{:S(2)}) %collective-permute-start.13) | collective-permute-done | bytes 67616 | tf_op jit(solution)/shard_map/ppermute | solution.py:363
  37.6 1.4 %collective-permute-done.14.refs_15_ = bf16[264,128]{1,0:T(8,128)(2,1)S(1)} collective-permute-done((bf16[264,128]{1,0:T(8,128)(2,1)S(1)}, bf16[264,128]{1,0:T(8,128)(2,1)S(1)}, u32[]{:S(2)}, u32[]{:S(2)}) %collective-permute-start.14) | collective-permute-done | bytes 67616 | tf_op jit(solution)/shard_map/ppermute | solution.py:363
  39.1 0.0 copy-done
  39.1 4.3 %focus.1 = bf16[2,256,1024]{2,1,0:T(8,128)(2,1)} custom-call(bf16[264,128]{1,0:T(8,128)(2,1)S(1)} %copy-done.2, bf16[264,128]{1,0:T(8,128)(2,1)S(1)} %collective-permute-done.refs_1_, bf16[264,128]{1,0:T(8,128)(2,1)S(1)} %collective-permute-done.1.refs_2_, bf16[264,128]{1,0:T(8,128)(2,1)S(1)} %collective-permute-done.2.refs_3_, ...), custom_call_target="tpu_custom_call" | custom-call | tf_op jit(solution)/shard_map/focus/pallas_call | solution.py:392
  (18 shorter events, 0.0 us)
Async XLA Ops:
  0.0 17.3 %copy-start.14 = (bf16[512,512]{1,0:T(8,128)(2,1)S(1)}, bf16[512,512]{1,0:T(8,128)(2,1)}, u32[]{:S(2)}) copy-start(bf16[512,512]{1,0:T(8,128)(2,1)} %constant.25.clone) | copy-start | bytes 1572868
  4.3 4.2 %collective-permute-start = (bf16[264,128]{1,0:T(8,128)(2,1)}, bf16[264,128]{1,0:T(8,128)(2,1)S(1)}, u32[]{:S(2)}, u32[]{:S(2)}) collective-permute-start(bf16[264,128]{1,0:T(8,128)(2,1)} %get-tuple-element.22), channel_id=1, source_target_pairs={{0,1},{1,0},{2,3},{3,2},{4,5},{5,4},{6,7},{7,6},{8,9},{9,8},{10,11... | collective-permute-start | bytes 202760 | tf_op jit(solution)/shard_map/ppermute | solution.py:363
  5.1 4.6 %collective-permute-start.1 = (bf16[264,128]{1,0:T(8,128)(2,1)}, bf16[264,128]{1,0:T(8,128)(2,1)S(1)}, u32[]{:S(2)}, u32[]{:S(2)}) collective-permute-start(bf16[264,128]{1,0:T(8,128)(2,1)} %get-tuple-element.23), channel_id=1, source_target_pairs={{0,2},{1,3},{2,0},{3,1},{4,6},{5,7},{6,4},{7,5},{8,10},{9,11},{10,... | collective-permute-start | bytes 202760 | tf_op jit(solution)/shard_map/ppermute | solution.py:363
  6.3 5.1 %collective-permute-start.2 = (bf16[264,128]{1,0:T(8,128)(2,1)}, bf16[264,128]{1,0:T(8,128)(2,1)S(1)}, u32[]{:S(2)}, u32[]{:S(2)}) collective-permute-start(bf16[264,128]{1,0:T(8,128)(2,1)} %get-tuple-element.24), channel_id=1, source_target_pairs={{0,3},{1,2},{2,1},{3,0},{4,7},{5,6},{6,5},{7,4},{8,11},{9,10},{10,... | collective-permute-start | bytes 202760 | tf_op jit(solution)/shard_map/ppermute | solution.py:363
  6.8 6.9 %collective-permute-start.3 = (bf16[264,128]{1,0:T(8,128)(2,1)}, bf16[264,128]{1,0:T(8,128)(2,1)S(1)}, u32[]{:S(2)}, u32[]{:S(2)}) collective-permute-start(bf16[264,128]{1,0:T(8,128)(2,1)} %get-tuple-element.25), channel_id=1, source_target_pairs={{0,4},{1,5},{2,6},{3,7},{4,0},{5,1},{6,2},{7,3},{8,12},{9,13},{10,... | collective-permute-start | bytes 202760 | tf_op jit(solution)/shard_map/ppermute | solution.py:363
  6.8 7.6 %collective-permute-start.4 = (bf16[264,128]{1,0:T(8,128)(2,1)}, bf16[264,128]{1,0:T(8,128)(2,1)S(1)}, u32[]{:S(2)}, u32[]{:S(2)}) collective-permute-start(bf16[264,128]{1,0:T(8,128)(2,1)} %get-tuple-element.26), channel_id=1, source_target_pairs={{0,5},{1,4},{2,7},{3,6},{4,1},{5,0},{6,3},{7,2},{8,13},{9,12},{10,... | collective-permute-start | bytes 202760 | tf_op jit(solution)/shard_map/ppermute | solution.py:363
  8.6 9.2 %collective-permute-start.5 = (bf16[264,128]{1,0:T(8,128)(2,1)}, bf16[264,128]{1,0:T(8,128)(2,1)S(1)}, u32[]{:S(2)}, u32[]{:S(2)}) collective-permute-start(bf16[264,128]{1,0:T(8,128)(2,1)} %get-tuple-element.27), channel_id=1, source_target_pairs={{0,6},{1,7},{2,4},{3,5},{4,2},{5,3},{6,0},{7,1},{8,14},{9,15},{10,... | collective-permute-start | bytes 202760 | tf_op jit(solution)/shard_map/ppermute | solution.py:363
  9.7 8.6 %collective-permute-start.6 = (bf16[264,128]{1,0:T(8,128)(2,1)}, bf16[264,128]{1,0:T(8,128)(2,1)S(1)}, u32[]{:S(2)}, u32[]{:S(2)}) collective-permute-start(bf16[264,128]{1,0:T(8,128)(2,1)} %get-tuple-element.28), channel_id=1, source_target_pairs={{0,7},{1,6},{2,5},{3,4},{4,3},{5,2},{6,1},{7,0},{8,15},{9,14},{10,... | collective-permute-start | bytes 202760 | tf_op jit(solution)/shard_map/ppermute | solution.py:363
  11.4 9.4 %collective-permute-start.7 = (bf16[264,128]{1,0:T(8,128)(2,1)}, bf16[264,128]{1,0:T(8,128)(2,1)S(1)}, u32[]{:S(2)}, u32[]{:S(2)}) collective-permute-start(bf16[264,128]{1,0:T(8,128)(2,1)} %get-tuple-element.29), channel_id=1, source_target_pairs={{0,8},{1,9},{2,10},{3,11},{4,12},{5,13},{6,14},{7,15},{8,0},{9,1},... | collective-permute-start | bytes 202760 | tf_op jit(solution)/shard_map/ppermute | solution.py:363
  13.7 10.4 %collective-permute-start.8 = (bf16[264,128]{1,0:T(8,128)(2,1)}, bf16[264,128]{1,0:T(8,128)(2,1)S(1)}, u32[]{:S(2)}, u32[]{:S(2)}) collective-permute-start(bf16[264,128]{1,0:T(8,128)(2,1)} %get-tuple-element.30), channel_id=1, source_target_pairs={{0,9},{1,8},{2,11},{3,10},{4,13},{5,12},{6,15},{7,14},{8,1},{9,0},... | collective-permute-start | bytes 202760 | tf_op jit(solution)/shard_map/ppermute | solution.py:363
  14.4 3.5 %copy-start.12 = (bf16[264,128]{1,0:T(8,128)(2,1)S(1)}, bf16[264,128]{1,0:T(8,128)(2,1)}, u32[]{:S(2)}) copy-start(bf16[264,128]{1,0:T(8,128)(2,1)} %get-tuple-element.32) | copy-start | bytes 202756
  14.4 4.0 %copy-start.11 = (bf16[264,128]{1,0:T(8,128)(2,1)S(1)}, bf16[264,128]{1,0:T(8,128)(2,1)}, u32[]{:S(2)}) copy-start(bf16[264,128]{1,0:T(8,128)(2,1)} %get-tuple-element.33) | copy-start | bytes 202756
  14.4 6.4 %copy-start.10 = (bf16[264,128]{1,0:T(8,128)(2,1)S(1)}, bf16[264,128]{1,0:T(8,128)(2,1)}, u32[]{:S(2)}) copy-start(bf16[264,128]{1,0:T(8,128)(2,1)} %get-tuple-element.34) | copy-start | bytes 202756
  14.4 9.7 %copy-start.9 = (bf16[264,128]{1,0:T(8,128)(2,1)S(1)}, bf16[264,128]{1,0:T(8,128)(2,1)}, u32[]{:S(2)}) copy-start(bf16[264,128]{1,0:T(8,128)(2,1)} %get-tuple-element.35) | copy-start | bytes 202756
  14.4 11.9 %copy-start.8 = (bf16[264,128]{1,0:T(8,128)(2,1)S(1)}, bf16[264,128]{1,0:T(8,128)(2,1)}, u32[]{:S(2)}) copy-start(bf16[264,128]{1,0:T(8,128)(2,1)} %get-tuple-element.36) | copy-start | bytes 202756
  14.4 24.7 %copy-start = (bf16[512,512]{1,0:T(8,128)(2,1)S(1)}, bf16[512,512]{1,0:T(8,128)(2,1)}, u32[]{:S(2)}) copy-start(bf16[512,512]{1,0:T(8,128)(2,1)} %constant.26.clone.refs_17_) | copy-start | bytes 1572868
  14.4 24.7 %copy-start.1 = (bf16[256,256]{1,0:T(8,128)(2,1)S(1)}, bf16[256,256]{1,0:T(8,128)(2,1)}, u32[]{:S(2)}) copy-start(bf16[256,256]{1,0:T(8,128)(2,1)} %constant.27.clone.refs_18_) | copy-start | bytes 393220
  14.4 11.9 %collective-permute-start.9 = (bf16[264,128]{1,0:T(8,128)(2,1)}, bf16[264,128]{1,0:T(8,128)(2,1)S(1)}, u32[]{:S(2)}, u32[]{:S(2)}) collective-permute-start(bf16[264,128]{1,0:T(8,128)(2,1)} %get-tuple-element.31), channel_id=1, source_target_pairs={{0,10},{1,11},{2,8},{3,9},{4,14},{5,15},{6,12},{7,13},{8,2},{9,3},... | collective-permute-start | bytes 202760 | tf_op jit(solution)/shard_map/ppermute | solution.py:363
  17.3 11.6 %copy-start.13 = (s32[8]{0:T(128)S(1)}, s32[8]{0:T(128)}, u32[]{:S(2)}) copy-start(s32[8]{0:T(128)} %param.18) | copy-start | bytes 100
  17.3 11.6 %copy-start.7 = (f32[16,8]{0,1:T(8,128)S(1)}, f32[16,8]{0,1:T(8,128)}, u32[]{:S(2)}) copy-start(f32[16,8]{0,1:T(8,128)} %param.15) | copy-start | bytes 1540
  17.3 21.8 %copy-start.2 = (bf16[264,128]{1,0:T(8,128)(2,1)S(1)}, bf16[264,128]{1,0:T(8,128)(2,1)}, u32[]{:S(2)}) copy-start(bf16[264,128]{1,0:T(8,128)(2,1)} %get-tuple-element.21.refs_0_) | copy-start | bytes 202756
  17.3 21.8 %copy-start.5 = (s32[8,256]{1,0:T(8,128)S(1)}, s32[8,256]{1,0:T(8,128)}, u32[]{:S(2)}) copy-start(s32[8,256]{1,0:T(8,128)} %param.17) | copy-start | bytes 24580
  17.3 21.8 %copy-start.6 = (bf16[32,128]{1,0:T(8,128)(2,1)S(1)}, bf16[32,128]{1,0:T(8,128)(2,1)}, u32[]{:S(2)}) copy-start(bf16[32,128]{1,0:T(8,128)(2,1)} %constant.28.clone.refs_19_) | copy-start | bytes 24580
  17.8 21.3 %copy-start.3 = (f32[2,8,256]{2,1,0:T(8,128)S(1)}, f32[2,8,256]{2,1,0:T(8,128)}, u32[]{:S(2)}) copy-start(f32[2,8,256]{2,1,0:T(8,128)} %refs_24_.1) | copy-start | bytes 49156
  17.8 11.1 %collective-permute-start.10 = (bf16[264,128]{1,0:T(8,128)(2,1)S(1)}, bf16[264,128]{1,0:T(8,128)(2,1)S(1)}, u32[]{:S(2)}, u32[]{:S(2)}) collective-permute-start(bf16[264,128]{1,0:T(8,128)(2,1)S(1)} %copy-done.12), channel_id=1, source_target_pairs={{0,11},{1,10},{2,9},{3,8},{4,15},{5,14},{6,13},{7,12},{8,3},{9,2},... | collective-permute-start | bytes 202760 | tf_op jit(solution)/shard_map/ppermute | solution.py:363
  18.4 14.2 %collective-permute-start.11 = (bf16[264,128]{1,0:T(8,128)(2,1)S(1)}, bf16[264,128]{1,0:T(8,128)(2,1)S(1)}, u32[]{:S(2)}, u32[]{:S(2)}) collective-permute-start(bf16[264,128]{1,0:T(8,128)(2,1)S(1)} %copy-done.11), channel_id=1, source_target_pairs={{0,12},{1,13},{2,14},{3,15},{4,8},{5,9},{6,10},{7,11},{8,4},{9,5},... | collective-permute-start | bytes 202760 | tf_op jit(solution)/shard_map/ppermute | solution.py:363
  20.8 14.5 %collective-permute-start.12 = (bf16[264,128]{1,0:T(8,128)(2,1)S(1)}, bf16[264,128]{1,0:T(8,128)(2,1)S(1)}, u32[]{:S(2)}, u32[]{:S(2)}) collective-permute-start(bf16[264,128]{1,0:T(8,128)(2,1)S(1)} %copy-done.10), channel_id=1, source_target_pairs={{0,13},{1,12},{2,15},{3,14},{4,9},{5,8},{6,11},{7,10},{8,5},{9,4},... | collective-permute-start | bytes 202760 | tf_op jit(solution)/shard_map/ppermute | solution.py:363
  24.1 13.5 %collective-permute-start.13 = (bf16[264,128]{1,0:T(8,128)(2,1)S(1)}, bf16[264,128]{1,0:T(8,128)(2,1)S(1)}, u32[]{:S(2)}, u32[]{:S(2)}) collective-permute-start(bf16[264,128]{1,0:T(8,128)(2,1)S(1)} %copy-done.9), channel_id=1, source_target_pairs={{0,14},{1,15},{2,12},{3,13},{4,10},{5,11},{6,8},{7,9},{8,6},{9,7},... | collective-permute-start | bytes 202760 | tf_op jit(solution)/shard_map/ppermute | solution.py:363
  26.3 12.8 %collective-permute-start.14 = (bf16[264,128]{1,0:T(8,128)(2,1)S(1)}, bf16[264,128]{1,0:T(8,128)(2,1)S(1)}, u32[]{:S(2)}, u32[]{:S(2)}) collective-permute-start(bf16[264,128]{1,0:T(8,128)(2,1)S(1)} %copy-done.8), channel_id=1, source_target_pairs={{0,15},{1,14},{2,13},{3,12},{4,11},{5,10},{6,9},{7,8},{8,7},{9,6},... | collective-permute-start | bytes 202760 | tf_op jit(solution)/shard_map/ppermute | solution.py:363
  28.9 10.3 %copy-start.4 = (s32[8,256]{1,0:T(8,128)S(1)}, s32[8,256]{1,0:T(8,128)}, u32[]{:S(2)}) copy-start(s32[8,256]{1,0:T(8,128)} %param.16) | copy-start | bytes 24580

commit v4 on v3

--- a/solution.py
+++ b/solution.py
@@ -17,7 +17,7 @@
 LEFT = 8
 BF = jnp.bfloat16
 F32 = jnp.float32
-TAP = BF
+CHUNK = 4
 AT_ONCE = 16
 
 
@@ -65,7 +65,7 @@
 
 def compress_kernel(dests, me_ref, x_hbm, m_hbm, t_hbm, r_hbm, *refs):
     outs = refs[:dests]
-    x_v, m_v, t_v, r_v, s_in, s_out, o_v, r_sq, in_sem, out_sem = refs[dests:]
+    x_v, m_v, t_v, r_v, s_in, s_out, r_sq, in_sem = refs[dests:]
     me = me_ref[0]
     pulses = x_hbm.shape[1]
     samples = x_hbm.shape[2]
@@ -152,13 +152,12 @@
         return s_out[pl.ds((dest * 2 + part) * blocks + block, pulses, stride=gap_out), :]
 
     lane = lax.broadcasted_iota(jnp.int32, (SUB, LANES), 1)
-    sends = []
     for k in reversed(range(dests)):
         dest = me ^ k
         for part in range(2):
             for block in range(blocks):
                 row = (part * blocks + block) * pulses
-                o_v[k, row : row + pulses, :] = tile(dest, part, block).astype(BF)
+                outs[k][row : row + pulses, :] = tile(dest, part, block).astype(BF)
         halo = jnp.zeros((SUB, LANES), F32)
         take = (lane < 2 * SUB) & (dest + 1 < dests)
         give = (lane >= LANES - 3) & (dest > 0)
@@ -171,33 +170,41 @@
                 slot = part * (pulses // SUB) + h
                 halo = halo + (pltpu.roll(piece, SLOT * slot, 1) if slot else piece)
         row = 2 * blocks * pulses
-        o_v[k, row : row + SUB, :] = halo.astype(BF)
-        sends.append(pltpu.make_async_copy(o_v.at[k], outs[k], out_sem.at[k]))
-        sends[-1].start()
-    for send in sends:
-        send.wait()
+        outs[k][row : row + SUB, :] = halo.astype(BF)
+
+
+def params_kernel(ph_ref, k_ref, c_ref, a_ref, w_ref, t_ref):
+    phases, taps = k_ref.shape
+    blocks = a_ref.shape[1]
+    phase = ph_ref[...]
+    weights = [jnp.zeros(phase.shape, F32) for _ in range(taps)]
+    for q in range(phases):
+        hit = phase == q
+        for t in range(taps):
+            weights[t] = jnp.where(hit, k_ref[q, t], weights[t])
+    for t in range(taps):
+        w_ref[t] = weights[t]
+    for part in range(2):
+        for b in range(blocks):
+            line = pltpu.roll(a_ref[part, b : b + 1, :], c_ref[b], 1)
+            for h in range(phase.shape[0] // blocks):
+                q = h * blocks + b
+                t_ref[part, q : q + 1, :] = line[:, h * LANES : (h + 1) * LANES]
 
 
 def focus_kernel(sources, *refs):
     y_refs = refs[:sources]
-    mf_ref, mi_ref, eye_ref, edge_ref, s_ref, ph_ref, k_ref, c_ref, a_ref = refs[sources:-4]
-    out_ref, x_ref, ar_ref, d_ref = refs[-4:]
-    bins = out_ref.shape[1]
-    cells = out_ref.shape[2]
+    mf_ref, mi_ref, edge_ref, s_ref, w_ref, a_ref = refs[sources : sources + 6]
+    out_hbm, x_ref, d_ref, o_v, out_sem = refs[sources + 6 :]
+    bins = out_hbm.shape[1]
+    cells = out_hbm.shape[2]
     blocks = cells // RB
     pulses = bins // sources
-    phases, taps = k_ref.shape
+    taps = w_ref.shape[0]
     halves = bins // LANES
     q_rows = halves * blocks
     stride = 2 * q_rows + 1
     lead = taps // 2 - 1
-
-    for part in range(2):
-        for b in range(blocks):
-            line = pltpu.roll(a_ref[part, b : b + 1, :], c_ref[b], 1)
-            for h in range(halves):
-                q = h * blocks + b
-                ar_ref[part, q : q + 1, :] = line[:, h * LANES : (h + 1) * LANES]
 
     def put(jj, count, part, h, b, values):
         x_ref[pl.ds(jj * stride + part * q_rows + h * blocks + b, count, stride=stride), :] = values
@@ -207,35 +214,32 @@
         own.append(
             jnp.concatenate(
                 [
-                    y_refs[r][(o * blocks + b) * pulses : (o * blocks + b + 1) * pulses, :]
-                    for r in range(sources)
+                    y[(o * blocks + b) * pulses : (o * blocks + b + 1) * pulses, :]
+                    for y in y_refs
                     for o in range(2)
                 ],
                 0,
             )
         )
     side = []
-    for r in range(sources):
-        held = y_refs[r][2 * blocks * pulses : 2 * blocks * pulses + SUB, :].astype(F32)
+    for y in y_refs:
+        held = y[2 * blocks * pulses : 2 * blocks * pulses + SUB, :].astype(F32)
         for o in range(2):
             for h in range(pulses // SUB):
                 slot = o * (pulses // SUB) + h
                 side.append(pltpu.roll(held, LANES - SLOT * slot, 1) if slot else held)
     own.append(jnp.concatenate(side, 0).astype(BF))
     d_ref[...] = dot(mf_ref[...], jnp.concatenate(own, 1)).astype(BF)
-    for first in range(0, blocks, 2):
-        turned = dot_t(eye_ref[...], d_ref[:, first * RB : (first + 2) * RB])
-        for k in range(2):
-            b = first + k
-            for part in range(2):
-                for h in range(halves):
-                    col = part * bins + h * LANES
-                    here = turned[k * RB : (k + 1) * RB, col : col + LANES]
-                    put(LEFT, RB, part, h, b, here)
-                    if b > 0:
-                        put(LEFT + RB, 2 * SUB, part, h, b - 1, here[: 2 * SUB])
-                    if b + 1 < blocks:
-                        put(0, LEFT, part, h, b + 1, here[RB - LEFT :])
+    for b in range(blocks):
+        for part in range(2):
+            for h in range(halves):
+                row = part * bins + h * LANES
+                here = jnp.transpose(d_ref[row : row + LANES, b * RB : (b + 1) * RB]).astype(F32)
+                put(LEFT, RB, part, h, b, here)
+                if b > 0:
+                    put(LEFT + RB, 2 * SUB, part, h, b - 1, here[: 2 * SUB])
+                if b + 1 < blocks:
+                    put(0, LEFT, part, h, b + 1, here[RB - LEFT :])
     turned = dot_t(edge_ref[...], d_ref[:, cells:])
     for part in range(2):
         for h in range(halves):
@@ -243,57 +247,66 @@
             put(LEFT + RB, 2 * SUB, part, h, blocks - 1, turned[: 2 * SUB, col : col + LANES])
             put(0, LEFT, part, h, 0, turned[2 * SUB : 3 * SUB, col : col + LANES])
 
-    high = SUB * (4 // jnp.dtype(TAP).itemsize)
+    high = 2 * SUB
     for g in range(q_rows // high):
-        shift = s_ref[g * high : (g + 1) * high, :]
-        phase = ph_ref[g * high : (g + 1) * high, :]
-        weights = [jnp.zeros((high, LANES), F32) for _ in range(taps)]
-        for q in range(phases):
-            hit = phase == q
-            for t in range(taps):
-                weights[t] = jnp.where(hit, k_ref[q, t], weights[t])
-        weights = [w.astype(TAP) for w in weights]
-        if TAP == BF:
-            shift = shift.astype(jnp.int16)
+        shift = s_ref[g * high : (g + 1) * high, :].astype(jnp.int16)
+        weights = [w_ref[t, g * high : (g + 1) * high, :].astype(BF) for t in range(taps)]
+        ar, ai = [a_ref[part, g * high : (g + 1) * high, :].astype(BF) for part in range(2)]
         bits = [(shift & (1 << k)) != 0 for k in range(4)]
-        for part in range(2):
-            base = part * q_rows + g * high
-            seen = [{} for _ in range(5)]
-
-            def moved(level, i):
-                if i not in seen[level]:
-                    if level == 0:
-                        row = (i + LEFT - lead) * stride + base
-                        seen[0][i] = x_ref[row : row + high, :].astype(TAP)
-                    else:
-                        step = 1 << (level - 1)
-                        seen[level][i] = jnp.where(
-                            bits[level - 1], moved(level - 1, i + step), moved(level - 1, i)
-                        )
-                return seen[level][i]
-
-            for j in range(RB):
-                total = weights[0] * moved(4, j)
-                for t in range(1, taps):
-                    total = total + weights[t] * moved(4, j + t)
-                x_ref[j * stride + base : j * stride + base + high, :] = total.astype(F32)
-
+        seen = [[{} for _ in range(5)] for _ in range(2)]
+
+        def moved(part, level, i):
+            here = seen[part][level]
+            if i not in here:
+                if level == 0:
+                    row = (i + LEFT - lead) * stride + part * q_rows + g * high
+                    here[i] = x_ref[row : row + high, :].astype(BF)
+                else:
+                    step = 1 << (level - 1)
+                    here[i] = jnp.where(
+                        bits[level - 1], moved(part, level - 1, i + step), moved(part, level - 1, i)
+                    )
+            return here[i]
+
+        for first in range(0, RB, CHUNK):
+            sums = []
+            for part in range(2):
+                for j in range(first, first + CHUNK):
+                    total = weights[0] * moved(part, 4, j)
+                    for t in range(1, taps):
+                        total = total + weights[t] * moved(part, 4, j + t)
+                    sums.append(total)
+            for k in range(CHUNK):
+                re, im = sums[k], sums[CHUNK + k]
+                row = (first + k) * stride + g * high
+                x_ref[row : row + high, :] = (re * ar - im * ai).astype(F32)
+                row += q_rows
+                x_ref[row : row + high, :] = (re * ai + im * ar).astype(F32)
+
+    sends = []
     for first in range(0, blocks, 2):
         lines = []
         for b in range(first, first + 2):
-            re_parts, im_parts = [], []
-            for h in range(halves):
-                q = h * blocks + b
-                re = x_ref[pl.ds(q, RB, stride=stride), :]
-                im = x_ref[pl.ds(q_rows + q, RB, stride=stride), :]
-                ar = ar_ref[0, q : q + 1, :]
-                ai = ar_ref[1, q : q + 1, :]
-                re_parts.append((re * ar - im * ai).astype(BF))
-                im_parts.append((re * ai + im * ar).astype(BF))
-            lines.append(jnp.concatenate(re_parts + im_parts, 1))
+            lines.append(
+                jnp.concatenate(
+                    [
+                        x_ref[pl.ds(part * q_rows + h * blocks + b, RB, stride=stride), :].astype(BF)
+                        for part in range(2)
+                        for h in range(halves)
+                    ],
+                    1,
+                )
+            )
         image = dot_t(mi_ref[...], jnp.concatenate(lines, 0)).astype(BF)
         for part in range(2):
-            out_ref[part, :, first * RB : (first + 2) * RB] = image[part * bins : (part + 1) * bins]
+            o_v[part, :, first * RB : (first + 2) * RB] = image[part * bins : (part + 1) * bins]
+        cols = pl.ds(first * RB, 2 * RB)
+        sends.append(
+            pltpu.make_async_copy(o_v.at[:, :, cols], out_hbm.at[:, :, cols], out_sem.at[first // 2])
+        )
+        sends[-1].start()
+    for send in sends:
+        send.wait()
 
 
 def order_of(ranks):
@@ -317,6 +330,7 @@
     cells = samples // ranks
     blocks = cells // RB
     bins = ranks * pulses
+    taps = kernels.shape[1]
     halves = bins // LANES
     q_rows = halves * blocks
     assert second == RB and pulses == 2 * SUB and bins % LANES == 0 and blocks % 2 == 0
@@ -330,12 +344,11 @@
     e4 = real_form(unit(n1, n1, first, 1.0)).reshape(2, ranks, blocks, 2 * first)
     e4 = e4.transpose(1, 0, 2, 3).reshape(2 * first, 2 * first)
     rows = 2 * blocks * pulses + SUB
-    anywhere = pl.BlockSpec(memory_space=pl.ANY)
     sent = pl.pallas_call(
         functools.partial(compress_kernel, ranks),
         out_shape=[jax.ShapeDtypeStruct((rows, LANES), BF)] * ranks,
-        in_specs=[pl.BlockSpec(memory_space=pltpu.SMEM)] + [anywhere] * 4,
-        out_specs=[anywhere] * ranks,
+        in_specs=[pl.BlockSpec(memory_space=pltpu.SMEM)] + [pl.BlockSpec(memory_space=pltpu.HBM)] * 4,
+        out_specs=vmem(ranks),
         scratch_shapes=[
             pltpu.VMEM((2, pulses, samples), BF),
             pltpu.VMEM((4, 2 * first, 2 * first), BF),
@@ -343,12 +356,10 @@
             pltpu.VMEM((2, samples), F32),
             pltpu.VMEM((2 * first * (pulses + 1), second), F32),
             pltpu.VMEM((pulses * (2 * first + 1), second), F32),
-            pltpu.VMEM((ranks, rows, LANES), BF),
             pltpu.VMEM((2 * first + SUB, second), F32),
             pltpu.SemaphoreType.DMA((8,)),
-            pltpu.SemaphoreType.DMA((ranks,)),
         ],
-        compiler_params=pltpu.CompilerParams(vmem_limit_bytes=60 << 20),
+        compiler_params=pltpu.CompilerParams(vmem_limit_bytes=55375000),
         name="compress",
     )(
         lax.axis_index("range").astype(jnp.int32).reshape(1),
@@ -389,35 +400,32 @@
     edge[: 2 * SUB, : 2 * SUB] = np.eye(2 * SUB)
     edge[2 * SUB : 3 * SUB, LANES - SUB :] = np.eye(SUB)
     span = LEFT + RB + 3 * SUB
+    smem = pl.BlockSpec(memory_space=pltpu.SMEM)
+    weights, turned = pl.pallas_call(
+        params_kernel,
+        out_shape=[
+            jax.ShapeDtypeStruct((taps, q_rows, LANES), F32),
+            jax.ShapeDtypeStruct((2, q_rows, LANES), F32),
+        ],
+        in_specs=vmem(1) + [smem, smem] + vmem(1),
+        out_specs=vmem(2),
+        compiler_params=pltpu.CompilerParams(vmem_limit_bytes=4 << 20),
+        name="params",
+    )(spread(phase_index), kernels, lax.rem(centroid, jnp.int32(bins)), azimuth_reference)
     return pl.pallas_call(
         functools.partial(focus_kernel, ranks),
         out_shape=jax.ShapeDtypeStruct((2, bins, cells), BF),
-        in_specs=vmem(6 + ranks)
-        + [
-            pl.BlockSpec(memory_space=pltpu.SMEM),
-            pl.BlockSpec(memory_space=pltpu.SMEM),
-            pl.BlockSpec(memory_space=pltpu.VMEM),
-        ],
-        out_specs=pl.BlockSpec(memory_space=pltpu.VMEM),
+        in_specs=vmem(6 + ranks),
+        out_specs=pl.BlockSpec(memory_space=pl.ANY),
         scratch_shapes=[
             pltpu.VMEM((span * (2 * q_rows + 1), LANES), F32),
-            pltpu.VMEM((2, q_rows, LANES), F32),
             pltpu.VMEM((2 * bins, cells + LANES), BF),
+            pltpu.VMEM((2, bins, cells), BF),
+            pltpu.SemaphoreType.DMA((blocks // 2,)),
         ],
         compiler_params=pltpu.CompilerParams(vmem_limit_bytes=48 << 20),
         name="focus",
-    )(
-        *arrived,
-        ahead,
-        as_bf(behind),
-        as_bf(np.eye(2 * RB)),
-        as_bf(edge),
-        spread(shifts),
-        spread(phase_index),
-        kernels,
-        lax.rem(centroid, jnp.int32(bins)),
-        azimuth_reference,
-    )
+    )(*arrived, ahead, as_bf(behind), as_bf(edge), spread(shifts), weights, turned)
 
 
 def solution(mesh):

time: 43.6 us -> 41.6 us (0.954)
  waiting for transfers between devices: 14.5 us -> 12.5 us
  starting transfers between devices: 19.5 us -> 20.6 us
  Pallas kernels: 8.67 us -> 7.71 us
    ppermute x15, waiting for transfers between devices: 14.5 us -> 12.5 us  [local(): lax.ppermute(sent[k], 'range', [(i, i ^ k) for i in range(ranks)])]
    ppermute x15, starting transfers between devices: 19.5 us -> 20.6 us  [local(): lax.ppermute(sent[k], 'range', [(i, i ^ k) for i in range(ranks)])]
    pallas_call x1, Pallas kernels: 4.33 us -> 3.34 us  [local(): pl.pallas_call(functools.partial(compress_kernel, ranks), out_shape=[jax....]
    pallas_call x0 -> x1, Pallas kernels: none -> 0.77 us  [local(): pl.pallas_call(params_kernel, out_shape=[jax.ShapeDtypeStruct((taps, q_ro...]
    pallas_call x1, Pallas kernels: 4.34 us -> 3.6 us  [local(): pl.pallas_call(functools.partial(focus_kernel, ranks), out_shape=jax.Shap...]
  transfers between devices with their start and end apart: 15 -> 15, of which waited for: 6 -> 6; matrix products, arithmetic and copies ran while one was open for 1% -> 1% of each run, Pallas kernels for 0% -> 2%
where the time goes in v4:
time: 41.6 us; the launch traced here: 41.5 us
  starting transfers between devices  20.6 us (50%)
  waiting for transfers between devices  12.5 us (30%)
  Pallas kernels  7.71 us (19%)
  matrix products  0.49 us (1%)
    ppermute x15, starting transfers between devices, local(): lax.ppermute(sent[k], 'range', [(i, i ^ k) for i in range(ranks)])  20.6 us
    ppermute x15, waiting for transfers between devices, local(): lax.ppermute(sent[k], 'range', [(i, i ^ k) for i in range(ranks)])  12.5 us
    pallas_call x1, Pallas kernels, local(): pl.pallas_call(functools.partial(focus_kernel, ranks), out_shape=jax.Shap...  3.6 us
    pallas_call x1, Pallas kernels, local(): pl.pallas_call(functools.partial(compress_kernel, ranks), out_shape=[jax....  3.34 us
  transfers between devices with their start and end apart: 15, of which 6 were waited for; matrix products, arithmetic and copies ran while one was open for 1% of the time, Pallas kernels for 2%

profile of v4, /device:TPU:9, one launch (start us, length us, event | category | flops | bytes accessed | tf_op | source)
XLA Modules:
  0.0 41.5 jit_solution(18336915455367486133)
XLA Ops:
  0.0 3.3 %compress.1 = (bf16[264,128]{1,0:T(8,128)(2,1)S(1)}, bf16[264,128]{1,0:T(8,128)(2,1)S(1)}, bf16[264,128]{1,0:T(8,128)(2,1)S(1)}, bf16[264,128]{1,0:T(8,128)(2,1)...) custom-call(s32[1]{0:T(128)} %bitcast.me_ref, ...), custom_call_target="tpu_custom_call" | custom-call | tf_op jit(solution)/shard_map/compress/pallas_call | solution.py:347
  3.4 0.7 %collective-permute-start = (bf16[264,128]{1,0:T(8,128)(2,1)S(1)}, bf16[264,128]{1,0:T(8,128)(2,1)S(1)}, u32[]{:S(2)}, u32[]{:S(2)}) collective-permute-start(bf16[264,128]{1,0:T(8,128)(2,1)S(1)} %get-tuple-element.24), channel_id=1, source_target_pairs={{0,1},{1,0},{2,3},{3,2},{4,5},{5,4},{6,7},{7,6},{8,9},{9,8},{10,11... | collective-permute-start | bytes 202760 | tf_op jit(solution)/shard_map/ppermute | solution.py:374
  4.1 1.2 %collective-permute-start.1 = (bf16[264,128]{1,0:T(8,128)(2,1)S(1)}, bf16[264,128]{1,0:T(8,128)(2,1)S(1)}, u32[]{:S(2)}, u32[]{:S(2)}) collective-permute-start(bf16[264,128]{1,0:T(8,128)(2,1)S(1)} %get-tuple-element.25), channel_id=1, source_target_pairs={{0,2},{1,3},{2,0},{3,1},{4,6},{5,7},{6,4},{7,5},{8,10},{9,11},{10,... | collective-permute-start | bytes 202760 | tf_op jit(solution)/shard_map/ppermute | solution.py:374
  5.3 0.5 %collective-permute-start.2 = (bf16[264,128]{1,0:T(8,128)(2,1)S(1)}, bf16[264,128]{1,0:T(8,128)(2,1)S(1)}, u32[]{:S(2)}, u32[]{:S(2)}) collective-permute-start(bf16[264,128]{1,0:T(8,128)(2,1)S(1)} %get-tuple-element.26), channel_id=1, source_target_pairs={{0,3},{1,2},{2,1},{3,0},{4,7},{5,6},{6,5},{7,4},{8,11},{9,10},{10,... | collective-permute-start | bytes 202760 | tf_op jit(solution)/shard_map/ppermute | solution.py:374
  5.8 0.0 collective-permute-start.3
  5.8 1.8 %collective-permute-start.4 = (bf16[264,128]{1,0:T(8,128)(2,1)S(1)}, bf16[264,128]{1,0:T(8,128)(2,1)S(1)}, u32[]{:S(2)}, u32[]{:S(2)}) collective-permute-start(bf16[264,128]{1,0:T(8,128)(2,1)S(1)} %get-tuple-element.28), channel_id=1, source_target_pairs={{0,5},{1,4},{2,7},{3,6},{4,1},{5,0},{6,3},{7,2},{8,13},{9,12},{10,... | collective-permute-start | bytes 202760 | tf_op jit(solution)/shard_map/ppermute | solution.py:374
  7.6 0.0 collective-permute-done.refs_1_
  7.6 1.1 %collective-permute-start.5 = (bf16[264,128]{1,0:T(8,128)(2,1)S(1)}, bf16[264,128]{1,0:T(8,128)(2,1)S(1)}, u32[]{:S(2)}, u32[]{:S(2)}) collective-permute-start(bf16[264,128]{1,0:T(8,128)(2,1)S(1)} %get-tuple-element.29), channel_id=1, source_target_pairs={{0,6},{1,7},{2,4},{3,5},{4,2},{5,3},{6,0},{7,1},{8,14},{9,15},{10,... | collective-permute-start | bytes 202760 | tf_op jit(solution)/shard_map/ppermute | solution.py:374
  8.7 0.0 collective-permute-done.1.refs_2_
  8.7 1.5 %collective-permute-start.6 = (bf16[264,128]{1,0:T(8,128)(2,1)S(1)}, bf16[264,128]{1,0:T(8,128)(2,1)S(1)}, u32[]{:S(2)}, u32[]{:S(2)}) collective-permute-start(bf16[264,128]{1,0:T(8,128)(2,1)S(1)} %get-tuple-element.30), channel_id=1, source_target_pairs={{0,7},{1,6},{2,5},{3,4},{4,3},{5,2},{6,1},{7,0},{8,15},{9,14},{10,... | collective-permute-start | bytes 202760 | tf_op jit(solution)/shard_map/ppermute | solution.py:374
  10.2 0.0 collective-permute-done.2.refs_3_
  10.2 2.3 %collective-permute-start.7 = (bf16[264,128]{1,0:T(8,128)(2,1)S(1)}, bf16[264,128]{1,0:T(8,128)(2,1)S(1)}, u32[]{:S(2)}, u32[]{:S(2)}) collective-permute-start(bf16[264,128]{1,0:T(8,128)(2,1)S(1)} %get-tuple-element.31), channel_id=1, source_target_pairs={{0,8},{1,9},{2,10},{3,11},{4,12},{5,13},{6,14},{7,15},{8,0},{9,1},... | collective-permute-start | bytes 202760 | tf_op jit(solution)/shard_map/ppermute | solution.py:374
  12.5 0.0 collective-permute-done.3.refs_4_
  12.5 0.6 %collective-permute-start.8 = (bf16[264,128]{1,0:T(8,128)(2,1)S(1)}, bf16[264,128]{1,0:T(8,128)(2,1)S(1)}, u32[]{:S(2)}, u32[]{:S(2)}) collective-permute-start(bf16[264,128]{1,0:T(8,128)(2,1)S(1)} %get-tuple-element.32), channel_id=1, source_target_pairs={{0,9},{1,8},{2,11},{3,10},{4,13},{5,12},{6,15},{7,14},{8,1},{9,0},... | collective-permute-start | bytes 202760 | tf_op jit(solution)/shard_map/ppermute | solution.py:374
  13.2 0.0 collective-permute-done.4.refs_5_
  13.2 0.0 copy-start
  13.2 3.0 %collective-permute-start.9 = (bf16[264,128]{1,0:T(8,128)(2,1)S(1)}, bf16[264,128]{1,0:T(8,128)(2,1)S(1)}, u32[]{:S(2)}, u32[]{:S(2)}) collective-permute-start(bf16[264,128]{1,0:T(8,128)(2,1)S(1)} %get-tuple-element.33), channel_id=1, source_target_pairs={{0,10},{1,11},{2,8},{3,9},{4,14},{5,15},{6,12},{7,13},{8,2},{9,3},... | collective-permute-start | bytes 202760 | tf_op jit(solution)/shard_map/ppermute | solution.py:374
  16.2 0.0 copy-done.7
  16.2 0.0 copy-start.6
  16.2 0.0 copy-start.5
  16.2 0.5 %fusion.refs_16_ = bf16[512,512]{1,0:T(8,128)(2,1)S(1)} fusion(bf16[512,512]{1,0:T(8,128)(2,1)S(1)} %copy-done.7, s32[512]{0:T(512)S(1)} %iota_xor_fusion), kind=kOutput, calls=%fused_computation.1 | convolution fusion | flops 268959744 | bytes 1050624 | tf_op jit(solution)/shard_map/dot_general | solution.py:398
  16.7 0.0 copy-start.1
  16.7 0.0 collective-permute-done.5.refs_6_
  16.7 0.4 collective-permute-start.10
  17.1 0.0 collective-permute-done.6.refs_7_
  17.1 2.4 %collective-permute-start.11 = (bf16[264,128]{1,0:T(8,128)(2,1)S(1)}, bf16[264,128]{1,0:T(8,128)(2,1)S(1)}, u32[]{:S(2)}, u32[]{:S(2)}) collective-permute-start(bf16[264,128]{1,0:T(8,128)(2,1)S(1)} %get-tuple-element.35), channel_id=1, source_target_pairs={{0,12},{1,13},{2,14},{3,15},{4,8},{5,9},{6,10},{7,11},{8,4},{9,5},... | collective-permute-start | bytes 202760 | tf_op jit(solution)/shard_map/ppermute | solution.py:374
  19.4 0.0 collective-permute-done.7.refs_8_
  19.4 0.0 collective-permute-start.12
  19.4 1.6 %collective-permute-done.8.refs_9_ = bf16[264,128]{1,0:T(8,128)(2,1)S(1)} collective-permute-done((bf16[264,128]{1,0:T(8,128)(2,1)S(1)}, bf16[264,128]{1,0:T(8,128)(2,1)S(1)}, u32[]{:S(2)}, u32[]{:S(2)}) %collective-permute-start.8) | collective-permute-done | bytes 67616 | tf_op jit(solution)/shard_map/ppermute | solution.py:374
  21.0 2.2 %collective-permute-start.13 = (bf16[264,128]{1,0:T(8,128)(2,1)S(1)}, bf16[264,128]{1,0:T(8,128)(2,1)S(1)}, u32[]{:S(2)}, u32[]{:S(2)}) collective-permute-start(bf16[264,128]{1,0:T(8,128)(2,1)S(1)} %get-tuple-element.37), channel_id=1, source_target_pairs={{0,14},{1,15},{2,12},{3,13},{4,10},{5,11},{6,8},{7,9},{8,6},{9,7},... | collective-permute-start | bytes 202760 | tf_op jit(solution)/shard_map/ppermute | solution.py:374
  23.2 1.4 %collective-permute-done.9.refs_10_ = bf16[264,128]{1,0:T(8,128)(2,1)S(1)} collective-permute-done((bf16[264,128]{1,0:T(8,128)(2,1)S(1)}, bf16[264,128]{1,0:T(8,128)(2,1)S(1)}, u32[]{:S(2)}, u32[]{:S(2)}) %collective-permute-start.9) | collective-permute-done | bytes 67616 | tf_op jit(solution)/shard_map/ppermute | solution.py:374
  24.7 0.0 copy-start.4
  24.7 2.9 %collective-permute-start.14 = (bf16[264,128]{1,0:T(8,128)(2,1)S(1)}, bf16[264,128]{1,0:T(8,128)(2,1)S(1)}, u32[]{:S(2)}, u32[]{:S(2)}) collective-permute-start(bf16[264,128]{1,0:T(8,128)(2,1)S(1)} %get-tuple-element.38), channel_id=1, source_target_pairs={{0,15},{1,14},{2,13},{3,12},{4,11},{5,10},{6,9},{7,8},{8,7},{9,6},... | collective-permute-start | bytes 202760 | tf_op jit(solution)/shard_map/ppermute | solution.py:374
  27.5 0.0 copy-done.6
  27.6 0.0 copy-done.5
  27.6 0.1 copy.14.k_ref
  27.6 0.0 copy-done.1
  27.6 0.0 copy-done.4
  27.6 0.8 %params.1 = (f32[8,16,128]{2,1,0:T(8,128)S(1)}, f32[2,16,128]{2,1,0:T(8,128)S(1)}) custom-call(s32[16,128]{1,0:T(8,128)S(1)} %bitcast.15, f32[16,8]{1,0:T(8,128)S(1)} %copy.14.k_ref, s32[8]{0:T(128)S(1)} %compare_select_fusion.c_ref, f32[2,8,256]{2,1,0:T(8,128)S(1)} %copy-done.1), custom_call_target="tpu_custom_call" | custom-call | tf_op jit(solution)/shard_map/params/pallas_call | solution.py:404
  28.4 0.0 collective-permute-done.10.refs_11_
  28.4 2.6 %collective-permute-done.11.refs_12_ = bf16[264,128]{1,0:T(8,128)(2,1)S(1)} collective-permute-done((bf16[264,128]{1,0:T(8,128)(2,1)S(1)}, bf16[264,128]{1,0:T(8,128)(2,1)S(1)}, u32[]{:S(2)}, u32[]{:S(2)}) %collective-permute-start.11) | collective-permute-done | bytes 67616 | tf_op jit(solution)/shard_map/ppermute | solution.py:374
  31.0 3.1 %collective-permute-done.12.refs_13_ = bf16[264,128]{1,0:T(8,128)(2,1)S(1)} collective-permute-done((bf16[264,128]{1,0:T(8,128)(2,1)S(1)}, bf16[264,128]{1,0:T(8,128)(2,1)S(1)}, u32[]{:S(2)}, u32[]{:S(2)}) %collective-permute-start.12) | collective-permute-done | bytes 67616 | tf_op jit(solution)/shard_map/ppermute | solution.py:374
  34.1 2.3 %collective-permute-done.13.refs_14_ = bf16[264,128]{1,0:T(8,128)(2,1)S(1)} collective-permute-done((bf16[264,128]{1,0:T(8,128)(2,1)S(1)}, bf16[264,128]{1,0:T(8,128)(2,1)S(1)}, u32[]{:S(2)}, u32[]{:S(2)}) %collective-permute-start.13) | collective-permute-done | bytes 67616 | tf_op jit(solution)/shard_map/ppermute | solution.py:374
  36.4 1.4 %collective-permute-done.14.refs_15_ = bf16[264,128]{1,0:T(8,128)(2,1)S(1)} collective-permute-done((bf16[264,128]{1,0:T(8,128)(2,1)S(1)}, bf16[264,128]{1,0:T(8,128)(2,1)S(1)}, u32[]{:S(2)}, u32[]{:S(2)}) %collective-permute-start.14) | collective-permute-done | bytes 67616 | tf_op jit(solution)/shard_map/ppermute | solution.py:374
  37.9 0.0 copy-done
  37.9 0.0 copy-done.2
  37.9 0.0 copy-done.3
  37.9 3.6 %focus.1 = bf16[2,256,1024]{2,1,0:T(8,128)(2,1)} custom-call(bf16[264,128]{1,0:T(8,128)(2,1)S(1)} %get-tuple-element.23.refs_0_, bf16[264,128]{1,0:T(8,128)(2,1)S(1)} %collective-permute-done.refs_1_, bf16[264,128]{1,0:T(8,128)(2,1)S(1)} %collective-permute-done.1.refs_2_, bf16[264,128]{1,0:T(8,128)(2,1)S(1)} %collective-permute-done.2.refs_3_, ...), custom_call_target="tpu_custom_call" | custom-call | tf_op jit(solution)/shard_map/focus/pallas_call | solution.py:415
  (5 shorter events, 0.0 us)
Async XLA Ops:
  0.0 16.2 %copy-start.7 = (bf16[512,512]{1,0:T(8,128)(2,1)S(1)}, bf16[512,512]{1,0:T(8,128)(2,1)}, u32[]{:S(2)}) copy-start(bf16[512,512]{1,0:T(8,128)(2,1)} %constant.23.clone) | copy-start | bytes 1572868
  3.4 4.2 %collective-permute-start = (bf16[264,128]{1,0:T(8,128)(2,1)S(1)}, bf16[264,128]{1,0:T(8,128)(2,1)S(1)}, u32[]{:S(2)}, u32[]{:S(2)}) collective-permute-start(bf16[264,128]{1,0:T(8,128)(2,1)S(1)} %get-tuple-element.24), channel_id=1, source_target_pairs={{0,1},{1,0},{2,3},{3,2},{4,5},{5,4},{6,7},{7,6},{8,9},{9,8},{10,11... | collective-permute-start | bytes 202760 | tf_op jit(solution)/shard_map/ppermute | solution.py:374
  4.1 4.6 %collective-permute-start.1 = (bf16[264,128]{1,0:T(8,128)(2,1)S(1)}, bf16[264,128]{1,0:T(8,128)(2,1)S(1)}, u32[]{:S(2)}, u32[]{:S(2)}) collective-permute-start(bf16[264,128]{1,0:T(8,128)(2,1)S(1)} %get-tuple-element.25), channel_id=1, source_target_pairs={{0,2},{1,3},{2,0},{3,1},{4,6},{5,7},{6,4},{7,5},{8,10},{9,11},{10,... | collective-permute-start | bytes 202760 | tf_op jit(solution)/shard_map/ppermute | solution.py:374
  5.3 4.9 %collective-permute-start.2 = (bf16[264,128]{1,0:T(8,128)(2,1)S(1)}, bf16[264,128]{1,0:T(8,128)(2,1)S(1)}, u32[]{:S(2)}, u32[]{:S(2)}) collective-permute-start(bf16[264,128]{1,0:T(8,128)(2,1)S(1)} %get-tuple-element.26), channel_id=1, source_target_pairs={{0,3},{1,2},{2,1},{3,0},{4,7},{5,6},{6,5},{7,4},{8,11},{9,10},{10,... | collective-permute-start | bytes 202760 | tf_op jit(solution)/shard_map/ppermute | solution.py:374
  5.8 6.7 %collective-permute-start.3 = (bf16[264,128]{1,0:T(8,128)(2,1)S(1)}, bf16[264,128]{1,0:T(8,128)(2,1)S(1)}, u32[]{:S(2)}, u32[]{:S(2)}) collective-permute-start(bf16[264,128]{1,0:T(8,128)(2,1)S(1)} %get-tuple-element.27), channel_id=1, source_target_pairs={{0,4},{1,5},{2,6},{3,7},{4,0},{5,1},{6,2},{7,3},{8,12},{9,13},{10,... | collective-permute-start | bytes 202760 | tf_op jit(solution)/shard_map/ppermute | solution.py:374
  5.8 7.4 %collective-permute-start.4 = (bf16[264,128]{1,0:T(8,128)(2,1)S(1)}, bf16[264,128]{1,0:T(8,128)(2,1)S(1)}, u32[]{:S(2)}, u32[]{:S(2)}) collective-permute-start(bf16[264,128]{1,0:T(8,128)(2,1)S(1)} %get-tuple-element.28), channel_id=1, source_target_pairs={{0,5},{1,4},{2,7},{3,6},{4,1},{5,0},{6,3},{7,2},{8,13},{9,12},{10,... | collective-permute-start | bytes 202760 | tf_op jit(solution)/shard_map/ppermute | solution.py:374
  7.6 9.1 %collective-permute-start.5 = (bf16[264,128]{1,0:T(8,128)(2,1)S(1)}, bf16[264,128]{1,0:T(8,128)(2,1)S(1)}, u32[]{:S(2)}, u32[]{:S(2)}) collective-permute-start(bf16[264,128]{1,0:T(8,128)(2,1)S(1)} %get-tuple-element.29), channel_id=1, source_target_pairs={{0,6},{1,7},{2,4},{3,5},{4,2},{5,3},{6,0},{7,1},{8,14},{9,15},{10,... | collective-permute-start | bytes 202760 | tf_op jit(solution)/shard_map/ppermute | solution.py:374
  8.7 8.3 %collective-permute-start.6 = (bf16[264,128]{1,0:T(8,128)(2,1)S(1)}, bf16[264,128]{1,0:T(8,128)(2,1)S(1)}, u32[]{:S(2)}, u32[]{:S(2)}) collective-permute-start(bf16[264,128]{1,0:T(8,128)(2,1)S(1)} %get-tuple-element.30), channel_id=1, source_target_pairs={{0,7},{1,6},{2,5},{3,4},{4,3},{5,2},{6,1},{7,0},{8,15},{9,14},{10,... | collective-permute-start | bytes 202760 | tf_op jit(solution)/shard_map/ppermute | solution.py:374
  10.2 9.2 %collective-permute-start.7 = (bf16[264,128]{1,0:T(8,128)(2,1)S(1)}, bf16[264,128]{1,0:T(8,128)(2,1)S(1)}, u32[]{:S(2)}, u32[]{:S(2)}) collective-permute-start(bf16[264,128]{1,0:T(8,128)(2,1)S(1)} %get-tuple-element.31), channel_id=1, source_target_pairs={{0,8},{1,9},{2,10},{3,11},{4,12},{5,13},{6,14},{7,15},{8,0},{9,1},... | collective-permute-start | bytes 202760 | tf_op jit(solution)/shard_map/ppermute | solution.py:374
  12.5 8.5 %collective-permute-start.8 = (bf16[264,128]{1,0:T(8,128)(2,1)S(1)}, bf16[264,128]{1,0:T(8,128)(2,1)S(1)}, u32[]{:S(2)}, u32[]{:S(2)}) collective-permute-start(bf16[264,128]{1,0:T(8,128)(2,1)S(1)} %get-tuple-element.32), channel_id=1, source_target_pairs={{0,9},{1,8},{2,11},{3,10},{4,13},{5,12},{6,15},{7,14},{8,1},{9,0},... | collective-permute-start | bytes 202760 | tf_op jit(solution)/shard_map/ppermute | solution.py:374
  13.2 24.7 %copy-start = (bf16[512,512]{1,0:T(8,128)(2,1)S(1)}, bf16[512,512]{1,0:T(8,128)(2,1)}, u32[]{:S(2)}) copy-start(bf16[512,512]{1,0:T(8,128)(2,1)} %constant.24.clone.refs_17_) | copy-start | bytes 1572868
  13.2 11.5 %collective-permute-start.9 = (bf16[264,128]{1,0:T(8,128)(2,1)S(1)}, bf16[264,128]{1,0:T(8,128)(2,1)S(1)}, u32[]{:S(2)}, u32[]{:S(2)}) collective-permute-start(bf16[264,128]{1,0:T(8,128)(2,1)S(1)} %get-tuple-element.33), channel_id=1, source_target_pairs={{0,10},{1,11},{2,8},{3,9},{4,14},{5,15},{6,12},{7,13},{8,2},{9,3},... | collective-permute-start | bytes 202760 | tf_op jit(solution)/shard_map/ppermute | solution.py:374
  16.2 11.4 %copy-start.6 = (s32[8]{0:T(128)S(1)}, s32[8]{0:T(128)}, u32[]{:S(2)}) copy-start(s32[8]{0:T(128)} %param.17) | copy-start | bytes 100
  16.2 11.4 %copy-start.5 = (f32[16,8]{0,1:T(8,128)S(1)}, f32[16,8]{0,1:T(8,128)}, u32[]{:S(2)}) copy-start(f32[16,8]{0,1:T(8,128)} %param.14) | copy-start | bytes 1540
  16.7 11.0 %copy-start.1 = (f32[2,8,256]{2,1,0:T(8,128)S(1)}, f32[2,8,256]{2,1,0:T(8,128)}, u32[]{:S(2)}) copy-start(f32[2,8,256]{2,1,0:T(8,128)} %a_ref.1) | copy-start | bytes 49156
  16.7 11.7 %collective-permute-start.10 = (bf16[264,128]{1,0:T(8,128)(2,1)S(1)}, bf16[264,128]{1,0:T(8,128)(2,1)S(1)}, u32[]{:S(2)}, u32[]{:S(2)}) collective-permute-start(bf16[264,128]{1,0:T(8,128)(2,1)S(1)} %get-tuple-element.34), channel_id=1, source_target_pairs={{0,11},{1,10},{2,9},{3,8},{4,15},{5,14},{6,13},{7,12},{8,3},{9,2},... | collective-permute-start | bytes 202760 | tf_op jit(solution)/shard_map/ppermute | solution.py:374
  17.1 13.9 %collective-permute-start.11 = (bf16[264,128]{1,0:T(8,128)(2,1)S(1)}, bf16[264,128]{1,0:T(8,128)(2,1)S(1)}, u32[]{:S(2)}, u32[]{:S(2)}) collective-permute-start(bf16[264,128]{1,0:T(8,128)(2,1)S(1)} %get-tuple-element.35), channel_id=1, source_target_pairs={{0,12},{1,13},{2,14},{3,15},{4,8},{5,9},{6,10},{7,11},{8,4},{9,5},... | collective-permute-start | bytes 202760 | tf_op jit(solution)/shard_map/ppermute | solution.py:374
  19.4 14.7 %collective-permute-start.12 = (bf16[264,128]{1,0:T(8,128)(2,1)S(1)}, bf16[264,128]{1,0:T(8,128)(2,1)S(1)}, u32[]{:S(2)}, u32[]{:S(2)}) collective-permute-start(bf16[264,128]{1,0:T(8,128)(2,1)S(1)} %get-tuple-element.36), channel_id=1, source_target_pairs={{0,13},{1,12},{2,15},{3,14},{4,9},{5,8},{6,11},{7,10},{8,5},{9,4},... | collective-permute-start | bytes 202760 | tf_op jit(solution)/shard_map/ppermute | solution.py:374
  21.0 15.4 %collective-permute-start.13 = (bf16[264,128]{1,0:T(8,128)(2,1)S(1)}, bf16[264,128]{1,0:T(8,128)(2,1)S(1)}, u32[]{:S(2)}, u32[]{:S(2)}) collective-permute-start(bf16[264,128]{1,0:T(8,128)(2,1)S(1)} %get-tuple-element.37), channel_id=1, source_target_pairs={{0,14},{1,15},{2,12},{3,13},{4,10},{5,11},{6,8},{7,9},{8,6},{9,7},... | collective-permute-start | bytes 202760 | tf_op jit(solution)/shard_map/ppermute | solution.py:374
  24.7 3.0 %copy-start.4 = (s32[8,256]{1,0:T(8,128)S(1)}, s32[8,256]{1,0:T(8,128)}, u32[]{:S(2)}) copy-start(s32[8,256]{1,0:T(8,128)} %param.16) | copy-start | bytes 24580
  24.7 13.2 %collective-permute-start.14 = (bf16[264,128]{1,0:T(8,128)(2,1)S(1)}, bf16[264,128]{1,0:T(8,128)(2,1)S(1)}, u32[]{:S(2)}, u32[]{:S(2)}) collective-permute-start(bf16[264,128]{1,0:T(8,128)(2,1)S(1)} %get-tuple-element.38), channel_id=1, source_target_pairs={{0,15},{1,14},{2,13},{3,12},{4,11},{5,10},{6,9},{7,8},{8,7},{9,6},... | collective-permute-start | bytes 202760 | tf_op jit(solution)/shard_map/ppermute | solution.py:374
  27.6 10.2 %copy-start.2 = (s32[8,256]{1,0:T(8,128)S(1)}, s32[8,256]{1,0:T(8,128)}, u32[]{:S(2)}) copy-start(s32[8,256]{1,0:T(8,128)} %param.15) | copy-start | bytes 24580
  27.6 10.2 %copy-start.3 = (bf16[32,128]{1,0:T(8,128)(2,1)S(1)}, bf16[32,128]{1,0:T(8,128)(2,1)}, u32[]{:S(2)}) copy-start(bf16[32,128]{1,0:T(8,128)(2,1)} %constant.25.clone.refs_18_) | copy-start | bytes 24580

commit v5 on v4

--- a/solution.py
+++ b/solution.py
@@ -57,9 +57,12 @@
     return lax.dot_general(left, right, (((1,), (1,)), ((), ())), preferred_element_type=F32)
 
 
-def turned_by(values, table, axis):
+def turned_by(values, table, axis, back=False):
     re, im = values
     tr, ti = table
+    if back:
+        real = (re * tr + im * ti).astype(BF)
+        return jnp.concatenate([real, (im * tr - re * ti).astype(BF)], axis)
     return jnp.concatenate([(re * tr - im * ti).astype(BF), (re * ti + im * tr).astype(BF)], axis)
 
 
@@ -77,7 +80,7 @@
     gap_out = 2 * first + 1
     parts = 2
 
-    copies = [pltpu.make_async_copy(r_hbm, r_v, in_sem.at[0])]
+    copies = []
     span = samples // parts
     for part in range(2):
         for k in range(parts):
@@ -89,29 +92,31 @@
             )
     copies.append(pltpu.make_async_copy(m_hbm, m_v, in_sem.at[len(copies)]))
     copies.append(pltpu.make_async_copy(t_hbm, t_v, in_sem.at[len(copies)]))
+    copies.append(pltpu.make_async_copy(r_hbm, r_v, in_sem.at[len(copies)]))
     for copy in copies:
         copy.start()
 
-    copies[0].wait()
-    for k2 in range(second):
-        r_sq[pl.ds(k2, 2, stride=second + 1), :] = r_v[:, k2 * first : (k2 + 1) * first]
-    slots = []
-    for part in range(2):
-        row = part * (second + 1)
-        slots.append(jnp.transpose(r_sq[row : row + second, :]) * (1.0 / math.sqrt(second)))
-    for part in range(2):
-        r_sq[part * first : (part + 1) * first, :] = slots[part]
-
     for part in range(2):
         for k in range(parts):
-            copies[1 + part * parts + k].wait()
+            copies[part * parts + k].wait()
             for n1 in range(k * first // parts, (k + 1) * first // parts):
                 row = (part * first + n1) * gap_in
                 s_in[row : row + pulses, :] = x_v[part, :, n1 * second : (n1 + 1) * second].astype(
                     F32
                 )
+    copies[-3].wait()
     copies[-2].wait()
+
     copies[-1].wait()
+    for k2 in range(second):
+        r_sq[pl.ds(k2, 2, stride=second + 1), :] = r_v[:, k2 * first : (k2 + 1) * first]
+    slots = []
+    for part in range(2):
+        row = part * (second + 1)
+        slots.append(jnp.transpose(r_sq[row : row + second, :]) * (1.0 / math.sqrt(second)))
+    for part in range(2):
+        r_sq[part * first : (part + 1) * first, :] = slots[part]
+
 
     for group in range(0, pulses, AT_ONCE):
         lines = []
@@ -138,11 +143,11 @@
             here = spec[k * first : (k + 1) * first]
             rows.append(turned_by((here[:, :second], here[:, second:]), table, 1))
         back = dot(jnp.concatenate(rows, 0), m_v[2])
-        table = (t_v[2], t_v[3])
+        table = (t_v[0], t_v[1])
         lines = []
         for k in range(AT_ONCE):
             here = back[k * first : (k + 1) * first]
-            lines.append(turned_by((here[:, :second], here[:, second:]), table, 0))
+            lines.append(turned_by((here[:, :second], here[:, second:]), table, 0, True))
         done = dot(m_v[3], jnp.concatenate(lines, 1))
         for k in range(AT_ONCE):
             row = (group + k) * gap_out
@@ -340,7 +345,6 @@
     t1 = turn(n1, n2, samples, -1.0) / math.sqrt(first)
     w2 = real_form(unit(n2, n2, second, -1.0)).transpose(2, 3, 0, 1).reshape(2 * second, 2 * second)
     w3 = real_form(unit(n2, n2, second, 1.0)).transpose(2, 3, 0, 1).reshape(2 * second, 2 * second)
-    t3 = turn(n1, n2, samples, 1.0) / math.sqrt(second)
     e4 = real_form(unit(n1, n1, first, 1.0)).reshape(2, ranks, blocks, 2 * first)
     e4 = e4.transpose(1, 0, 2, 3).reshape(2 * first, 2 * first)
     rows = 2 * blocks * pulses + SUB
@@ -352,7 +356,7 @@
         scratch_shapes=[
             pltpu.VMEM((2, pulses, samples), BF),
             pltpu.VMEM((4, 2 * first, 2 * first), BF),
-            pltpu.VMEM((4, first, second), F32),
+            pltpu.VMEM((2, first, second), F32),
             pltpu.VMEM((2, samples), F32),
             pltpu.VMEM((2 * first * (pulses + 1), second), F32),
             pltpu.VMEM((pulses * (2 * first + 1), second), F32),
@@ -365,7 +369,7 @@
         lax.axis_index("range").astype(jnp.int32).reshape(1),
         echoes,
         np.stack([as_bf(e1), as_bf(w2), as_bf(w3), as_bf(e4)]),
-        np.concatenate([planes(t1), planes(t3)]),
+        planes(t1),
         range_reference,
     )
 

time: 41.6 us -> 41.6 us (level)
  no operation moved by 1% of the time
where the time goes in v5:
time: 41.6 us; the launch traced here: 41.5 us
  starting transfers between devices  20.6 us (50%)
  waiting for transfers between devices  12.5 us (30%)
  Pallas kernels  7.72 us (19%)
  matrix products  0.49 us (1%)
    ppermute x15, starting transfers between devices, local(): lax.ppermute(sent[k], 'range', [(i, i ^ k) for i in range(ranks)])  20.6 us
    ppermute x15, waiting for transfers between devices, local(): lax.ppermute(sent[k], 'range', [(i, i ^ k) for i in range(ranks)])  12.5 us
    pallas_call x1, Pallas kernels, local(): pl.pallas_call(functools.partial(focus_kernel, ranks), out_shape=jax.Shap...  3.6 us
    pallas_call x1, Pallas kernels, local(): pl.pallas_call(functools.partial(compress_kernel, ranks), out_shape=[jax....  3.34 us
  transfers between devices with their start and end apart: 15, of which 6 were waited for; matrix products, arithmetic and copies ran while one was open for 1% of the time, Pallas kernels for 2%

profile of v5, /device:TPU:9, one launch (start us, length us, event | category | flops | bytes accessed | tf_op | source)
XLA Modules:
  0.0 41.5 jit_solution(18132657970569713293)
XLA Ops:
  0.0 3.3 %compress.1 = (bf16[264,128]{1,0:T(8,128)(2,1)S(1)}, bf16[264,128]{1,0:T(8,128)(2,1)S(1)}, bf16[264,128]{1,0:T(8,128)(2,1)S(1)}, bf16[264,128]{1,0:T(8,128)(2,1)...) custom-call(s32[1]{0:T(128)} %bitcast.me_ref, ...), custom_call_target="tpu_custom_call" | custom-call | tf_op jit(solution)/shard_map/compress/pallas_call | solution.py:351
  3.4 0.7 %collective-permute-start = (bf16[264,128]{1,0:T(8,128)(2,1)S(1)}, bf16[264,128]{1,0:T(8,128)(2,1)S(1)}, u32[]{:S(2)}, u32[]{:S(2)}) collective-permute-start(bf16[264,128]{1,0:T(8,128)(2,1)S(1)} %get-tuple-element.24), channel_id=1, source_target_pairs={{0,1},{1,0},{2,3},{3,2},{4,5},{5,4},{6,7},{7,6},{8,9},{9,8},{10,11... | collective-permute-start | bytes 202760 | tf_op jit(solution)/shard_map/ppermute | solution.py:378
  4.1 1.2 %collective-permute-start.1 = (bf16[264,128]{1,0:T(8,128)(2,1)S(1)}, bf16[264,128]{1,0:T(8,128)(2,1)S(1)}, u32[]{:S(2)}, u32[]{:S(2)}) collective-permute-start(bf16[264,128]{1,0:T(8,128)(2,1)S(1)} %get-tuple-element.25), channel_id=1, source_target_pairs={{0,2},{1,3},{2,0},{3,1},{4,6},{5,7},{6,4},{7,5},{8,10},{9,11},{10,... | collective-permute-start | bytes 202760 | tf_op jit(solution)/shard_map/ppermute | solution.py:378
  5.3 0.5 %collective-permute-start.2 = (bf16[264,128]{1,0:T(8,128)(2,1)S(1)}, bf16[264,128]{1,0:T(8,128)(2,1)S(1)}, u32[]{:S(2)}, u32[]{:S(2)}) collective-permute-start(bf16[264,128]{1,0:T(8,128)(2,1)S(1)} %get-tuple-element.26), channel_id=1, source_target_pairs={{0,3},{1,2},{2,1},{3,0},{4,7},{5,6},{6,5},{7,4},{8,11},{9,10},{10,... | collective-permute-start | bytes 202760 | tf_op jit(solution)/shard_map/ppermute | solution.py:378
  5.8 0.0 collective-permute-start.3
  5.8 1.8 %collective-permute-start.4 = (bf16[264,128]{1,0:T(8,128)(2,1)S(1)}, bf16[264,128]{1,0:T(8,128)(2,1)S(1)}, u32[]{:S(2)}, u32[]{:S(2)}) collective-permute-start(bf16[264,128]{1,0:T(8,128)(2,1)S(1)} %get-tuple-element.28), channel_id=1, source_target_pairs={{0,5},{1,4},{2,7},{3,6},{4,1},{5,0},{6,3},{7,2},{8,13},{9,12},{10,... | collective-permute-start | bytes 202760 | tf_op jit(solution)/shard_map/ppermute | solution.py:378
  7.6 0.0 collective-permute-done.refs_1_
  7.6 1.1 %collective-permute-start.5 = (bf16[264,128]{1,0:T(8,128)(2,1)S(1)}, bf16[264,128]{1,0:T(8,128)(2,1)S(1)}, u32[]{:S(2)}, u32[]{:S(2)}) collective-permute-start(bf16[264,128]{1,0:T(8,128)(2,1)S(1)} %get-tuple-element.29), channel_id=1, source_target_pairs={{0,6},{1,7},{2,4},{3,5},{4,2},{5,3},{6,0},{7,1},{8,14},{9,15},{10,... | collective-permute-start | bytes 202760 | tf_op jit(solution)/shard_map/ppermute | solution.py:378
  8.7 0.0 collective-permute-done.1.refs_2_
  8.7 1.5 %collective-permute-start.6 = (bf16[264,128]{1,0:T(8,128)(2,1)S(1)}, bf16[264,128]{1,0:T(8,128)(2,1)S(1)}, u32[]{:S(2)}, u32[]{:S(2)}) collective-permute-start(bf16[264,128]{1,0:T(8,128)(2,1)S(1)} %get-tuple-element.30), channel_id=1, source_target_pairs={{0,7},{1,6},{2,5},{3,4},{4,3},{5,2},{6,1},{7,0},{8,15},{9,14},{10,... | collective-permute-start | bytes 202760 | tf_op jit(solution)/shard_map/ppermute | solution.py:378
  10.2 0.0 collective-permute-done.2.refs_3_
  10.2 2.3 %collective-permute-start.7 = (bf16[264,128]{1,0:T(8,128)(2,1)S(1)}, bf16[264,128]{1,0:T(8,128)(2,1)S(1)}, u32[]{:S(2)}, u32[]{:S(2)}) collective-permute-start(bf16[264,128]{1,0:T(8,128)(2,1)S(1)} %get-tuple-element.31), channel_id=1, source_target_pairs={{0,8},{1,9},{2,10},{3,11},{4,12},{5,13},{6,14},{7,15},{8,0},{9,1},... | collective-permute-start | bytes 202760 | tf_op jit(solution)/shard_map/ppermute | solution.py:378
  12.5 0.0 collective-permute-done.3.refs_4_
  12.5 0.6 %collective-permute-start.8 = (bf16[264,128]{1,0:T(8,128)(2,1)S(1)}, bf16[264,128]{1,0:T(8,128)(2,1)S(1)}, u32[]{:S(2)}, u32[]{:S(2)}) collective-permute-start(bf16[264,128]{1,0:T(8,128)(2,1)S(1)} %get-tuple-element.32), channel_id=1, source_target_pairs={{0,9},{1,8},{2,11},{3,10},{4,13},{5,12},{6,15},{7,14},{8,1},{9,0},... | collective-permute-start | bytes 202760 | tf_op jit(solution)/shard_map/ppermute | solution.py:378
  13.2 0.0 collective-permute-done.4.refs_5_
  13.2 0.0 copy-start
  13.2 3.0 %collective-permute-start.9 = (bf16[264,128]{1,0:T(8,128)(2,1)S(1)}, bf16[264,128]{1,0:T(8,128)(2,1)S(1)}, u32[]{:S(2)}, u32[]{:S(2)}) collective-permute-start(bf16[264,128]{1,0:T(8,128)(2,1)S(1)} %get-tuple-element.33), channel_id=1, source_target_pairs={{0,10},{1,11},{2,8},{3,9},{4,14},{5,15},{6,12},{7,13},{8,2},{9,3},... | collective-permute-start | bytes 202760 | tf_op jit(solution)/shard_map/ppermute | solution.py:378
  16.2 0.0 copy-done.7
  16.2 0.0 copy-start.6
  16.2 0.0 copy-start.5
  16.2 0.5 %fusion.refs_16_ = bf16[512,512]{1,0:T(8,128)(2,1)S(1)} fusion(bf16[512,512]{1,0:T(8,128)(2,1)S(1)} %copy-done.7, s32[512]{0:T(512)S(1)} %iota_xor_fusion), kind=kOutput, calls=%fused_computation.1 | convolution fusion | flops 268959744 | bytes 1050624 | tf_op jit(solution)/shard_map/dot_general | solution.py:402
  16.7 0.0 copy-start.1
  16.7 0.0 collective-permute-done.5.refs_6_
  16.7 0.4 collective-permute-start.10
  17.1 0.0 collective-permute-done.6.refs_7_
  17.1 2.3 %collective-permute-start.11 = (bf16[264,128]{1,0:T(8,128)(2,1)S(1)}, bf16[264,128]{1,0:T(8,128)(2,1)S(1)}, u32[]{:S(2)}, u32[]{:S(2)}) collective-permute-start(bf16[264,128]{1,0:T(8,128)(2,1)S(1)} %get-tuple-element.35), channel_id=1, source_target_pairs={{0,12},{1,13},{2,14},{3,15},{4,8},{5,9},{6,10},{7,11},{8,4},{9,5},... | collective-permute-start | bytes 202760 | tf_op jit(solution)/shard_map/ppermute | solution.py:378
  19.4 0.0 collective-permute-done.7.refs_8_
  19.4 0.0 collective-permute-start.12
  19.4 1.6 %collective-permute-done.8.refs_9_ = bf16[264,128]{1,0:T(8,128)(2,1)S(1)} collective-permute-done((bf16[264,128]{1,0:T(8,128)(2,1)S(1)}, bf16[264,128]{1,0:T(8,128)(2,1)S(1)}, u32[]{:S(2)}, u32[]{:S(2)}) %collective-permute-start.8) | collective-permute-done | bytes 67616 | tf_op jit(solution)/shard_map/ppermute | solution.py:378
  21.0 2.2 %collective-permute-start.13 = (bf16[264,128]{1,0:T(8,128)(2,1)S(1)}, bf16[264,128]{1,0:T(8,128)(2,1)S(1)}, u32[]{:S(2)}, u32[]{:S(2)}) collective-permute-start(bf16[264,128]{1,0:T(8,128)(2,1)S(1)} %get-tuple-element.37), channel_id=1, source_target_pairs={{0,14},{1,15},{2,12},{3,13},{4,10},{5,11},{6,8},{7,9},{8,6},{9,7},... | collective-permute-start | bytes 202760 | tf_op jit(solution)/shard_map/ppermute | solution.py:378
  23.2 1.4 %collective-permute-done.9.refs_10_ = bf16[264,128]{1,0:T(8,128)(2,1)S(1)} collective-permute-done((bf16[264,128]{1,0:T(8,128)(2,1)S(1)}, bf16[264,128]{1,0:T(8,128)(2,1)S(1)}, u32[]{:S(2)}, u32[]{:S(2)}) %collective-permute-start.9) | collective-permute-done | bytes 67616 | tf_op jit(solution)/shard_map/ppermute | solution.py:378
  24.7 0.0 copy-start.4
  24.7 2.9 %collective-permute-start.14 = (bf16[264,128]{1,0:T(8,128)(2,1)S(1)}, bf16[264,128]{1,0:T(8,128)(2,1)S(1)}, u32[]{:S(2)}, u32[]{:S(2)}) collective-permute-start(bf16[264,128]{1,0:T(8,128)(2,1)S(1)} %get-tuple-element.38), channel_id=1, source_target_pairs={{0,15},{1,14},{2,13},{3,12},{4,11},{5,10},{6,9},{7,8},{8,7},{9,6},... | collective-permute-start | bytes 202760 | tf_op jit(solution)/shard_map/ppermute | solution.py:378
  27.5 0.0 copy-done.6
  27.6 0.0 copy-done.5
  27.6 0.1 copy.14.k_ref
  27.6 0.0 copy-done.1
  27.6 0.0 copy-done.4
  27.6 0.8 %params.1 = (f32[8,16,128]{2,1,0:T(8,128)S(1)}, f32[2,16,128]{2,1,0:T(8,128)S(1)}) custom-call(s32[16,128]{1,0:T(8,128)S(1)} %bitcast.15, f32[16,8]{1,0:T(8,128)S(1)} %copy.14.k_ref, s32[8]{0:T(128)S(1)} %compare_select_fusion.c_ref, f32[2,8,256]{2,1,0:T(8,128)S(1)} %copy-done.1), custom_call_target="tpu_custom_call" | custom-call | tf_op jit(solution)/shard_map/params/pallas_call | solution.py:408
  28.4 0.0 collective-permute-done.10.refs_11_
  28.4 2.6 %collective-permute-done.11.refs_12_ = bf16[264,128]{1,0:T(8,128)(2,1)S(1)} collective-permute-done((bf16[264,128]{1,0:T(8,128)(2,1)S(1)}, bf16[264,128]{1,0:T(8,128)(2,1)S(1)}, u32[]{:S(2)}, u32[]{:S(2)}) %collective-permute-start.11) | collective-permute-done | bytes 67616 | tf_op jit(solution)/shard_map/ppermute | solution.py:378
  31.0 3.1 %collective-permute-done.12.refs_13_ = bf16[264,128]{1,0:T(8,128)(2,1)S(1)} collective-permute-done((bf16[264,128]{1,0:T(8,128)(2,1)S(1)}, bf16[264,128]{1,0:T(8,128)(2,1)S(1)}, u32[]{:S(2)}, u32[]{:S(2)}) %collective-permute-start.12) | collective-permute-done | bytes 67616 | tf_op jit(solution)/shard_map/ppermute | solution.py:378
  34.1 2.3 %collective-permute-done.13.refs_14_ = bf16[264,128]{1,0:T(8,128)(2,1)S(1)} collective-permute-done((bf16[264,128]{1,0:T(8,128)(2,1)S(1)}, bf16[264,128]{1,0:T(8,128)(2,1)S(1)}, u32[]{:S(2)}, u32[]{:S(2)}) %collective-permute-start.13) | collective-permute-done | bytes 67616 | tf_op jit(solution)/shard_map/ppermute | solution.py:378
  36.4 1.4 %collective-permute-done.14.refs_15_ = bf16[264,128]{1,0:T(8,128)(2,1)S(1)} collective-permute-done((bf16[264,128]{1,0:T(8,128)(2,1)S(1)}, bf16[264,128]{1,0:T(8,128)(2,1)S(1)}, u32[]{:S(2)}, u32[]{:S(2)}) %collective-permute-start.14) | collective-permute-done | bytes 67616 | tf_op jit(solution)/shard_map/ppermute | solution.py:378
  37.9 0.0 copy-done
  37.9 0.0 copy-done.2
  37.9 0.0 copy-done.3
  37.9 3.6 %focus.1 = bf16[2,256,1024]{2,1,0:T(8,128)(2,1)} custom-call(bf16[264,128]{1,0:T(8,128)(2,1)S(1)} %get-tuple-element.23.refs_0_, bf16[264,128]{1,0:T(8,128)(2,1)S(1)} %collective-permute-done.refs_1_, bf16[264,128]{1,0:T(8,128)(2,1)S(1)} %collective-permute-done.1.refs_2_, bf16[264,128]{1,0:T(8,128)(2,1)S(1)} %collective-permute-done.2.refs_3_, ...), custom_call_target="tpu_custom_call" | custom-call | tf_op jit(solution)/shard_map/focus/pallas_call | solution.py:419
  (5 shorter events, 0.0 us)
Async XLA Ops:
  0.0 16.2 %copy-start.7 = (bf16[512,512]{1,0:T(8,128)(2,1)S(1)}, bf16[512,512]{1,0:T(8,128)(2,1)}, u32[]{:S(2)}) copy-start(bf16[512,512]{1,0:T(8,128)(2,1)} %constant.23.clone) | copy-start | bytes 1572868
  3.4 4.2 %collective-permute-start = (bf16[264,128]{1,0:T(8,128)(2,1)S(1)}, bf16[264,128]{1,0:T(8,128)(2,1)S(1)}, u32[]{:S(2)}, u32[]{:S(2)}) collective-permute-start(bf16[264,128]{1,0:T(8,128)(2,1)S(1)} %get-tuple-element.24), channel_id=1, source_target_pairs={{0,1},{1,0},{2,3},{3,2},{4,5},{5,4},{6,7},{7,6},{8,9},{9,8},{10,11... | collective-permute-start | bytes 202760 | tf_op jit(solution)/shard_map/ppermute | solution.py:378
  4.1 4.6 %collective-permute-start.1 = (bf16[264,128]{1,0:T(8,128)(2,1)S(1)}, bf16[264,128]{1,0:T(8,128)(2,1)S(1)}, u32[]{:S(2)}, u32[]{:S(2)}) collective-permute-start(bf16[264,128]{1,0:T(8,128)(2,1)S(1)} %get-tuple-element.25), channel_id=1, source_target_pairs={{0,2},{1,3},{2,0},{3,1},{4,6},{5,7},{6,4},{7,5},{8,10},{9,11},{10,... | collective-permute-start | bytes 202760 | tf_op jit(solution)/shard_map/ppermute | solution.py:378
  5.3 4.9 %collective-permute-start.2 = (bf16[264,128]{1,0:T(8,128)(2,1)S(1)}, bf16[264,128]{1,0:T(8,128)(2,1)S(1)}, u32[]{:S(2)}, u32[]{:S(2)}) collective-permute-start(bf16[264,128]{1,0:T(8,128)(2,1)S(1)} %get-tuple-element.26), channel_id=1, source_target_pairs={{0,3},{1,2},{2,1},{3,0},{4,7},{5,6},{6,5},{7,4},{8,11},{9,10},{10,... | collective-permute-start | bytes 202760 | tf_op jit(solution)/shard_map/ppermute | solution.py:378
  5.8 6.7 %collective-permute-start.3 = (bf16[264,128]{1,0:T(8,128)(2,1)S(1)}, bf16[264,128]{1,0:T(8,128)(2,1)S(1)}, u32[]{:S(2)}, u32[]{:S(2)}) collective-permute-start(bf16[264,128]{1,0:T(8,128)(2,1)S(1)} %get-tuple-element.27), channel_id=1, source_target_pairs={{0,4},{1,5},{2,6},{3,7},{4,0},{5,1},{6,2},{7,3},{8,12},{9,13},{10,... | collective-permute-start | bytes 202760 | tf_op jit(solution)/shard_map/ppermute | solution.py:378
  5.8 7.4 %collective-permute-start.4 = (bf16[264,128]{1,0:T(8,128)(2,1)S(1)}, bf16[264,128]{1,0:T(8,128)(2,1)S(1)}, u32[]{:S(2)}, u32[]{:S(2)}) collective-permute-start(bf16[264,128]{1,0:T(8,128)(2,1)S(1)} %get-tuple-element.28), channel_id=1, source_target_pairs={{0,5},{1,4},{2,7},{3,6},{4,1},{5,0},{6,3},{7,2},{8,13},{9,12},{10,... | collective-permute-start | bytes 202760 | tf_op jit(solution)/shard_map/ppermute | solution.py:378
  7.6 9.1 %collective-permute-start.5 = (bf16[264,128]{1,0:T(8,128)(2,1)S(1)}, bf16[264,128]{1,0:T(8,128)(2,1)S(1)}, u32[]{:S(2)}, u32[]{:S(2)}) collective-permute-start(bf16[264,128]{1,0:T(8,128)(2,1)S(1)} %get-tuple-element.29), channel_id=1, source_target_pairs={{0,6},{1,7},{2,4},{3,5},{4,2},{5,3},{6,0},{7,1},{8,14},{9,15},{10,... | collective-permute-start | bytes 202760 | tf_op jit(solution)/shard_map/ppermute | solution.py:378
  8.7 8.3 %collective-permute-start.6 = (bf16[264,128]{1,0:T(8,128)(2,1)S(1)}, bf16[264,128]{1,0:T(8,128)(2,1)S(1)}, u32[]{:S(2)}, u32[]{:S(2)}) collective-permute-start(bf16[264,128]{1,0:T(8,128)(2,1)S(1)} %get-tuple-element.30), channel_id=1, source_target_pairs={{0,7},{1,6},{2,5},{3,4},{4,3},{5,2},{6,1},{7,0},{8,15},{9,14},{10,... | collective-permute-start | bytes 202760 | tf_op jit(solution)/shard_map/ppermute | solution.py:378
  10.2 9.2 %collective-permute-start.7 = (bf16[264,128]{1,0:T(8,128)(2,1)S(1)}, bf16[264,128]{1,0:T(8,128)(2,1)S(1)}, u32[]{:S(2)}, u32[]{:S(2)}) collective-permute-start(bf16[264,128]{1,0:T(8,128)(2,1)S(1)} %get-tuple-element.31), channel_id=1, source_target_pairs={{0,8},{1,9},{2,10},{3,11},{4,12},{5,13},{6,14},{7,15},{8,0},{9,1},... | collective-permute-start | bytes 202760 | tf_op jit(solution)/shard_map/ppermute | solution.py:378
  12.5 8.5 %collective-permute-start.8 = (bf16[264,128]{1,0:T(8,128)(2,1)S(1)}, bf16[264,128]{1,0:T(8,128)(2,1)S(1)}, u32[]{:S(2)}, u32[]{:S(2)}) collective-permute-start(bf16[264,128]{1,0:T(8,128)(2,1)S(1)} %get-tuple-element.32), channel_id=1, source_target_pairs={{0,9},{1,8},{2,11},{3,10},{4,13},{5,12},{6,15},{7,14},{8,1},{9,0},... | collective-permute-start | bytes 202760 | tf_op jit(solution)/shard_map/ppermute | solution.py:378
  13.2 24.7 %copy-start = (bf16[512,512]{1,0:T(8,128)(2,1)S(1)}, bf16[512,512]{1,0:T(8,128)(2,1)}, u32[]{:S(2)}) copy-start(bf16[512,512]{1,0:T(8,128)(2,1)} %constant.24.clone.refs_17_) | copy-start | bytes 1572868
  13.2 11.5 %collective-permute-start.9 = (bf16[264,128]{1,0:T(8,128)(2,1)S(1)}, bf16[264,128]{1,0:T(8,128)(2,1)S(1)}, u32[]{:S(2)}, u32[]{:S(2)}) collective-permute-start(bf16[264,128]{1,0:T(8,128)(2,1)S(1)} %get-tuple-element.33), channel_id=1, source_target_pairs={{0,10},{1,11},{2,8},{3,9},{4,14},{5,15},{6,12},{7,13},{8,2},{9,3},... | collective-permute-start | bytes 202760 | tf_op jit(solution)/shard_map/ppermute | solution.py:378
  16.2 11.4 %copy-start.6 = (s32[8]{0:T(128)S(1)}, s32[8]{0:T(128)}, u32[]{:S(2)}) copy-start(s32[8]{0:T(128)} %param.17) | copy-start | bytes 100
  16.2 11.4 %copy-start.5 = (f32[16,8]{0,1:T(8,128)S(1)}, f32[16,8]{0,1:T(8,128)}, u32[]{:S(2)}) copy-start(f32[16,8]{0,1:T(8,128)} %param.14) | copy-start | bytes 1540
  16.7 11.0 %copy-start.1 = (f32[2,8,256]{2,1,0:T(8,128)S(1)}, f32[2,8,256]{2,1,0:T(8,128)}, u32[]{:S(2)}) copy-start(f32[2,8,256]{2,1,0:T(8,128)} %a_ref.1) | copy-start | bytes 49156
  16.7 11.7 %collective-permute-start.10 = (bf16[264,128]{1,0:T(8,128)(2,1)S(1)}, bf16[264,128]{1,0:T(8,128)(2,1)S(1)}, u32[]{:S(2)}, u32[]{:S(2)}) collective-permute-start(bf16[264,128]{1,0:T(8,128)(2,1)S(1)} %get-tuple-element.34), channel_id=1, source_target_pairs={{0,11},{1,10},{2,9},{3,8},{4,15},{5,14},{6,13},{7,12},{8,3},{9,2},... | collective-permute-start | bytes 202760 | tf_op jit(solution)/shard_map/ppermute | solution.py:378
  17.1 13.9 %collective-permute-start.11 = (bf16[264,128]{1,0:T(8,128)(2,1)S(1)}, bf16[264,128]{1,0:T(8,128)(2,1)S(1)}, u32[]{:S(2)}, u32[]{:S(2)}) collective-permute-start(bf16[264,128]{1,0:T(8,128)(2,1)S(1)} %get-tuple-element.35), channel_id=1, source_target_pairs={{0,12},{1,13},{2,14},{3,15},{4,8},{5,9},{6,10},{7,11},{8,4},{9,5},... | collective-permute-start | bytes 202760 | tf_op jit(solution)/shard_map/ppermute | solution.py:378
  19.4 14.7 %collective-permute-start.12 = (bf16[264,128]{1,0:T(8,128)(2,1)S(1)}, bf16[264,128]{1,0:T(8,128)(2,1)S(1)}, u32[]{:S(2)}, u32[]{:S(2)}) collective-permute-start(bf16[264,128]{1,0:T(8,128)(2,1)S(1)} %get-tuple-element.36), channel_id=1, source_target_pairs={{0,13},{1,12},{2,15},{3,14},{4,9},{5,8},{6,11},{7,10},{8,5},{9,4},... | collective-permute-start | bytes 202760 | tf_op jit(solution)/shard_map/ppermute | solution.py:378
  21.0 15.4 %collective-permute-start.13 = (bf16[264,128]{1,0:T(8,128)(2,1)S(1)}, bf16[264,128]{1,0:T(8,128)(2,1)S(1)}, u32[]{:S(2)}, u32[]{:S(2)}) collective-permute-start(bf16[264,128]{1,0:T(8,128)(2,1)S(1)} %get-tuple-element.37), channel_id=1, source_target_pairs={{0,14},{1,15},{2,12},{3,13},{4,10},{5,11},{6,8},{7,9},{8,6},{9,7},... | collective-permute-start | bytes 202760 | tf_op jit(solution)/shard_map/ppermute | solution.py:378
  24.7 3.0 %copy-start.4 = (s32[8,256]{1,0:T(8,128)S(1)}, s32[8,256]{1,0:T(8,128)}, u32[]{:S(2)}) copy-start(s32[8,256]{1,0:T(8,128)} %param.16) | copy-start | bytes 24580
  24.7 13.2 %collective-permute-start.14 = (bf16[264,128]{1,0:T(8,128)(2,1)S(1)}, bf16[264,128]{1,0:T(8,128)(2,1)S(1)}, u32[]{:S(2)}, u32[]{:S(2)}) collective-permute-start(bf16[264,128]{1,0:T(8,128)(2,1)S(1)} %get-tuple-element.38), channel_id=1, source_target_pairs={{0,15},{1,14},{2,13},{3,12},{4,11},{5,10},{6,9},{7,8},{8,7},{9,6},... | collective-permute-start | bytes 202760 | tf_op jit(solution)/shard_map/ppermute | solution.py:378
  27.6 10.2 %copy-start.2 = (s32[8,256]{1,0:T(8,128)S(1)}, s32[8,256]{1,0:T(8,128)}, u32[]{:S(2)}) copy-start(s32[8,256]{1,0:T(8,128)} %param.15) | copy-start | bytes 24580
  27.6 10.2 %copy-start.3 = (bf16[32,128]{1,0:T(8,128)(2,1)S(1)}, bf16[32,128]{1,0:T(8,128)(2,1)}, u32[]{:S(2)}) copy-start(bf16[32,128]{1,0:T(8,128)(2,1)} %constant.25.clone.refs_18_) | copy-start | bytes 24580
